TPU v7x, 32 devices: a whole 2x2x4 slice. The times are simulated.
32 devices in a mesh: leaf: 8 (over z, x), lvl: 4 (over y, core).
Axes of the slice: x: 2, y: 2, z: 4, core: 2. Of those that a mesh axis runs over, the one named last changes fastest.
Arguments:
- offsets: float32 [3, 16384], P(None, 'leaf'), may hold values from -0.5 to 0.5
- vel_cot: float32 [3, 16384], P(None, 'leaf'), may hold values from -0.18 to 0.18
- m2l_ops: bfloat16 [16, 456, 456], P('lvl'), may hold values from -0.25 to 0.25
- child_ops: bfloat16 [8, 456, 456], P('lvl'), may hold values from -0.25 to 0.25
- check_map: float32 [456, 456], replicated, may hold values from -0.015625 to 0.015625
- leaf_dest: int32 [4, 256, 4, 1], P('lvl', 'leaf'), may hold values from 0 to 7; in each aligned block of 128 rows (0 to 127, 128 to 255, ..., all dimensions but the last counted through in order) at most 32 rows name the same one
- leaf_slot: int32 [4, 256, 4], P('lvl', 'leaf'), may hold values from 0 to 31
- coarse_dest: int32 [4, 32, 4, 1], P('lvl'), may hold values from 0 to 7
- coarse_slot: int32 [4, 32, 4], P('lvl'), may hold values from 0 to 3
- near_box: int32 [256, 16], P('leaf', 'lvl'), may hold values from 0 to 31
- near_dir: int32 [256, 16], P('leaf', 'lvl'), may hold values from 0 to 26
Outputs:
- force_cot: float32 [3, 16384], P(None, 'leaf')
Inputs may be any that keep to these rules, and one draw needn't show every extreme that they name: `leaf_dest`: in the rows of one device (aligned blocks of 128 rows in the order of the leading dimensions) no subtree is named more than 32 times. `near_box`: A place among the 32 leaf boxes of the same subtree.
All inputs are finite; a program needn't handle non-finite values.
Results may differ from a plain program's by a relative error of at most 0.0095.
Values may be sent and summed in bfloat16 or wider, within the bound.
No kernel may reach another device: no remote copies, remote signals or barrier semaphores. Data moves between devices by JAX's collectives and lax.ppermute only.
A program may use at most 64 MiB of HBM per device.

v0:
```python
import jax
import jax.numpy as jnp
import numpy as np
from jax import lax
from jax.sharding import PartitionSpec as P

SIDE = 6


EPSILON2 = 0.01
RADIUS = 0.525


def surface_points(edge_count):
    levels = np.linspace(-1.0, 1.0, edge_count)
    lattice = np.stack(np.meshgrid(levels, levels, levels, indexing="ij"), 0).reshape(3, -1)
    on_shell = np.max(np.abs(lattice), 0) > 1.0 - 1e-09
    return jnp.asarray(lattice[:, on_shell] * RADIUS, jnp.float32)


def stokes_apply(relative, source):
    squared = jnp.sum(relative * relative, axis=0)
    weights = (squared + EPSILON2) ** (-1.5)
    spread = source[..., None, :]
    along = jnp.sum(relative * spread, axis=0)
    return jnp.sum(weights * ((squared + 2.0 * EPSILON2) * spread + relative * along), axis=-1)


def to_surface(points, vectors, shell):
    relative = shell[:, None, :, None] - points[:, :, None, :]
    values = stokes_apply(relative, vectors)
    return values.transpose(1, 0, 2).reshape(values.shape[1], -1)


def from_surface(points, density, shell):
    source = density.reshape(density.shape[0], 3, -1).transpose(1, 0, 2)
    relative = points[:, :, :, None] - shell[:, None, None, :]
    return stokes_apply(relative, source)


def directions(codes):
    return jnp.stack([codes // 9 - 1, codes // 3 % 3 - 1, codes % 3 - 1], 0).astype(jnp.float32)


def near_terms(points, src_points, src_vectors, shifts):
    moved = src_points + shifts[..., None]
    relative = points[:, :, None, :, None] - moved[:, :, :, None, :]
    return jnp.sum(stokes_apply(relative, src_vectors), axis=2)


def local(
    offsets,
    vel_cot,
    m2l_ops,
    child_ops,
    check_map,
    leaf_dest,
    leaf_slot,
    coarse_dest,
    coarse_slot,
    near_box,
    near_dir,
):
    shell = surface_points(SIDE)
    width = m2l_ops.shape[1]
    classes_here = m2l_ops.shape[0]
    octants_here = child_ops.shape[0]
    boxes = near_box.shape[0]
    per_box = offsets.shape[1] // boxes
    parents = boxes // 8
    blocks = boxes // 8
    items = boxes * classes_here
    leaf_count = lax.axis_size("leaf")
    capacity = max(2, (2 * items + leaf_count - 1) // leaf_count)
    leaf_index = lax.axis_index("leaf")
    lvl_index = lax.axis_index("lvl")
    points = offsets.reshape(3, boxes, per_box)
    vectors = vel_cot.reshape(3, boxes, per_box)
    point_blocks = points.reshape(3, blocks, 8, per_box).transpose(1, 0, 2, 3)
    vector_blocks = vectors.reshape(3, blocks, 8, per_box).transpose(1, 0, 2, 3)
    local_float = lax.map(
        lambda packed: to_surface(packed[0], packed[1], shell), (point_blocks, vector_blocks)
    )
    leaf_local = local_float.reshape(boxes, width).astype(jnp.bfloat16)
    leaf_terms = jnp.einsum("tm,cmn->tcn", leaf_local, m2l_ops, preferred_element_type=jnp.float32)
    leaf_terms = leaf_terms.astype(jnp.bfloat16).reshape(items, width)
    owners = leaf_dest[0, :, :, 0].reshape(items)
    places = leaf_slot[0].reshape(items)
    owner_hits = (owners[:, None] == jnp.arange(leaf_count, dtype=jnp.int32)[None, :]).astype(
        jnp.int32
    )
    earlier = jnp.cumsum(owner_hits, axis=0) - owner_hits
    send_pos = owners * capacity + jnp.sum(earlier * owner_hits, axis=1)
    placing = send_pos[None, :] == jnp.arange(leaf_count * capacity, dtype=jnp.int32)[:, None]
    send_rows = jnp.dot(
        placing.astype(jnp.bfloat16), leaf_terms, preferred_element_type=jnp.float32
    ).astype(jnp.bfloat16)
    send_ids = jnp.dot(
        placing.astype(jnp.float32),
        (places + 1).astype(jnp.float32),
        precision=lax.Precision.HIGHEST,
    )
    send_ids = send_ids.astype(jnp.int32) - 1
    got_rows, got_ids = (
        lax.all_to_all(
            send_rows.reshape(leaf_count, capacity, width),
            "leaf",
            split_axis=0,
            concat_axis=0,
            tiled=True,
        ),
        lax.all_to_all(
            send_ids.reshape(leaf_count, capacity), "leaf", split_axis=0, concat_axis=0, tiled=True
        ),
    )
    landing = got_ids.reshape(-1)[None, :] == jnp.arange(boxes, dtype=jnp.int32)[:, None]
    leaf_far = jnp.dot(
        landing.astype(jnp.bfloat16),
        got_rows.reshape(-1, width),
        preferred_element_type=jnp.float32,
    )
    children = leaf_local.reshape(parents, 8, width)
    my_children = lax.dynamic_slice_in_dim(children, lvl_index * octants_here, octants_here, 1)
    parent_part = jnp.einsum(
        "pom,omn->pn", my_children, child_ops, preferred_element_type=jnp.float32
    )
    parent_local = lax.psum(parent_part, "lvl").astype(jnp.bfloat16)
    coarse_ids = coarse_dest[0, :, :, 0] * parents + coarse_slot[0]
    mine = leaf_index * parents + jnp.arange(parents, dtype=jnp.int32)
    terms = 0.5 * jnp.einsum(
        "rm,cmn->crn",
        lax.all_gather(parent_local, "leaf", axis=0, tiled=True),
        m2l_ops,
        preferred_element_type=jnp.float32,
    )
    select = (coarse_ids.T[:, None, :] == mine[None, :, None]).astype(jnp.float32)
    coarse_part = jnp.einsum("cpr,crn->pn", select, terms, precision=lax.Precision.HIGHEST)
    parent_mult = lax.psum(coarse_part, "lvl").astype(jnp.bfloat16)
    lowered = jnp.einsum("pm,onm->pon", parent_mult, child_ops, preferred_element_type=jnp.float32)
    placed = lax.dynamic_update_slice_in_dim(
        jnp.zeros((parents, 8, width), jnp.float32), lowered, lvl_index * octants_here, 1
    )
    leaf_part = leaf_far + placed.reshape(boxes, width)
    neighbour_blocks = near_box.reshape(blocks, 8, near_box.shape[1])
    shift_blocks = (
        directions(near_dir).reshape(3, blocks, 8, near_box.shape[1]).transpose(1, 0, 2, 3)
    )

    def near_block(packed):
        here, chosen, moved = packed
        return near_terms(here, points[:, chosen], vectors[:, chosen], moved)

    near_blocks = lax.map(near_block, (point_blocks, neighbour_blocks, shift_blocks))
    near_part = near_blocks.transpose(1, 0, 2, 3).reshape(3, boxes * per_box)
    total_mult, near_cot = (
        lax.psum(leaf_part.astype(jnp.bfloat16), "lvl").astype(jnp.float32),
        lax.psum(near_part.astype(jnp.bfloat16), "lvl").astype(jnp.float32),
    )
    check_cot = jnp.dot(total_mult, check_map, precision=lax.Precision.HIGHEST)
    check_blocks = check_cot.reshape(blocks, 8, width)
    far_blocks = lax.map(
        lambda packed: from_surface(packed[0], packed[1], shell), (point_blocks, check_blocks)
    )
    return far_blocks.transpose(1, 0, 2, 3).reshape(3, boxes * per_box) + near_cot


def solution(mesh):
    placed = (
        P(None, "leaf"),
        P(None, "leaf"),
        P("lvl", None, None),
        P("lvl", None, None),
        P(),
        P("lvl", "leaf", None, None),
        P("lvl", "leaf", None),
        P("lvl", None, None, None),
        P("lvl", None, None),
        P("leaf", "lvl"),
        P("leaf", "lvl"),
    )
    return jax.shard_map(
        local, mesh=mesh, in_specs=placed, out_specs=P(None, "leaf"), check_vma=False
    )
```

profile of v0, /device:TPU:0, one launch (start us, length us, event | category | flops | bytes accessed | tf_op | source)
XLA Modules:
  0.0 121.7 jit_solution(14257357847229150357)
XLA Ops:
  0.0 0.9 copy.93
  1.5 0.7 add_convert_fusion.1
  2.5 0.7 all_to_all.9
  3.2 7.3 %all-to-all-start = ((s32[8,1,32]{2,1,0:T(1,128)}), s32[8,1,32]{2,1,0:T(1,128)S(1)}, u32[]{:S(2)}, u32[]{:S(2)}) async-start(s32[8,1,32]{2,1,0:T(1,128)} %all_to_all.9), calls=%async_computation | async-start | bytes 8192 | tf_op jit(solution)/shard_map/all_to_all | solution.py:112
  10.5 0.9 reshape_reshape.6
  11.4 0.9 reshape.146
  12.2 0.9 reshape_reshape.7
  13.1 0.9 reshape.147
  14.0 9.3 %while.36 = (s32[]{:T(128)}, bf16[4,8,456]{2,0,1:T(4,128)(2,1)S(1)}, f32[4,3,8,64]{3,2,1,0:T(8,128)S(1)}, f32[4,3,8,64]{3,2,0,1:T(8,128)S(1)}, f32[3,152]{1,0:T(4,128)}) while((s32[]{:T(128)}, bf16[4,8,456]{2,0,1:T(4,128)(2,1)S(1)}, f32[4,3,8,64]{3,2,1,0:T(8,128)S(1)}, f32[4,3,8,64]{3,2,0,1:T(8,128)S(1)}, ...), condition=%wide.region_6.7_spmd.clone.clone, body=%wide.region_2.6_spmd.sunk.clone.sunk.clone | while | flops 2564546 | bytes 2601637 | solution.py:81
  14.0 1.2 %fusion.64 = (f32[8,152,64]{1,2,0:T(8,128)S(1)}, f32[8,152,64]{1,2,0:T(8,128)S(1)}) fusion(f32[3,8,64]{2,1,0:T(8,128)S(1)} %dynamic-slice_bitcast_fusion.13, f32[3,152]{1,0:T(4,128)} %get-tuple-element.429, f32[3,8,64]{2,1,0:T(8,128)S(1)} %dynamic-slice_bitcast_fusion.14), kind=kLoop, calls=%fused_computation.5.clone.1.clone | loop fusion | flops 1011712 | bytes 636704 | tf_op jit(solution)/shard_map/while/body/eval_jaxpr/reduce_sum | solution.py:22
  15.5 0.6 fusion.65
  16.3 1.2 %fusion.64 = (f32[8,152,64]{1,2,0:T(8,128)S(1)}, f32[8,152,64]{1,2,0:T(8,128)S(1)}) fusion(f32[3,8,64]{2,1,0:T(8,128)S(1)} %dynamic-slice_bitcast_fusion.13, f32[3,152]{1,0:T(4,128)} %get-tuple-element.429, f32[3,8,64]{2,1,0:T(8,128)S(1)} %dynamic-slice_bitcast_fusion.14), kind=kLoop, calls=%fused_computation.5.clone.1.clone | loop fusion | flops 1011712 | bytes 636704 | tf_op jit(solution)/shard_map/while/body/eval_jaxpr/reduce_sum | solution.py:22
  17.8 0.6 fusion.65
  18.7 1.2 %fusion.64 = (f32[8,152,64]{1,2,0:T(8,128)S(1)}, f32[8,152,64]{1,2,0:T(8,128)S(1)}) fusion(f32[3,8,64]{2,1,0:T(8,128)S(1)} %dynamic-slice_bitcast_fusion.13, f32[3,152]{1,0:T(4,128)} %get-tuple-element.429, f32[3,8,64]{2,1,0:T(8,128)S(1)} %dynamic-slice_bitcast_fusion.14), kind=kLoop, calls=%fused_computation.5.clone.1.clone | loop fusion | flops 1011712 | bytes 636704 | tf_op jit(solution)/shard_map/while/body/eval_jaxpr/reduce_sum | solution.py:22
  21.0 1.2 %fusion.64 = (f32[8,152,64]{1,2,0:T(8,128)S(1)}, f32[8,152,64]{1,2,0:T(8,128)S(1)}) fusion(f32[3,8,64]{2,1,0:T(8,128)S(1)} %dynamic-slice_bitcast_fusion.13, f32[3,152]{1,0:T(4,128)} %get-tuple-element.429, f32[3,8,64]{2,1,0:T(8,128)S(1)} %dynamic-slice_bitcast_fusion.14), kind=kLoop, calls=%fused_computation.5.clone.1.clone | loop fusion | flops 1011712 | bytes 636704 | tf_op jit(solution)/shard_map/while/body/eval_jaxpr/reduce_sum | solution.py:22
  23.5 6.4 %psum.28 = bf16[4,456]{1,0:T(4,128)(2,1)S(1)} all-reduce(f32[4,456]{1,0:T(4,128)S(1)} %convolution_bitcast_fusion.2), channel_id=1, replica_groups=mesh['leaf'=8,'lvl'=4] {'lvl'}, use_global_device_ids=true, to_apply=%region_7.8 | all-reduce | flops 1824 | bytes 10944 | tf_op jit(solution)/shard_map/psum | solution.py:127
  29.9 30.9 %all-gather = bf16[8,4,456]{2,1,0:T(4,128)(2,1)S(1)} all-gather(bf16[1,4,456]{2,1,0:T(4,128)(2,1)S(1)} %bitcast.143), channel_id=1, replica_groups=mesh['leaf'=8,'lvl'=4] {'leaf'}, dimensions={0}, use_global_device_ids=true | all-gather | bytes 32832 | tf_op jit(solution)/shard_map/all_gather | solution.py:132
  62.1 1.0 convolution_convert_fusion
  63.6 16.4 %while.35 = (s32[]{:T(128)}, bf16[4,3,8,64]{3,2,1,0:T(8,128)(2,1)S(1)}, f32[4,3,8,64]{3,2,1,0:T(8,128)S(1)}, s32[4,8,4]{1,0,2:T(4,128)S(1)}, f32[3,32,64]{2,0,1:...) while((s32[]{:T(128)}, bf16[4,3,8,64]{3,2,1,0:T(8,128)(2,1)S(1)}, ...), condition=%wide.region_19.20_spmd.clone, body=%wide.region_15.19_spmd.sunk.clone | while | flops 4331106 | bytes 4585821 | solution.py:153
  63.8 0.6 gather_fusion
  64.7 0.6 gather_fusion.1
  65.3 0.8 fusion.62
  66.5 1.2 fusion.63
  67.9 0.6 gather_fusion
  68.8 0.6 gather_fusion.1
  69.4 0.8 fusion.62
  70.6 1.2 fusion.63
  72.0 0.6 gather_fusion
  72.9 0.6 gather_fusion.1
  73.5 0.8 fusion.62
  74.7 1.2 fusion.63
  76.1 0.6 gather_fusion
  77.0 0.6 gather_fusion.1
  77.6 0.8 fusion.62
  78.8 1.2 fusion.63
  80.3 5.7 %psum.29 = bf16[4,456]{1,0:T(4,128)(2,1)S(1)} all-reduce(f32[4,456]{1,0:T(4,128)S(1)} %convolution_bitcast_fusion.1), channel_id=1, replica_groups=mesh['leaf'=8,'lvl'=4] {'lvl'}, use_global_device_ids=true, to_apply=%region_8.9 | all-reduce | flops 1824 | bytes 10944 | tf_op jit(solution)/shard_map/psum | solution.py:138
  86.1 1.8 %copy.100 = bf16[256,456]{1,0:T(8,128)(2,1)} copy(bf16[256,456]{0,1:T(8,128)(2,1)} %convolution_convert_fusion) | data formatting | bytes 466944 | tf_op jit(solution)/shard_map/convert_element_type | solution.py:97
  88.0 5.4 %all-to-all-start.1 = ((bf16[8,32,456]{2,1,0:T(8,128)(2,1)}), bf16[8,32,456]{2,1,0:T(8,128)(2,1)S(1)}, u32[]{:S(2)}, u32[]{:S(2)}) async-start(bf16[8,32,456]{2,1,0:T(8,128)(2,1)} %bitcast.13), calls=%async_computation.1 | async-start | bytes 524288 | tf_op jit(solution)/shard_map/all_to_all | solution.py:105
  94.3 0.7 reduce.4
  95.1 7.3 %all-to-all-done.1 = bf16[8,32,456]{2,1,0:T(8,128)(2,1)S(1)} async-done(((bf16[8,32,456]{2,1,0:T(8,128)(2,1)}), bf16[8,32,456]{2,1,0:T(8,128)(2,1)S(1)}, u32[]{:S(2)}, u32[]{:S(2)}) %all-to-all-start.1) | async-done | bytes 233504 | tf_op jit(solution)/shard_map/all_to_all | solution.py:105
  102.5 10.6 %all-reduce = (bf16[32,456]{1,0:T(8,128)(2,1)S(1)}, bf16[3,2048]{1,0:T(4,128)(2,1)S(1)}) all-reduce(bf16[32,456]{1,0:T(8,128)(2,1)S(1)} %fusion.16, bf16[3,2048]{1,0:T(4,128)(2,1)S(1)} %convert_element_type.69), channel_id=1, replica_groups=mesh['leaf'=8,'lvl'=4] {'lvl'}, use_global_device_ids=true, to_apply=%region_9.10 | all-reduce | flops 20736 | bytes 82944 | tf_op jit(solution)/shard_map/psum | solution.py:156
  113.1 1.6 %convolution_bitcast_fusion = f32[4,8,456]{2,1,0:T(8,128)S(1)} fusion(bf16[32,456]{1,0:T(8,128)(2,1)S(1)} %get-tuple-element.232, f32[456,456]{1,0:T(8,128)} %param.22), kind=kOutput, calls=%fused_computation.48 | convolution fusion | flops 79847424 | bytes 919296 | tf_op jit(solution)/shard_map/dot_general | solution.py:159
  114.7 6.3 %while.37 = (s32[]{:T(128)}, f32[4,3,8,64]{3,2,1,0:T(8,128)S(1)}, f32[4,3,8,64]{3,2,1,0:T(8,128)S(1)}, f32[4,8,456]{2,1,0:T(8,128)S(1)}, f32[3,152]{1,0:T(4,128)S(1)}) while((s32[]{:T(128)}, f32[4,3,8,64]{3,2,1,0:T(8,128)S(1)}, f32[4,3,8,64]{3,2,1,0:T(8,128)S(1)}, f32[4,8,456]{2,1,0:T(8,128)S(1)}, ...), condition=%wide.region_14.15_spmd.clone.clone, body=%wide.region_10.14_spmd.sunk.clone.sunk.clone | while | flops 2566658 | bytes 2666121 | solution.py:161
  115.5 0.8 fusion.67
  117.0 0.8 fusion.67
  118.6 0.8 fusion.67
  120.2 0.8 fusion.67
  121.1 0.6 convert_add_fusion
  (170 shorter events, 13.5 us)
Async XLA Ops:
  0.0 60.8 %copy-start = (bf16[4,456,456]{2,1,0:T(8,128)(2,1)S(1)}, bf16[4,456,456]{2,1,0:T(8,128)(2,1)}, u32[]{:S(2)}) copy-start(bf16[4,456,456]{2,1,0:T(8,128)(2,1)} %param.20) | copy-start | bytes 4990468
  3.2 84.7 %all-to-all-start = ((s32[8,1,32]{2,1,0:T(1,128)}), s32[8,1,32]{2,1,0:T(1,128)S(1)}, u32[]{:S(2)}, u32[]{:S(2)}) async-start(s32[8,1,32]{2,1,0:T(1,128)} %all_to_all.9), calls=%async_computation | async-start | bytes 8192 | tf_op jit(solution)/shard_map/all_to_all | solution.py:112
  13.9 9.3 %copy-start.1 = (bf16[2,456,456]{2,1,0:T(8,128)(2,1)S(1)}, bf16[2,456,456]{2,1,0:T(8,128)(2,1)}, u32[]{:S(2)}) copy-start(bf16[2,456,456]{2,1,0:T(8,128)(2,1)} %param.21) | copy-start | bytes 2495236
  14.0 1.5 %copy-start.3 = (f32[3,152]{1,0:T(4,128)S(1)}, f32[3,152]{1,0:T(4,128)}, u32[]{:S(2)}) copy-start(f32[3,152]{1,0:T(4,128)} %get-tuple-element.429) | copy-start | bytes 5476 | tf_op jit(solution)/shard_map/while
  16.3 1.5 %copy-start.3 = (f32[3,152]{1,0:T(4,128)S(1)}, f32[3,152]{1,0:T(4,128)}, u32[]{:S(2)}) copy-start(f32[3,152]{1,0:T(4,128)} %get-tuple-element.429) | copy-start | bytes 5476 | tf_op jit(solution)/shard_map/while
  18.6 1.5 %copy-start.3 = (f32[3,152]{1,0:T(4,128)S(1)}, f32[3,152]{1,0:T(4,128)}, u32[]{:S(2)}) copy-start(f32[3,152]{1,0:T(4,128)} %get-tuple-element.429) | copy-start | bytes 5476 | tf_op jit(solution)/shard_map/while
  20.9 1.5 %copy-start.3 = (f32[3,152]{1,0:T(4,128)S(1)}, f32[3,152]{1,0:T(4,128)}, u32[]{:S(2)}) copy-start(f32[3,152]{1,0:T(4,128)} %get-tuple-element.429) | copy-start | bytes 5476 | tf_op jit(solution)/shard_map/while
  61.3 0.7 copy-start.6
  61.3 1.8 %copy-start.7 = (s32[32,4]{0,1:T(4,128)S(1)}, s32[32,4]{0,1:T(4,128)}, u32[]{:S(2)}) copy-start(s32[32,4]{0,1:T(4,128)} %param.28) | copy-start | bytes 1540
  61.3 2.2 %copy-start.4 = (s32[32,4]{0,1:T(4,128)S(1)}, s32[32,4]{0,1:T(4,128)}, u32[]{:S(2)}) copy-start(s32[32,4]{0,1:T(4,128)} %param.27) | copy-start | bytes 1540
  63.6 16.4 %copy-start.5 = (s32[1,32,4]{1,2,0:T(4,128)S(1)}, s32[1,32,4]{1,2,0:T(4,128)}, u32[]{:S(2)}) copy-start(s32[1,32,4]{1,2,0:T(4,128)} %param.26) | copy-start | bytes 1540
  87.9 26.8 %copy-start.2 = (f32[3,152]{1,0:T(4,128)S(1)}, f32[3,152]{1,0:T(4,128)}, u32[]{:S(2)}) copy-start(f32[3,152]{1,0:T(4,128)} %constant.191) | copy-start | bytes 5476
  88.0 14.4 %all-to-all-start.1 = ((bf16[8,32,456]{2,1,0:T(8,128)(2,1)}), bf16[8,32,456]{2,1,0:T(8,128)(2,1)S(1)}, u32[]{:S(2)}, u32[]{:S(2)}) async-start(bf16[8,32,456]{2,1,0:T(8,128)(2,1)} %bitcast.13), calls=%async_computation.1 | async-start | bytes 524288 | tf_op jit(solution)/shard_map/all_to_all | solution.py:105
where the time goes:
time: 123 us; the launch traced here: 122 us
  blocking collectives  53.6 us (44%)
  other arithmetic  26 us (21%)
  local copies, waits for them, and re-layouts  16.3 us (13%)
  starting transfers between devices  12.7 us (10%)
  waiting for transfers between devices  7.28 us (6%)
  matrix products  4.62 us (4%)
    all_gather x1, blocking collectives, local(): lax.all_gather(parent_local, 'leaf', axis=0, tiled=True)  30.9 us
    psum x1, blocking collectives, local(): lax.psum(leaf_part.astype(jnp.bfloat16), 'lvl').astype(jnp.float32)  10.6 us
    reduce_sum x12, other arithmetic, stokes_apply(): squared = jnp.sum(relative * relative, axis=0)  9.45 us
    all_to_all x1, starting transfers between devices, local(): lax.all_to_all(send_ids.reshape(leaf_count, capacity), 'leaf', split_axis...  7.28 us
    all_to_all x1, waiting for transfers between devices, local(): lax.all_to_all(send_rows.reshape(leaf_count, capacity, width), 'leaf', sp...  7.27 us
    psum x1, blocking collectives, local(): parent_local = lax.psum(parent_part, 'lvl').astype(jnp.bfloat16)  6.42 us
    psum x1, blocking collectives, local(): parent_mult = lax.psum(coarse_part, 'lvl').astype(jnp.bfloat16)  5.74 us
    reduce_sum x8, other arithmetic, stokes_apply(): jnp.sum(weights * ((squared + 2.0 * EPSILON2) * spread + relative * along...  5.59 us
  transfers between devices with their start and end apart: 2, of which 1 were waited for; matrix products, arithmetic and copies ran while one was open for 29% of the time, Pallas kernels for 0%

commit v1 on v0

v1 whole, which is shorter than its diff:
```python
import jax
import jax.numpy as jnp
import numpy as np
from jax import lax
from jax.experimental import pallas as pl
from jax.experimental.pallas import tpu as pltpu
from jax.sharding import PartitionSpec as P

SIDE = 6
EPSILON2 = 0.01
RADIUS = 0.525
LANES = 128
F32 = jnp.float32
BF16 = jnp.bfloat16
VMEM = pl.BlockSpec(memory_space=pltpu.VMEM)
SMEM = pl.BlockSpec(memory_space=pltpu.SMEM)
NN = (((1,), (0,)), ((), ()))
NT = (((1,), (1,)), ((), ()))
TN = (((0,), (0,)), ((), ()))


def surface_points(edge_count):
    levels = np.linspace(-1.0, 1.0, edge_count)
    lattice = np.stack(np.meshgrid(levels, levels, levels, indexing="ij"), 0).reshape(3, -1)
    on_shell = np.max(np.abs(lattice), 0) > 1.0 - 1e-09
    return np.asarray(lattice[:, on_shell] * RADIUS, np.float32)


def dot(a, b, dims=NN):
    return lax.dot_general(a, b, dims, preferred_element_type=F32)


def iota(shape, axis):
    return lax.broadcasted_iota(jnp.int32, shape, axis)


def stokeslet(d, v):
    r2 = d[0] * d[0] + d[1] * d[1] + (d[2] * d[2] + EPSILON2)
    rs = lax.rsqrt(r2)
    weight = rs * (rs * rs)
    scale = rs + EPSILON2 * weight
    along = weight * (d[0] * v[0] + d[1] * v[1] + d[2] * v[2])
    return [scale * v[c] + along * d[c] for c in range(3)]


def call(body, outs, cost, scratch=(), ins=None, vmem=24):
    return pl.pallas_call(
        body,
        out_shape=outs,
        in_specs=ins,
        out_specs=jax.tree.map(lambda _: VMEM, outs),
        scratch_shapes=list(scratch),
        cost_estimate=pl.CostEstimate(flops=cost, bytes_accessed=1 << 20, transcendentals=0),
        compiler_params=pltpu.CompilerParams(vmem_limit_bytes=vmem << 20),
    )


def shape(dims, dtype):
    return jax.ShapeDtypeStruct(tuple(dims), dtype)


def surface_block(points, vectors, shell_ref, fields, column):
    count = shell_ref.shape[0]
    for row in range(0, count, 8):
        d = [shell_ref[row : row + 8, c : c + 1] - points[c] for c in range(3)]
        for c, value in enumerate(stokeslet(d, vectors)):
            fields[c * count + row : c * count + row + 8, column] = value


def blocks128(matrix):
    width = matrix.shape[1]
    fill = -width % LANES
    if fill:
        matrix = jnp.concatenate([matrix, jnp.zeros((matrix.shape[0], fill), matrix.dtype)], 1)
    return [matrix[:, k : k + LANES] for k in range(0, width, LANES)]


def local(
    offsets,
    vel_cot,
    m2l_ops,
    child_ops,
    check_map,
    leaf_dest,
    leaf_slot,
    coarse_dest,
    coarse_slot,
    near_box,
    near_dir,
):
    shell_np = surface_points(SIDE)
    count = shell_np.shape[1]
    width = m2l_ops.shape[1]
    classes = m2l_ops.shape[0]
    octants = child_ops.shape[0]
    boxes, slots = near_box.shape
    per_box = offsets.shape[1] // boxes
    parents = boxes // 8
    own = parents * octants
    leaves = lax.axis_size("leaf")
    lvls = lax.axis_size("lvl")
    pieces = -(-width // LANES)
    group = octants * per_box
    groups = parents * lvls
    assert group == LANES and own == 8 and parents == 4 and lvls * octants == 8
    up_rows = pieces * parents
    leaf_rows = pieces * boxes
    own_rows = pieces * own
    tall = groups * LANES
    shell = jnp.asarray(np.pad(shell_np.T, ((0, 0), (0, LANES - 3))))

    leaf_owner = leaf_dest.transpose(0, 2, 3, 1)[0]
    leaf_place = leaf_slot.transpose(0, 2, 1)[0]
    coarse_owner = coarse_dest.transpose(0, 2, 3, 1)[0]
    coarse_place = coarse_slot.transpose(0, 2, 1)[0]
    near_q = near_box.T
    near_d = near_dir.T

    def lanes_of(parent, lvl):
        return pl.ds(pl.multiple_of((parent * lvls + lvl) * LANES, LANES), LANES)

    def rows3(ref, lanes):
        return [ref[c : c + 1, lanes] for c in range(3)]

    def up_body(offsets_ref, vel_ref, child_ref, shell_ref, up_ref, fields):
        me = lax.axis_index("lvl")
        for p in range(parents):
            lanes = lanes_of(p, me)
            surface_block(
                rows3(offsets_ref, lanes),
                rows3(vel_ref, lanes),
                shell_ref,
                fields,
                slice(p * LANES, (p + 1) * LANES),
            )
        here = parents * LANES
        lane = iota((8 * octants, here), 1)
        row = iota((8 * octants, here), 0)
        target = (lane % LANES) // per_box * 8 + lane // LANES
        pick = (row == target).astype(F32).astype(BF16)
        leaf = dot(pick, fields[...].astype(BF16), NT).astype(BF16)
        total = dot(leaf[0:8], child_ref[0])
        for o in range(1, octants):
            total = total + dot(leaf[8 * o : 8 * o + 8], child_ref[o])
        for k, block in enumerate(blocks128(total)):
            up_ref[k * parents : (k + 1) * parents, :] = block[0:parents]

    up = call(
        up_body,
        shape((up_rows, LANES), F32),
        20_000_000,
        [pltpu.VMEM((3 * count, parents * LANES), F32)],
        [VMEM] * 4,
    )(offsets, vel_cot, child_ops, shell)

    def shifted(value, k):
        return lax.ppermute(value, "lvl", [(i, (i + k) % lvls) for i in range(lvls)])

    ups = [up] + [shifted(up, k) for k in range(1, lvls)]

    def push_body(offsets_ref, vel_ref, m2l_ref, shell_ref, owner_ref, place_ref, out_ref, fields):
        def block(j, _):
            lanes = pl.ds(pl.multiple_of(j * LANES, LANES), LANES)
            surface_block(
                rows3(offsets_ref, lanes), rows3(vel_ref, lanes), shell_ref, fields, lanes
            )
            return 0

        lax.fori_loop(0, groups, block, 0)
        pick = (iota((boxes, tall), 0) == iota((boxes, tall), 1) // per_box).astype(F32)
        leaf = dot(pick.astype(BF16), fields[...].astype(BF16), NT).astype(BF16)
        total = None
        for c in range(classes):
            term = dot(leaf, m2l_ref[c]).astype(BF16)
            place = place_ref[c : c + 1, :]
            octant = lax.rem(place, 8)
            slot = (
                lax.div(octant, octants) * own
                + lax.rem(octant, octants) * parents
                + lax.div(place, 8)
            )
            code = owner_ref[c] * boxes + slot
            hit = (iota((leaves * boxes, boxes), 0) == code).astype(F32).astype(BF16)
            part = dot(hit, term)
            total = part if total is None else total + part
        for k, block_k in enumerate(blocks128(total.astype(BF16))):
            out_ref[:, k * boxes : (k + 1) * boxes, :] = block_k.reshape(leaves, boxes, LANES)

    pushed = call(
        push_body,
        shape((leaves, leaf_rows, LANES), BF16),
        80_000_000,
        [pltpu.VMEM((3 * count, tall), F32)],
        [VMEM] * 6,
        40,
    )(offsets, vel_cot, m2l_ops, shell, leaf_owner, leaf_place)

    def pack_body(pushed_ref, *refs):
        *up_refs, out_ref = refs
        total = up_refs[0][...]
        for ref in up_refs[1:]:
            total = total + ref[...]
        out_ref[:, :leaf_rows, :] = pushed_ref[...]
        out_ref[:, leaf_rows:, :] = jnp.broadcast_to(
            total.astype(BF16)[None], (leaves, up_rows, LANES)
        )

    sent = call(
        pack_body, shape((leaves, leaf_rows + up_rows, LANES), BF16), 1_000_000, (), [VMEM] * (1 + lvls)
    )(pushed, *ups)
    got = lax.all_to_all(sent, "leaf", split_axis=0, concat_axis=0, tiled=True)

    def near_body(
        q_ref, dir_ref, offsets_ref, vel_ref, owner_ref, place_ref, map_ref, near_ref, sel_ref, split_ref, source
    ):
        mapped = map_ref[...]
        high = mapped.astype(BF16)
        split_ref[0] = high
        split_ref[1] = (mapped - high.astype(F32)).astype(BF16)
        mine = lax.axis_index("leaf") * parents
        coarse = leaves * parents
        pick = jnp.concatenate(
            [
                (
                    owner_ref[c] * parents + place_ref[c : c + 1, :]
                    == mine + iota((8, coarse), 0) % parents
                ).astype(F32)
                for c in range(classes)
            ],
            0,
        ).astype(BF16)
        spread = (coarse, leaves * up_rows)
        lane = iota(spread, 1)
        for k in range(pieces):
            expand = (iota(spread, 0) == lane // up_rows * parents + lane % parents) & (
                lane % up_rows // parents == k
            )
            sel_ref[k] = dot(pick, expand.astype(F32).astype(BF16)).astype(BF16)

        source[...] = jnp.concatenate(
            [offsets_ref[...], vel_ref[...], jnp.zeros((2, tall), F32)], 0
        ).T
        near_ref[...] = jnp.zeros_like(near_ref)
        left = iota((8, LANES), 1) < per_box

        def block(j, _):
            lanes = pl.ds(pl.multiple_of(j * LANES, LANES), LANES)
            target = rows3(offsets_ref, lanes)
            force = [jnp.zeros((8, LANES), F32) for _ in range(3)]
            for n in range(slots):
                qs = [q_ref[n, 2 * j + h] * per_box for h in range(2)]
                codes = [dir_ref[n, 2 * j + h] for h in range(2)]
                moves = [
                    (lax.div(code, 9) - 1, lax.rem(lax.div(code, 3), 3) - 1, lax.rem(code, 3) - 1)
                    for code in codes
                ]
                here = [
                    target[c]
                    - jnp.where(left, moves[0][c].astype(F32), moves[1][c].astype(F32))
                    for c in range(3)
                ]
                for row in range(0, per_box, 8):
                    tiles = [source[pl.ds(pl.multiple_of(q + row, 8), 8), :] for q in qs]
                    both = [
                        jnp.where(left, tiles[0][:, c : c + 1], tiles[1][:, c : c + 1])
                        for c in range(6)
                    ]
                    part = stokeslet([here[c] - both[c] for c in range(3)], both[3:])
                    force = [force[c] + part[c] for c in range(3)]
            p, lvl = lax.div(j, lvls), lax.rem(j, lvls)
            for c in range(3):
                near_ref[lvl, pl.ds(p * 4 + c, 1), :] = jnp.sum(force[c], 0, keepdims=True)
            return 0

        lax.fori_loop(0, groups, block, 0)

    near, select, map_split = call(
        near_body,
        (
            shape((lvls, parents * 4, LANES), F32),
            shape((pieces, 8 * classes, leaves * up_rows), BF16),
            shape((2, width, width), BF16),
        ),
        100_000_000,
        [pltpu.VMEM((tall, 8), F32)],
        [SMEM, SMEM] + [VMEM] * 5,
        40,
    )(near_q, near_d, offsets, vel_cot, coarse_owner, coarse_place, check_map)

    def mid_body(got_ref, sel_ref, m2l_ref, near_ref, *refs):
        *out_refs, leaf_sum = refs
        me = lax.axis_index("lvl")
        leaf_sum[...] = jnp.sum(got_ref[:, :leaf_rows, :].astype(F32), 0)
        tops = got_ref[:, leaf_rows:, :].reshape(leaves * up_rows, LANES)
        chosen = jnp.concatenate([dot(sel_ref[k], tops) for k in range(pieces)], 1)
        high = chosen.astype(BF16).astype(F32)
        parts = jnp.where(iota(chosen.shape, 0) % 8 < parents, high, chosen - high)
        parts = parts[:, :width].astype(BF16)
        total = dot(parts[0:8], m2l_ref[0])
        for c in range(1, classes):
            total = total + dot(parts[8 * c : 8 * c + 8], m2l_ref[c])
        total = 0.5 * (total[0:parents] + total[parents : 2 * parents])
        total_blocks = blocks128(total)
        for k, out_ref in enumerate(out_refs):
            peer = lax.rem(me + k, lvls)
            for i, block in enumerate(total_blocks):
                out_ref[i * parents : (i + 1) * parents, :] = block.astype(out_ref.dtype)
            for i in range(pieces):
                rows = leaf_sum[pl.ds(pl.multiple_of(i * boxes + peer * own, own), own), :]
                out_ref[up_rows + i * own : up_rows + (i + 1) * own, :] = rows.astype(out_ref.dtype)
            out_ref[up_rows + own_rows :, :] = near_ref[peer].astype(out_ref.dtype)

    pay_rows = up_rows + own_rows + parents * 4
    mids = call(
        mid_body,
        tuple(shape((pay_rows, LANES), BF16 if k else F32) for k in range(lvls)),
        20_000_000,
        [pltpu.VMEM((leaf_rows, LANES), F32)],
        [VMEM] * 4,
    )(got, select, m2l_ops, near)
    mids = [mids[0]] + [shifted(mids[k], k) for k in range(1, lvls)]

    def down_body(child_ref, split_ref, offsets_ref, shell_ref, *refs):
        *mid_refs, out_ref, dens = refs
        me = lax.axis_index("lvl")
        total = mid_refs[0][...]
        for ref in mid_refs[1:]:
            total = total + ref[...].astype(F32)
        top = jnp.concatenate(
            [total[k * parents : (k + 1) * parents] for k in range(pieces)], 1
        )[:, :width].astype(BF16)
        lowered = jnp.concatenate([dot(top, child_ref[o], NT) for o in range(octants)], 0)
        leaf = jnp.concatenate(
            [total[up_rows + k * own : up_rows + (k + 1) * own] for k in range(pieces)], 1
        )[:, :width]
        mult = leaf + lowered
        high = mult.astype(BF16)
        pair = jnp.concatenate([high.astype(F32), mult - high.astype(F32)], 0).astype(BF16)
        first, second = dot(pair, split_ref[0]), dot(pair, split_ref[1])
        check = first[0:own] + first[own:] + second[0:own] + second[own:]
        high = check.astype(BF16).astype(F32)
        pair = jnp.concatenate([high, check - high], 0).astype(BF16)
        here = parents * LANES
        lane = iota((2 * own, here), 1)
        box = lane % LANES // per_box * parents + lane // LANES
        hit = (iota((2 * own, here), 0) % own == box).astype(F32).astype(BF16)
        dens[...] = dot(pair, hit, TN)
        out_ref[...] = total[up_rows + own_rows :]
        for p in range(parents):
            target = rows3(offsets_ref, lanes_of(p, me))
            lanes = slice(p * LANES, (p + 1) * LANES)
            force = [jnp.zeros((8, LANES), F32) for _ in range(3)]
            for row in range(0, count, 8):
                d = [target[c] - shell_ref[row : row + 8, c : c + 1] for c in range(3)]
                q = [dens[c * count + row : c * count + row + 8, lanes] for c in range(3)]
                part = stokeslet(d, q)
                force = [force[c] + part[c] for c in range(3)]
            for c in range(3):
                row = p * 4 + c
                out_ref[row : row + 1, :] += jnp.sum(force[c], 0, keepdims=True)

    forces = call(
        down_body,
        shape((parents * 4, LANES), F32),
        20_000_000,
        [pltpu.VMEM((3 * count, parents * LANES), F32)],
        [VMEM] * (4 + lvls),
    )(child_ops, map_split, offsets, shell, *mids)
    forces = [forces] + [shifted(forces, k) for k in range(1, lvls)]

    def join_body(*refs):
        *parts, out_ref = refs
        me = lax.axis_index("lvl")
        for k, ref in enumerate(parts):
            peer = lax.rem(me + lvls - k, lvls)
            for p in range(parents):
                out_ref[:, lanes_of(p, peer)] = ref[p * 4 : p * 4 + 3, :]

    return call(join_body, shape((3, tall), F32), 100_000, (), [VMEM] * lvls)(*forces)


def solution(mesh):
    placed = (
        P(None, "leaf"),
        P(None, "leaf"),
        P("lvl", None, None),
        P("lvl", None, None),
        P(),
        P("lvl", "leaf", None, None),
        P("lvl", "leaf", None),
        P("lvl", None, None, None),
        P("lvl", None, None),
        P("leaf", "lvl"),
        P("leaf", "lvl"),
    )
    return jax.shard_map(
        local, mesh=mesh, in_specs=placed, out_specs=P(None, "leaf"), check_vma=False
    )
```

time: 123 us -> 51.7 us (0.42)
  blocking collectives: 53.6 us -> 0 us
  other arithmetic: 26 us -> 0 us
  Pallas kernels: 0 us -> 20.8 us
  local copies, waits for them, and re-layouts: 16.3 us -> 11 us
  matrix products: 4.62 us -> 0 us
  waiting for transfers between devices: 7.28 us -> 5.19 us
    all_gather x1 -> x0, blocking collectives: 30.9 us -> none  [local(): lax.all_gather(parent_local, 'leaf', axis=0, tiled=True)]
    psum x3 -> x0, blocking collectives: 22.7 us -> none  [the longest x1 10.6 us: local(): lax.psum(leaf_part.astype(jnp.bfloat16), 'lvl').astype(jnp.float32)]
    pallas_call x0 -> x7, Pallas kernels: none -> 20.8 us  [the longest x1 12.6 us: local(): call(near_body, (shape((lvls, parents * 4, LANES), F32), shape((pieces, 8...]
    reduce_sum x25 -> x0, other arithmetic: 19.9 us -> none  [the longest x12 9.45 us: stokes_apply(): squared = jnp.sum(relative * relative, axis=0)]
    unnamed x17 -> x44, local copies, waits for them, and re-layouts: 1.18 us -> 11 us
    ppermute x0 -> x9, starting transfers between devices: none -> 7.84 us  [shifted(): lax.ppermute(value, 'lvl', [(i, (i + k) % lvls) for i in range(lvls)])]
    all_to_all x2 -> x1, waiting for transfers between devices: 7.28 us -> 0.01 us  [local(): got = lax.all_to_all(sent, 'leaf', split_axis=0, concat_axis=0, tiled=True)]
    all_to_all x2 -> x1, starting transfers between devices: 12.7 us -> 5.94 us  [local(): got = lax.all_to_all(sent, 'leaf', split_axis=0, concat_axis=0, tiled=True)]
  transfers between devices with their start and end apart: 2 -> 10, of which waited for: 1 -> 5; matrix products, arithmetic and copies ran while one was open for 29% -> 0% of each run, Pallas kernels for 0% -> 33%
where the time goes in v1:
time: 51.7 us; the launch traced here: 51 us
  Pallas kernels  20.8 us (40%)
  starting transfers between devices  13.8 us (27%)
  local copies, waits for them, and re-layouts  11 us (21%)
  waiting for transfers between devices  5.19 us (10%)
    pallas_call x1, Pallas kernels, local(): call(near_body, (shape((lvls, parents * 4, LANES), F32), shape((pieces, 8...  12.6 us
    unnamed x44, local copies, waits for them, and re-layouts  11 us
    ppermute x9, starting transfers between devices, shifted(): lax.ppermute(value, 'lvl', [(i, (i + k) % lvls) for i in range(lvls)])  7.84 us
    all_to_all x1, starting transfers between devices, local(): got = lax.all_to_all(sent, 'leaf', split_axis=0, concat_axis=0, tiled=True)  5.94 us
    ppermute x9, waiting for transfers between devices, shifted(): lax.ppermute(value, 'lvl', [(i, (i + k) % lvls) for i in range(lvls)])  5.19 us
    pallas_call x1, Pallas kernels, local(): call(push_body, shape((leaves, leaf_rows, LANES), BF16), 80000000, [pltpu...  4.45 us
    pallas_call x1, Pallas kernels, local(): call(down_body, shape((parents * 4, LANES), F32), 20000000, [pltpu.VMEM((...  1.11 us
  transfers between devices with their start and end apart: 10, of which 5 were waited for; matrix products, arithmetic and copies ran while one was open for 0% of the time, Pallas kernels for 33%

profile of v1, /device:TPU:0, one launch (start us, length us, event | category | flops | bytes accessed | tf_op | source)
XLA Modules:
  0.0 51.0 jit_solution(12798296754324004656)
XLA Ops:
  0.0 1.2 %copy-done.2 = bf16[2,456,456]{2,1,0:T(8,128)(2,1)S(1)} copy-done((bf16[2,456,456]{2,1,0:T(8,128)(2,1)S(1)}, bf16[2,456,456]{2,1,0:T(8,128)(2,1)}, u32[]{:S(2)}) %copy-start.2) | copy-done | bytes 831768
  1.2 0.9 %copy-done.7 = f32[152,128]{1,0:T(8,128)S(1)} copy-done((f32[152,128]{1,0:T(8,128)S(1)}, f32[152,128]{1,0:T(8,128)}, u32[]{:S(2)}) %copy-start.7) | copy-done | bytes 77848
  2.1 0.8 %copy-done.10 = f32[3,2048]{1,0:T(4,128)S(1)} copy-done((f32[3,2048]{1,0:T(4,128)S(1)}, f32[3,2048]{1,0:T(4,128)}, u32[]{:S(2)}) %copy-start.10) | copy-done | bytes 24600
  2.8 0.8 %copy-done.13 = f32[3,2048]{1,0:T(4,128)S(1)} copy-done((f32[3,2048]{1,0:T(4,128)S(1)}, f32[3,2048]{1,0:T(4,128)}, u32[]{:S(2)}) %copy-start.13) | copy-done | bytes 24600
  3.6 0.0 copy-start.21
  3.6 0.8 %shard_map.120.refs_0_ = f32[16,128]{1,0:T(8,128)S(1)} custom-call(f32[3,2048]{1,0:T(4,128)S(1)} %copy-done.10, f32[3,2048]{1,0:T(4,128)S(1)} %copy-done.13, bf16[2,456,456]{2,1,0:T(8,128)(2,1)S(1)} %copy-done.2, f32[152,128]{1,0:T(8,128)S(1)} %copy-done.7), custom_call_target="tpu_custom_call" | custom-call | flops 20000000 | bytes 1048576 | tf_op jit(solution)/shard_map/pallas_call | solution.py:148
  4.4 2.4 %collective-permute-start.2 = (f32[16,128]{1,0:T(8,128)S(1)}, f32[16,128]{1,0:T(8,128)S(1)}, u32[]{:S(2)}, u32[]{:S(2)}) collective-permute-start(f32[16,128]{1,0:T(8,128)S(1)} %shard_map.120.refs_0_), channel_id=1, source_target_pairs={{0,3},{1,0},{2,1},{3,2},{4,7},{5,4},{6,5},{7,6},{8,11},{9,8},{10,9... | collective-permute-start | bytes 24584 | tf_op jit(solution)/shard_map/ppermute | solution.py:157
  6.9 0.6 %collective-permute-start.1 = (f32[16,128]{1,0:T(8,128)S(1)}, f32[16,128]{1,0:T(8,128)S(1)}, u32[]{:S(2)}, u32[]{:S(2)}) collective-permute-start(f32[16,128]{1,0:T(8,128)S(1)} %shard_map.120.refs_0_), channel_id=1, source_target_pairs={{0,2},{1,3},{2,0},{3,1},{4,6},{5,7},{6,4},{7,5},{8,10},{9,11},{10,... | collective-permute-start | bytes 24584 | tf_op jit(solution)/shard_map/ppermute | solution.py:157
  7.5 0.2 collective-permute-start
  7.7 1.5 %copy-done = bf16[4,456,456]{2,1,0:T(8,128)(2,1)S(1)} copy-done((bf16[4,456,456]{2,1,0:T(8,128)(2,1)S(1)}, bf16[4,456,456]{2,1,0:T(8,128)(2,1)}, u32[]{:S(2)}) %copy-start) | copy-done | bytes 1663512
  9.2 0.9 %copy-done.8 = f32[152,128]{1,0:T(8,128)S(1)} copy-done((f32[152,128]{1,0:T(8,128)S(1)}, f32[152,128]{1,0:T(8,128)}, u32[]{:S(2)}) %copy-start.8) | copy-done | bytes 77848
  10.1 0.8 %copy-done.11 = f32[3,2048]{1,0:T(4,128)S(1)} copy-done((f32[3,2048]{1,0:T(4,128)S(1)}, f32[3,2048]{1,0:T(4,128)}, u32[]{:S(2)}) %copy-start.11) | copy-done | bytes 24600
  10.8 0.8 %copy-done.14 = f32[3,2048]{1,0:T(4,128)S(1)} copy-done((f32[3,2048]{1,0:T(4,128)S(1)}, f32[3,2048]{1,0:T(4,128)}, u32[]{:S(2)}) %copy-start.14) | copy-done | bytes 24600
  11.6 0.7 %copy-done.16 = s32[1,32,4,1]{1,3,2,0:T(1,128)S(1)} copy-done((s32[1,32,4,1]{1,3,2,0:T(1,128)S(1)}, s32[1,32,4,1]{1,3,2,0:T(1,128)}, u32[]{:S(2)}) %copy-start.16) | copy-done | bytes 536
  12.3 0.7 %copy-done.17 = s32[1,32,4]{1,2,0:T(4,128)S(1)} copy-done((s32[1,32,4]{1,2,0:T(4,128)S(1)}, s32[1,32,4]{1,2,0:T(4,128)}, u32[]{:S(2)}) %copy-start.17) | copy-done | bytes 536
  12.9 4.4 %shard_map.119.pushed_ref = bf16[8,128,128]{2,1,0:T(8,128)(2,1)S(1)} custom-call(f32[3,2048]{1,0:T(4,128)S(1)} %copy-done.11, f32[3,2048]{1,0:T(4,128)S(1)} %copy-done.14, bf16[4,456,456]{2,1,0:T(8,128)(2,1)S(1)} %copy-done, f32[152,128]{1,0:T(8,128)S(1)} %copy-done.8, s32[4,1,32]{2,1,0:T(1,128)S(1)} %bitcast.18, s32[4,32]{1,0:T(4,128)S(1)} %bitcast.19), custom_call_target="tpu_custom_call" | custom-call | flops 80000000 | bytes 1048576 | tf_op jit(solution)/shard_map/pallas_call | solution.py:189
  17.4 0.0 collective-permute-done.2.refs_3_
  17.4 0.0 collective-permute-done.1.refs_2_
  17.4 0.0 collective-permute-done.refs_1_
  17.4 0.0 copy-start.9
  17.4 0.7 %shard_map.121 = bf16[8,144,128]{2,1,0:T(8,128)(2,1)} custom-call(bf16[8,128,128]{2,1,0:T(8,128)(2,1)S(1)} %shard_map.119.pushed_ref, f32[16,128]{1,0:T(8,128)S(1)} %shard_map.120.refs_0_, f32[16,128]{1,0:T(8,128)S(1)} %collective-permute-done.refs_1_, f32[16,128]{1,0:T(8,128)S(1)} %collective-permute-done.1.refs_2_, ...), custom_call_target="tpu_custom_call" | custom-call | flops 1000000 | bytes 1048576 | tf_op jit(solution)/shard_map/pallas_call | solution.py:208
  18.2 5.9 %all-to-all-start = ((bf16[8,144,128]{2,1,0:T(8,128)(2,1)}), bf16[8,144,128]{2,1,0:T(8,128)(2,1)S(1)}, u32[]{:S(2)}, u32[]{:S(2)}) async-start(bf16[8,144,128]{2,1,0:T(8,128)(2,1)} %shard_map.121), calls=%async_computation | async-start | bytes 589824 | tf_op jit(solution)/shard_map/all_to_all | solution.py:211
  24.1 0.0 copy-done.12
  24.1 0.0 copy-done.15
  24.1 0.0 copy-done.19
  24.2 0.0 copy-start.4
  24.2 1.2 %copy-done.4 = f32[456,456]{1,0:T(8,128)S(1)} copy-done((f32[456,456]{1,0:T(8,128)S(1)}, f32[456,456]{1,0:T(8,128)}, u32[]{:S(2)}) %copy-start.4) | copy-done | bytes 831768
  25.4 12.6 %shard_map.118 = (f32[4,16,128]{2,1,0:T(8,128)S(1)}, bf16[4,32,128]{2,1,0:T(8,128)(2,1)S(1)}, bf16[2,456,456]{2,1,0:T(8,128)(2,1)S(1)}) custom-call(s32[4,32]{1,0:T(4,128)S(1)} %bitcast.20, s32[4,32]{1,0:T(4,128)S(1)} %bitcast.21, f32[3,2048]{1,0:T(4,128)S(1)} %copy-done.12, f32[3,2048]{1,0:T(4,128)S(1)} %copy-done.15, s32[4,1,32]{2,1,0:T(1,128)S(1)} %bitcast.22, ...), custom_call_target="tpu_custom_call" | custom-call | flops 100000000 | bytes 1048576 | tf_op jit(solution)/shard_map/pallas_call | solution.py:277
  38.0 0.0 copy-start.5
  38.0 0.9 %copy-done.5 = bf16[2,456,456]{2,1,0:T(8,128)(2,1)} copy-done((bf16[2,456,456]{2,1,0:T(8,128)(2,1)}, bf16[2,456,456]{2,1,0:T(8,128)(2,1)S(1)}, u32[]{:S(2)}) %copy-start.5) | copy-done | bytes 831768
  38.9 0.0 all-to-all-done.got_ref
  38.9 0.0 copy-done.1
  38.9 0.5 shard_map.122
  39.4 1.1 %collective-permute-start.3 = (bf16[64,128]{1,0:T(8,128)(2,1)S(1)}, bf16[64,128]{1,0:T(8,128)(2,1)S(1)}, u32[]{:S(2)}, u32[]{:S(2)}) collective-permute-start(bf16[64,128]{1,0:T(8,128)(2,1)S(1)} %get-tuple-element.16), channel_id=1, source_target_pairs={{0,1},{1,2},{2,3},{3,0},{4,5},{5,6},{6,7},{7,4},{8,9},{9,10},{10,1... | collective-permute-start | bytes 49160 | tf_op jit(solution)/shard_map/ppermute | solution.py:157
  40.5 0.6 %collective-permute-start.4 = (bf16[64,128]{1,0:T(8,128)(2,1)S(1)}, bf16[64,128]{1,0:T(8,128)(2,1)S(1)}, u32[]{:S(2)}, u32[]{:S(2)}) collective-permute-start(bf16[64,128]{1,0:T(8,128)(2,1)S(1)} %get-tuple-element.17), channel_id=1, source_target_pairs={{0,2},{1,3},{2,0},{3,1},{4,6},{5,7},{6,4},{7,5},{8,10},{9,11},{10,... | collective-permute-start | bytes 49160 | tf_op jit(solution)/shard_map/ppermute | solution.py:157
  41.1 1.0 %collective-permute-start.5 = (bf16[64,128]{1,0:T(8,128)(2,1)S(1)}, bf16[64,128]{1,0:T(8,128)(2,1)S(1)}, u32[]{:S(2)}, u32[]{:S(2)}) collective-permute-start(bf16[64,128]{1,0:T(8,128)(2,1)S(1)} %get-tuple-element.18), channel_id=1, source_target_pairs={{0,3},{1,0},{2,1},{3,2},{4,7},{5,4},{6,5},{7,6},{8,11},{9,8},{10,9... | collective-permute-start | bytes 49160 | tf_op jit(solution)/shard_map/ppermute | solution.py:157
  42.1 0.5 collective-permute-done.3.refs_1_
  42.6 1.6 %collective-permute-done.4.refs_2_ = bf16[64,128]{1,0:T(8,128)(2,1)S(1)} collective-permute-done((bf16[64,128]{1,0:T(8,128)(2,1)S(1)}, bf16[64,128]{1,0:T(8,128)(2,1)S(1)}, u32[]{:S(2)}, u32[]{:S(2)}) %collective-permute-start.4) | collective-permute-done | bytes 16416 | tf_op jit(solution)/shard_map/ppermute | solution.py:157
  44.2 0.0 collective-permute-done.5.refs_3_
  44.2 0.0 copy-done.9
  44.2 1.1 %shard_map.123.refs_0_ = f32[16,128]{1,0:T(8,128)S(1)} custom-call(bf16[2,456,456]{2,1,0:T(8,128)(2,1)S(1)} %copy-done.3, bf16[2,456,456]{2,1,0:T(8,128)(2,1)S(1)} %copy-done.6, f32[3,2048]{1,0:T(4,128)S(1)} %copy-done.12, f32[152,128]{1,0:T(8,128)S(1)} %copy-done.9, f32[64,128]{1,0:T(8,128)S(1)} %get-tuple-element.15.refs_0_, ...), custom_call_target="tpu_custom_call" | custom-call | flops 20000000 | bytes 1048576 | tf_op jit(solution)/shard_map/pallas_call | solution.py:362
  45.4 1.1 %collective-permute-start.8 = (f32[16,128]{1,0:T(8,128)S(1)}, f32[16,128]{1,0:T(8,128)S(1)}, u32[]{:S(2)}, u32[]{:S(2)}) collective-permute-start(f32[16,128]{1,0:T(8,128)S(1)} %shard_map.123.refs_0_), channel_id=1, source_target_pairs={{0,3},{1,0},{2,1},{3,2},{4,7},{5,4},{6,5},{7,6},{8,11},{9,8},{10,9... | collective-permute-start | bytes 24584 | tf_op jit(solution)/shard_map/ppermute | solution.py:157
  46.5 0.8 %collective-permute-start.7 = (f32[16,128]{1,0:T(8,128)S(1)}, f32[16,128]{1,0:T(8,128)S(1)}, u32[]{:S(2)}, u32[]{:S(2)}) collective-permute-start(f32[16,128]{1,0:T(8,128)S(1)} %shard_map.123.refs_0_), channel_id=1, source_target_pairs={{0,2},{1,3},{2,0},{3,1},{4,6},{5,7},{6,4},{7,5},{8,10},{9,11},{10,... | collective-permute-start | bytes 24584 | tf_op jit(solution)/shard_map/ppermute | solution.py:157
  47.3 0.0 collective-permute-start.6
  47.3 0.6 %collective-permute-done.8.refs_3_ = f32[16,128]{1,0:T(8,128)S(1)} collective-permute-done((f32[16,128]{1,0:T(8,128)S(1)}, f32[16,128]{1,0:T(8,128)S(1)}, u32[]{:S(2)}, u32[]{:S(2)}) %collective-permute-start.8) | collective-permute-done | bytes 8224 | tf_op jit(solution)/shard_map/ppermute | solution.py:157
  47.8 2.3 %collective-permute-done.7.refs_2_ = f32[16,128]{1,0:T(8,128)S(1)} collective-permute-done((f32[16,128]{1,0:T(8,128)S(1)}, f32[16,128]{1,0:T(8,128)S(1)}, u32[]{:S(2)}, u32[]{:S(2)}) %collective-permute-start.7) | collective-permute-done | bytes 8224 | tf_op jit(solution)/shard_map/ppermute | solution.py:157
  50.1 0.2 collective-permute-done.6.refs_1_
  50.3 0.6 %shard_map.124 = f32[3,2048]{1,0:T(4,128)} custom-call(f32[16,128]{1,0:T(8,128)S(1)} %shard_map.123.refs_0_, f32[16,128]{1,0:T(8,128)S(1)} %collective-permute-done.6.refs_1_, f32[16,128]{1,0:T(8,128)S(1)} %collective-permute-done.7.refs_2_, f32[16,128]{1,0:T(8,128)S(1)} %collective-permute-done.8.refs_3_), custom_call_target="tpu_custom_call" | custom-call | flops 100000 | bytes 1048576 | tf_op jit(solution)/shard_map/pallas_call | solution.py:379
  (23 shorter events, 0.0 us)
Async XLA Ops:
  0.0 1.2 %copy-start.2 = (bf16[2,456,456]{2,1,0:T(8,128)(2,1)S(1)}, bf16[2,456,456]{2,1,0:T(8,128)(2,1)}, u32[]{:S(2)}) copy-start(bf16[2,456,456]{2,1,0:T(8,128)(2,1)} %child_ref.3) | copy-start | bytes 2495236
  1.2 0.9 %copy-start.7 = (f32[152,128]{1,0:T(8,128)S(1)}, f32[152,128]{1,0:T(8,128)}, u32[]{:S(2)}) copy-start(f32[152,128]{1,0:T(8,128)} %constant.2.clone.shell_ref) | copy-start | bytes 233476
  2.1 0.8 %copy-start.10 = (f32[3,2048]{1,0:T(4,128)S(1)}, f32[3,2048]{1,0:T(4,128)}, u32[]{:S(2)}) copy-start(f32[3,2048]{1,0:T(4,128)} %offsets_ref.7) | copy-start | bytes 73732
  2.8 0.8 %copy-start.13 = (f32[3,2048]{1,0:T(4,128)S(1)}, f32[3,2048]{1,0:T(4,128)}, u32[]{:S(2)}) copy-start(f32[3,2048]{1,0:T(4,128)} %vel_ref.5) | copy-start | bytes 73732
  3.6 20.5 %copy-start.12 = (f32[3,2048]{1,0:T(4,128)S(1)}, f32[3,2048]{1,0:T(4,128)}, u32[]{:S(2)}) copy-start(f32[3,2048]{1,0:T(4,128)} %offsets_ref.7) | copy-start | bytes 73732
  3.6 20.5 %copy-start.15 = (f32[3,2048]{1,0:T(4,128)S(1)}, f32[3,2048]{1,0:T(4,128)}, u32[]{:S(2)}) copy-start(f32[3,2048]{1,0:T(4,128)} %vel_ref.5) | copy-start | bytes 73732
  3.6 20.5 %copy-start.19 = (s32[32,4]{0,1:T(4,128)S(1)}, s32[32,4]{0,1:T(4,128)}, u32[]{:S(2)}) copy-start(s32[32,4]{0,1:T(4,128)} %param.22) | copy-start | bytes 1540
  3.6 20.5 %copy-start.20 = (s32[1,32,4,1]{1,3,2,0:T(1,128)S(1)}, s32[1,32,4,1]{1,3,2,0:T(1,128)}, u32[]{:S(2)}) copy-start(s32[1,32,4,1]{1,3,2,0:T(1,128)} %param.19) | copy-start | bytes 1540
  3.6 20.5 %copy-start.21 = (s32[1,32,4]{1,2,0:T(4,128)S(1)}, s32[1,32,4]{1,2,0:T(4,128)}, u32[]{:S(2)}) copy-start(s32[1,32,4]{1,2,0:T(4,128)} %param.20) | copy-start | bytes 1540
  4.4 19.7 %copy-start.18 = (s32[32,4]{0,1:T(4,128)S(1)}, s32[32,4]{0,1:T(4,128)}, u32[]{:S(2)}) copy-start(s32[32,4]{0,1:T(4,128)} %param.21) | copy-start | bytes 1540
  4.4 13.0 %collective-permute-start.2 = (f32[16,128]{1,0:T(8,128)S(1)}, f32[16,128]{1,0:T(8,128)S(1)}, u32[]{:S(2)}, u32[]{:S(2)}) collective-permute-start(f32[16,128]{1,0:T(8,128)S(1)} %shard_map.120.refs_0_), channel_id=1, source_target_pairs={{0,3},{1,0},{2,1},{3,2},{4,7},{5,4},{6,5},{7,6},{8,11},{9,8},{10,9... | collective-permute-start | bytes 24584 | tf_op jit(solution)/shard_map/ppermute | solution.py:157
  6.9 10.5 %collective-permute-start.1 = (f32[16,128]{1,0:T(8,128)S(1)}, f32[16,128]{1,0:T(8,128)S(1)}, u32[]{:S(2)}, u32[]{:S(2)}) collective-permute-start(f32[16,128]{1,0:T(8,128)S(1)} %shard_map.120.refs_0_), channel_id=1, source_target_pairs={{0,2},{1,3},{2,0},{3,1},{4,6},{5,7},{6,4},{7,5},{8,10},{9,11},{10,... | collective-permute-start | bytes 24584 | tf_op jit(solution)/shard_map/ppermute | solution.py:157
  7.5 10.0 %collective-permute-start = (f32[16,128]{1,0:T(8,128)S(1)}, f32[16,128]{1,0:T(8,128)S(1)}, u32[]{:S(2)}, u32[]{:S(2)}) collective-permute-start(f32[16,128]{1,0:T(8,128)S(1)} %shard_map.120.refs_0_), channel_id=1, source_target_pairs={{0,1},{1,2},{2,3},{3,0},{4,5},{5,6},{6,7},{7,4},{8,9},{9,10},{10,1... | collective-permute-start | bytes 24584 | tf_op jit(solution)/shard_map/ppermute | solution.py:157
  7.7 1.5 %copy-start = (bf16[4,456,456]{2,1,0:T(8,128)(2,1)S(1)}, bf16[4,456,456]{2,1,0:T(8,128)(2,1)}, u32[]{:S(2)}) copy-start(bf16[4,456,456]{2,1,0:T(8,128)(2,1)} %m2l_ref.3) | copy-start | bytes 4990468
  9.2 0.9 %copy-start.8 = (f32[152,128]{1,0:T(8,128)S(1)}, f32[152,128]{1,0:T(8,128)}, u32[]{:S(2)}) copy-start(f32[152,128]{1,0:T(8,128)} %constant.2.clone.shell_ref) | copy-start | bytes 233476
  10.1 0.8 %copy-start.11 = (f32[3,2048]{1,0:T(4,128)S(1)}, f32[3,2048]{1,0:T(4,128)}, u32[]{:S(2)}) copy-start(f32[3,2048]{1,0:T(4,128)} %offsets_ref.7) | copy-start | bytes 73732
  10.8 0.8 %copy-start.14 = (f32[3,2048]{1,0:T(4,128)S(1)}, f32[3,2048]{1,0:T(4,128)}, u32[]{:S(2)}) copy-start(f32[3,2048]{1,0:T(4,128)} %vel_ref.5) | copy-start | bytes 73732
  11.6 0.7 %copy-start.16 = (s32[1,32,4,1]{1,3,2,0:T(1,128)S(1)}, s32[1,32,4,1]{1,3,2,0:T(1,128)}, u32[]{:S(2)}) copy-start(s32[1,32,4,1]{1,3,2,0:T(1,128)} %param.17) | copy-start | bytes 1540
  12.3 0.7 %copy-start.17 = (s32[1,32,4]{1,2,0:T(4,128)S(1)}, s32[1,32,4]{1,2,0:T(4,128)}, u32[]{:S(2)}) copy-start(s32[1,32,4]{1,2,0:T(4,128)} %param.18) | copy-start | bytes 1540
  12.9 26.0 %copy-start.1 = (bf16[4,456,456]{2,1,0:T(8,128)(2,1)S(1)}, bf16[4,456,456]{2,1,0:T(8,128)(2,1)}, u32[]{:S(2)}) copy-start(bf16[4,456,456]{2,1,0:T(8,128)(2,1)} %m2l_ref.3) | copy-start | bytes 4990468
  17.4 26.8 %copy-start.9 = (f32[152,128]{1,0:T(8,128)S(1)}, f32[152,128]{1,0:T(8,128)}, u32[]{:S(2)}) copy-start(f32[152,128]{1,0:T(8,128)} %constant.2.clone.shell_ref) | copy-start | bytes 233476
  18.2 26.1 %copy-start.3 = (bf16[2,456,456]{2,1,0:T(8,128)(2,1)S(1)}, bf16[2,456,456]{2,1,0:T(8,128)(2,1)}, u32[]{:S(2)}) copy-start(bf16[2,456,456]{2,1,0:T(8,128)(2,1)} %child_ref.3) | copy-start | bytes 2495236
  18.2 20.8 %all-to-all-start = ((bf16[8,144,128]{2,1,0:T(8,128)(2,1)}), bf16[8,144,128]{2,1,0:T(8,128)(2,1)S(1)}, u32[]{:S(2)}, u32[]{:S(2)}) async-start(bf16[8,144,128]{2,1,0:T(8,128)(2,1)} %shard_map.121), calls=%async_computation | async-start | bytes 589824 | tf_op jit(solution)/shard_map/all_to_all | solution.py:211
  24.2 1.2 %copy-start.4 = (f32[456,456]{1,0:T(8,128)S(1)}, f32[456,456]{1,0:T(8,128)}, u32[]{:S(2)}) copy-start(f32[456,456]{1,0:T(8,128)} %map_ref.1) | copy-start | bytes 2495236
  38.0 0.9 %copy-start.5 = (bf16[2,456,456]{2,1,0:T(8,128)(2,1)}, bf16[2,456,456]{2,1,0:T(8,128)(2,1)S(1)}, u32[]{:S(2)}) copy-start(bf16[2,456,456]{2,1,0:T(8,128)(2,1)S(1)} %get-tuple-element.12.split_ref) | copy-start | bytes 2495236
  38.9 5.3 %copy-start.6 = (bf16[2,456,456]{2,1,0:T(8,128)(2,1)S(1)}, bf16[2,456,456]{2,1,0:T(8,128)(2,1)}, u32[]{:S(2)}) copy-start(bf16[2,456,456]{2,1,0:T(8,128)(2,1)} %copy-done.5) | copy-start | bytes 2495236
  39.4 3.2 %collective-permute-start.3 = (bf16[64,128]{1,0:T(8,128)(2,1)S(1)}, bf16[64,128]{1,0:T(8,128)(2,1)S(1)}, u32[]{:S(2)}, u32[]{:S(2)}) collective-permute-start(bf16[64,128]{1,0:T(8,128)(2,1)S(1)} %get-tuple-element.16), channel_id=1, source_target_pairs={{0,1},{1,2},{2,3},{3,0},{4,5},{5,6},{6,7},{7,4},{8,9},{9,10},{10,1... | collective-permute-start | bytes 49160 | tf_op jit(solution)/shard_map/ppermute | solution.py:157
  40.5 3.7 %collective-permute-start.4 = (bf16[64,128]{1,0:T(8,128)(2,1)S(1)}, bf16[64,128]{1,0:T(8,128)(2,1)S(1)}, u32[]{:S(2)}, u32[]{:S(2)}) collective-permute-start(bf16[64,128]{1,0:T(8,128)(2,1)S(1)} %get-tuple-element.17), channel_id=1, source_target_pairs={{0,2},{1,3},{2,0},{3,1},{4,6},{5,7},{6,4},{7,5},{8,10},{9,11},{10,... | collective-permute-start | bytes 49160 | tf_op jit(solution)/shard_map/ppermute | solution.py:157
  41.1 3.1 %collective-permute-start.5 = (bf16[64,128]{1,0:T(8,128)(2,1)S(1)}, bf16[64,128]{1,0:T(8,128)(2,1)S(1)}, u32[]{:S(2)}, u32[]{:S(2)}) collective-permute-start(bf16[64,128]{1,0:T(8,128)(2,1)S(1)} %get-tuple-element.18), channel_id=1, source_target_pairs={{0,3},{1,0},{2,1},{3,2},{4,7},{5,4},{6,5},{7,6},{8,11},{9,8},{10,9... | collective-permute-start | bytes 49160 | tf_op jit(solution)/shard_map/ppermute | solution.py:157
  45.4 2.5 %collective-permute-start.8 = (f32[16,128]{1,0:T(8,128)S(1)}, f32[16,128]{1,0:T(8,128)S(1)}, u32[]{:S(2)}, u32[]{:S(2)}) collective-permute-start(f32[16,128]{1,0:T(8,128)S(1)} %shard_map.123.refs_0_), channel_id=1, source_target_pairs={{0,3},{1,0},{2,1},{3,2},{4,7},{5,4},{6,5},{7,6},{8,11},{9,8},{10,9... | collective-permute-start | bytes 24584 | tf_op jit(solution)/shard_map/ppermute | solution.py:157
  46.5 3.7 %collective-permute-start.7 = (f32[16,128]{1,0:T(8,128)S(1)}, f32[16,128]{1,0:T(8,128)S(1)}, u32[]{:S(2)}, u32[]{:S(2)}) collective-permute-start(f32[16,128]{1,0:T(8,128)S(1)} %shard_map.123.refs_0_), channel_id=1, source_target_pairs={{0,2},{1,3},{2,0},{3,1},{4,6},{5,7},{6,4},{7,5},{8,10},{9,11},{10,... | collective-permute-start | bytes 24584 | tf_op jit(solution)/shard_map/ppermute | solution.py:157
  47.3 3.1 %collective-permute-start.6 = (f32[16,128]{1,0:T(8,128)S(1)}, f32[16,128]{1,0:T(8,128)S(1)}, u32[]{:S(2)}, u32[]{:S(2)}) collective-permute-start(f32[16,128]{1,0:T(8,128)S(1)} %shard_map.123.refs_0_), channel_id=1, source_target_pairs={{0,1},{1,2},{2,3},{3,0},{4,5},{5,6},{6,7},{7,4},{8,9},{9,10},{10,1... | collective-permute-start | bytes 24584 | tf_op jit(solution)/shard_map/ppermute | solution.py:157

commit v2 on v1

--- a/solution.py
+++ b/solution.py
@@ -13,6 +13,7 @@
 F32 = jnp.float32
 BF16 = jnp.bfloat16
 VMEM = pl.BlockSpec(memory_space=pltpu.VMEM)
+HBM = pl.BlockSpec(memory_space=pltpu.HBM)
 SMEM = pl.BlockSpec(memory_space=pltpu.SMEM)
 NN = (((1,), (0,)), ((), ()))
 NT = (((1,), (1,)), ((), ()))
@@ -43,28 +44,33 @@
     return [scale * v[c] + along * d[c] for c in range(3)]
 
 
-def call(body, outs, cost, scratch=(), ins=None, vmem=24):
+def call(body, outs, cost, scratch=(), ins=None, vmem=24, touched=1 << 20):
     return pl.pallas_call(
         body,
         out_shape=outs,
         in_specs=ins,
         out_specs=jax.tree.map(lambda _: VMEM, outs),
         scratch_shapes=list(scratch),
-        cost_estimate=pl.CostEstimate(flops=cost, bytes_accessed=1 << 20, transcendentals=0),
+        cost_estimate=pl.CostEstimate(flops=cost, bytes_accessed=touched, transcendentals=0),
         compiler_params=pltpu.CompilerParams(vmem_limit_bytes=vmem << 20),
     )
 
 
+def in_hbm(*arrays):
+    return [pltpu.with_memory_space_constraint(array, pltpu.HBM) for array in arrays]
+
+
 def shape(dims, dtype):
     return jax.ShapeDtypeStruct(tuple(dims), dtype)
 
 
 def surface_block(points, vectors, shell_ref, fields, column):
-    count = shell_ref.shape[0]
+    count = shell_ref.shape[0] // 3
     for row in range(0, count, 8):
-        d = [shell_ref[row : row + 8, c : c + 1] - points[c] for c in range(3)]
+        spots = [slice(c * count + row, c * count + row + 8) for c in range(3)]
+        d = [shell_ref[spots[c], :] - points[c] for c in range(3)]
         for c, value in enumerate(stokeslet(d, vectors)):
-            fields[c * count + row : c * count + row + 8, column] = value
+            fields[spots[c], column] = value
 
 
 def blocks128(matrix):
@@ -107,7 +113,7 @@
     leaf_rows = pieces * boxes
     own_rows = pieces * own
     tall = groups * LANES
-    shell = jnp.asarray(np.pad(shell_np.T, ((0, 0), (0, LANES - 3))))
+    shell = jnp.asarray(np.repeat(shell_np.reshape(-1, 1), LANES, 1))
 
     leaf_owner = leaf_dest.transpose(0, 2, 3, 1)[0]
     leaf_place = leaf_slot.transpose(0, 2, 1)[0]
@@ -122,8 +128,25 @@
     def rows3(ref, lanes):
         return [ref[c : c + 1, lanes] for c in range(3)]
 
-    def up_body(offsets_ref, vel_ref, child_ref, shell_ref, up_ref, fields):
+    def up_body(
+        offsets_hbm, vel_hbm, child_hbm, shell_hbm, up_ref, offsets_ref, vel_ref, shell_ref, child_ref, fields, sems
+    ):
         me = lax.axis_index("lvl")
+        copies = [
+            pltpu.make_async_copy(source, target, sems.at[i])
+            for i, (source, target) in enumerate(
+                (
+                    (offsets_hbm, offsets_ref),
+                    (vel_hbm, vel_ref),
+                    (shell_hbm, shell_ref),
+                    (child_hbm, child_ref),
+                )
+            )
+        ]
+        for copy in copies:
+            copy.start()
+        for copy in copies[:3]:
+            copy.wait()
         for p in range(parents):
             lanes = lanes_of(p, me)
             surface_block(
@@ -139,36 +162,60 @@
         target = (lane % LANES) // per_box * 8 + lane // LANES
         pick = (row == target).astype(F32).astype(BF16)
         leaf = dot(pick, fields[...].astype(BF16), NT).astype(BF16)
+        copies[3].wait()
         total = dot(leaf[0:8], child_ref[0])
         for o in range(1, octants):
             total = total + dot(leaf[8 * o : 8 * o + 8], child_ref[o])
         for k, block in enumerate(blocks128(total)):
             up_ref[k * parents : (k + 1) * parents, :] = block[0:parents]
 
-    up = call(
+    up, offsets, vel_cot, shell = call(
         up_body,
-        shape((up_rows, LANES), F32),
+        (
+            shape((up_rows, LANES), F32),
+            shape(offsets.shape, F32),
+            shape(vel_cot.shape, F32),
+            shape(shell.shape, F32),
+        ),
         20_000_000,
-        [pltpu.VMEM((3 * count, parents * LANES), F32)],
-        [VMEM] * 4,
-    )(offsets, vel_cot, child_ops, shell)
+        [
+            pltpu.VMEM(child_ops.shape, BF16),
+            pltpu.VMEM((3 * count, parents * LANES), F32),
+            pltpu.SemaphoreType.DMA((4,)),
+        ],
+        [HBM] * 4,
+        40,
+        0,
+    )(*in_hbm(offsets, vel_cot, child_ops, shell))
 
     def shifted(value, k):
         return lax.ppermute(value, "lvl", [(i, (i + k) % lvls) for i in range(lvls)])
 
     ups = [up] + [shifted(up, k) for k in range(1, lvls)]
 
-    def push_body(offsets_ref, vel_ref, m2l_ref, shell_ref, owner_ref, place_ref, out_ref, fields):
-        def block(j, _):
-            lanes = pl.ds(pl.multiple_of(j * LANES, LANES), LANES)
+    def push_body(
+        offsets_ref, vel_ref, shell_ref, m2l_hbm, owner_hbm, place_hbm, out_ref, m2l_ref, owner_ref, place_ref, fields, sems
+    ):
+        copies = [
+            pltpu.make_async_copy(source, target, sems.at[i])
+            for i, (source, target) in enumerate(
+                ((m2l_hbm, m2l_ref), (owner_hbm, owner_ref), (place_hbm, place_ref))
+            )
+        ]
+        for copy in copies:
+            copy.start()
+        leaf = jnp.zeros((boxes, 3 * count), F32)
+        for j in range(groups):
+            lanes = slice(j * LANES, (j + 1) * LANES)
             surface_block(
-                rows3(offsets_ref, lanes), rows3(vel_ref, lanes), shell_ref, fields, lanes
-            )
-            return 0
-
-        lax.fori_loop(0, groups, block, 0)
-        pick = (iota((boxes, tall), 0) == iota((boxes, tall), 1) // per_box).astype(F32)
-        leaf = dot(pick.astype(BF16), fields[...].astype(BF16), NT).astype(BF16)
+                rows3(offsets_ref, lanes), rows3(vel_ref, lanes), shell_ref, fields.at[j % 2], slice(None)
+            )
+            box = iota((boxes, LANES), 1) // per_box + j * LANES // per_box
+            pick = (iota((boxes, LANES), 0) == box).astype(F32).astype(BF16)
+            leaf = leaf + dot(pick, fields[j % 2].astype(BF16), NT)
+        leaf = leaf.astype(BF16)
+        for copy in copies:
+            copy.wait()
         total = None
         for c in range(classes):
             term = dot(leaf, m2l_ref[c]).astype(BF16)
@@ -190,10 +237,17 @@
         push_body,
         shape((leaves, leaf_rows, LANES), BF16),
         80_000_000,
-        [pltpu.VMEM((3 * count, tall), F32)],
-        [VMEM] * 6,
+        [
+            pltpu.VMEM(m2l_ops.shape, BF16),
+            pltpu.VMEM(leaf_owner.shape, jnp.int32),
+            pltpu.VMEM(leaf_place.shape, jnp.int32),
+            pltpu.VMEM((2, 3 * count, LANES), F32),
+            pltpu.SemaphoreType.DMA((3,)),
+        ],
+        [VMEM] * 3 + [HBM] * 3,
         40,
-    )(offsets, vel_cot, m2l_ops, shell, leaf_owner, leaf_place)
+        0,
+    )(offsets, vel_cot, shell, *in_hbm(m2l_ops, leaf_owner, leaf_place))
 
     def pack_body(pushed_ref, *refs):
         *up_refs, out_ref = refs
@@ -211,12 +265,8 @@
     got = lax.all_to_all(sent, "leaf", split_axis=0, concat_axis=0, tiled=True)
 
     def near_body(
-        q_ref, dir_ref, offsets_ref, vel_ref, owner_ref, place_ref, map_ref, near_ref, sel_ref, split_ref, source
+        q_ref, dir_ref, offsets_ref, vel_ref, owner_ref, place_ref, near_ref, sel_ref, columns, table, sums
     ):
-        mapped = map_ref[...]
-        high = mapped.astype(BF16)
-        split_ref[0] = high
-        split_ref[1] = (mapped - high.astype(F32)).astype(BF16)
         mine = lax.axis_index("leaf") * parents
         coarse = leaves * parents
         pick = jnp.concatenate(
@@ -237,55 +287,72 @@
             )
             sel_ref[k] = dot(pick, expand.astype(F32).astype(BF16)).astype(BF16)
 
-        source[...] = jnp.concatenate(
-            [offsets_ref[...], vel_ref[...], jnp.zeros((2, tall), F32)], 0
-        ).T
+        left = iota((8, LANES), 1) < per_box
+        for j in range(groups):
+            lanes = slice(j * LANES, (j + 1) * LANES)
+            tile = jnp.concatenate(
+                [offsets_ref[:, lanes], vel_ref[:, lanes], jnp.zeros((2, LANES), F32)], 0
+            )
+            columns[lanes, :] = tile.T
+            turned = pltpu.roll(tile, per_box, 1)
+            table[2 * j] = jnp.where(left, tile, turned)
+            table[2 * j + 1] = jnp.where(left, turned, tile)
         near_ref[...] = jnp.zeros_like(near_ref)
-        left = iota((8, LANES), 1) < per_box
+        ones = jnp.ones((8, LANES), BF16)
 
         def block(j, _):
-            lanes = pl.ds(pl.multiple_of(j * LANES, LANES), LANES)
-            target = rows3(offsets_ref, lanes)
-            force = [jnp.zeros((8, LANES), F32) for _ in range(3)]
-            for n in range(slots):
-                qs = [q_ref[n, 2 * j + h] * per_box for h in range(2)]
-                codes = [dir_ref[n, 2 * j + h] for h in range(2)]
-                moves = [
-                    (lax.div(code, 9) - 1, lax.rem(lax.div(code, 3), 3) - 1, lax.rem(code, 3) - 1)
-                    for code in codes
-                ]
-                here = [
-                    target[c]
-                    - jnp.where(left, moves[0][c].astype(F32), moves[1][c].astype(F32))
-                    for c in range(3)
-                ]
+            for h in range(2):
+                box = 2 * j + h
+                sources = []
+                for n in range(0, slots, 2):
+                    codes = [dir_ref[n + i, box] for i in range(2)]
+                    moves = [
+                        (
+                            lax.div(code, 9) - 1,
+                            lax.rem(lax.div(code, 3), 3) - 1,
+                            lax.rem(code, 3) - 1,
+                        )
+                        for code in codes
+                    ]
+                    tile = jnp.where(left, table[q_ref[n, box]], table[q_ref[n + 1, box]])
+                    rows = [jnp.broadcast_to(tile[c : c + 1], (8, LANES)) for c in range(6)]
+                    for c in range(3):
+                        rows[c] = rows[c] + jnp.where(
+                            left, moves[0][c].astype(F32), moves[1][c].astype(F32)
+                        )
+                    sources.append(rows)
                 for row in range(0, per_box, 8):
-                    tiles = [source[pl.ds(pl.multiple_of(q + row, 8), 8), :] for q in qs]
-                    both = [
-                        jnp.where(left, tiles[0][:, c : c + 1], tiles[1][:, c : c + 1])
-                        for c in range(6)
-                    ]
-                    part = stokeslet([here[c] - both[c] for c in range(3)], both[3:])
-                    force = [force[c] + part[c] for c in range(3)]
+                    tile = columns[pl.ds(pl.multiple_of(box * per_box + row, 8), 8), :]
+                    target = [jnp.broadcast_to(tile[:, c : c + 1], (8, LANES)) for c in range(3)]
+                    force = None
+                    for rows in sources:
+                        part = stokeslet([target[c] - rows[c] for c in range(3)], rows[3:])
+                        force = part if force is None else [x + y for x, y in zip(force, part)]
+                    for c in range(3):
+                        sums[c, h * per_box + row : h * per_box + row + 8, :] = force[c]
             p, lvl = lax.div(j, lvls), lax.rem(j, lvls)
             for c in range(3):
-                near_ref[lvl, pl.ds(p * 4 + c, 1), :] = jnp.sum(force[c], 0, keepdims=True)
+                total = dot(ones, sums[c].astype(BF16), NT)
+                near_ref[lvl, pl.ds(p * 4 + c, 1), :] = total[0:1]
             return 0
 
         lax.fori_loop(0, groups, block, 0)
 
-    near, select, map_split = call(
+    near, select = call(
         near_body,
         (
             shape((lvls, parents * 4, LANES), F32),
             shape((pieces, 8 * classes, leaves * up_rows), BF16),
-            shape((2, width, width), BF16),
         ),
         100_000_000,
-        [pltpu.VMEM((tall, 8), F32)],
-        [SMEM, SMEM] + [VMEM] * 5,
-        40,
-    )(near_q, near_d, offsets, vel_cot, coarse_owner, coarse_place, check_map)
+        [
+            pltpu.VMEM((tall, 8), F32),
+            pltpu.VMEM((boxes, 8, LANES), F32),
+            pltpu.VMEM((3, LANES, LANES), F32),
+        ],
+        [SMEM, SMEM] + [VMEM] * 4,
+        24,
+    )(near_q, near_d, offsets, vel_cot, coarse_owner, coarse_place)
 
     def mid_body(got_ref, sel_ref, m2l_ref, near_ref, *refs):
         *out_refs, leaf_sum = refs
@@ -320,7 +387,7 @@
     )(got, select, m2l_ops, near)
     mids = [mids[0]] + [shifted(mids[k], k) for k in range(1, lvls)]
 
-    def down_body(child_ref, split_ref, offsets_ref, shell_ref, *refs):
+    def down_body(child_ref, map_ref, offsets_ref, shell_ref, *refs):
         *mid_refs, out_ref, dens = refs
         me = lax.axis_index("lvl")
         total = mid_refs[0][...]
@@ -336,7 +403,10 @@
         mult = leaf + lowered
         high = mult.astype(BF16)
         pair = jnp.concatenate([high.astype(F32), mult - high.astype(F32)], 0).astype(BF16)
-        first, second = dot(pair, split_ref[0]), dot(pair, split_ref[1])
+        mapped = map_ref[...]
+        coarse_map = mapped.astype(BF16)
+        fine_map = (mapped - coarse_map.astype(F32)).astype(BF16)
+        first, second = dot(pair, coarse_map), dot(pair, fine_map)
         check = first[0:own] + first[own:] + second[0:own] + second[own:]
         high = check.astype(BF16).astype(F32)
         pair = jnp.concatenate([high, check - high], 0).astype(BF16)
@@ -351,7 +421,10 @@
             lanes = slice(p * LANES, (p + 1) * LANES)
             force = [jnp.zeros((8, LANES), F32) for _ in range(3)]
             for row in range(0, count, 8):
-                d = [target[c] - shell_ref[row : row + 8, c : c + 1] for c in range(3)]
+                d = [
+                    target[c] - shell_ref[c * count + row : c * count + row + 8, :]
+                    for c in range(3)
+                ]
                 q = [dens[c * count + row : c * count + row + 8, lanes] for c in range(3)]
                 part = stokeslet(d, q)
                 force = [force[c] + part[c] for c in range(3)]
@@ -365,7 +438,7 @@
         20_000_000,
         [pltpu.VMEM((3 * count, parents * LANES), F32)],
         [VMEM] * (4 + lvls),
-    )(child_ops, map_split, offsets, shell, *mids)
+    )(child_ops, check_map, offsets, shell, *mids)
     forces = [forces] + [shifted(forces, k) for k in range(1, lvls)]
 
     def join_body(*refs):

time: 51.7 us -> 37.1 us (0.72)
  local copies, waits for them, and re-layouts: 11 us -> 0.04 us
  Pallas kernels: 20.8 us -> 15.4 us
  starting transfers between devices: 13.8 us -> 15.5 us
  waiting for transfers between devices: 5.19 us -> 5.78 us
    unnamed x44 -> x14, local copies, waits for them, and re-layouts: 11 us -> 0.04 us
    pallas_call x1, Pallas kernels: 12.6 us -> 6.71 us  [local(): call(near_body, (shape((lvls, parents * 4, LANES), F32), shape((pieces, 8...]
    all_to_all x1, waiting for transfers between devices: 0.01 us -> 2.22 us  [local(): got = lax.all_to_all(sent, 'leaf', split_axis=0, concat_axis=0, tiled=True)]
    ppermute x9, starting transfers between devices: 7.84 us -> 9.69 us  [shifted(): lax.ppermute(value, 'lvl', [(i, (i + k) % lvls) for i in range(lvls)])]
    ppermute x9, waiting for transfers between devices: 5.19 us -> 3.56 us  [shifted(): lax.ppermute(value, 'lvl', [(i, (i + k) % lvls) for i in range(lvls)])]
    pallas_call x1, Pallas kernels: 0.81 us -> 1.72 us  [local(): call(up_body, (shape((up_rows, LANES), F32), shape(offsets.shape, F32), s...]
  transfers between devices with their start and end apart: 10 -> 10, of which waited for: 5 -> 6; matrix products, arithmetic and copies ran while one was open for 0% -> 0% of each run, Pallas kernels for 33% -> 29%
where the time goes in v2:
time: 37.1 us; the launch traced here: 36.8 us
  starting transfers between devices  15.5 us (42%)
  Pallas kernels  15.4 us (42%)
  waiting for transfers between devices  5.78 us (16%)
    ppermute x9, starting transfers between devices, shifted(): lax.ppermute(value, 'lvl', [(i, (i + k) % lvls) for i in range(lvls)])  9.69 us
    pallas_call x1, Pallas kernels, local(): call(near_body, (shape((lvls, parents * 4, LANES), F32), shape((pieces, 8...  6.71 us
    all_to_all x1, starting transfers between devices, local(): got = lax.all_to_all(sent, 'leaf', split_axis=0, concat_axis=0, tiled=True)  5.81 us
    pallas_call x1, Pallas kernels, local(): call(push_body, shape((leaves, leaf_rows, LANES), BF16), 80000000, [pltpu...  4.02 us
    ppermute x9, waiting for transfers between devices, shifted(): lax.ppermute(value, 'lvl', [(i, (i + k) % lvls) for i in range(lvls)])  3.56 us
    all_to_all x1, waiting for transfers between devices, local(): got = lax.all_to_all(sent, 'leaf', split_axis=0, concat_axis=0, tiled=True)  2.22 us
    pallas_call x1, Pallas kernels, local(): call(up_body, (shape((up_rows, LANES), F32), shape(offsets.shape, F32), s...  1.72 us
    pallas_call x1, Pallas kernels, local(): call(down_body, shape((parents * 4, LANES), F32), 20000000, [pltpu.VMEM((...  1.08 us
  transfers between devices with their start and end apart: 10, of which 6 were waited for; matrix products, arithmetic and copies ran while one was open for 0% of the time, Pallas kernels for 29%

profile of v2, /device:TPU:0, one launch (start us, length us, event | category | flops | bytes accessed | tf_op | source)
XLA Modules:
  0.0 36.8 jit_solution(8996774033271362456)
XLA Ops:
  0.0 1.7 %shard_map.118 = (f32[16,128]{1,0:T(8,128)S(1)}, f32[3,2048]{1,0:T(4,128)S(1)}, f32[3,2048]{1,0:T(4,128)S(1)}, f32[456,128]{1,0:T(8,128)S(1)}) custom-call(f32[3,2048]{1,0:T(4,128)} %offsets_hbm.1, f32[3,2048]{1,0:T(4,128)} %vel_hbm.1, bf16[2,456,456]{2,1,0:T(8,128)(2,1)} %child_ref.1, f32[456,128]{1,0:T(8,128)} %constant.2.clone.shell_hbm), custom_call_target="tpu_custom_call" | custom-call | flops 20000000 | tf_op jit(solution)/shard_map/pallas_call | solution.py:172
  1.7 0.0 copy-start.3
  1.7 0.0 copy-start.4
  1.7 0.0 copy-start.5
  1.8 0.0 copy-start.6
  1.8 0.5 %collective-permute-start = (f32[16,128]{1,0:T(8,128)S(1)}, f32[16,128]{1,0:T(8,128)S(1)}, u32[]{:S(2)}, u32[]{:S(2)}) collective-permute-start(f32[16,128]{1,0:T(8,128)S(1)} %get-tuple-element.18.refs_0_), channel_id=1, source_target_pairs={{0,1},{1,2},{2,3},{3,0},{4,5},{5,6},{6,7},{7,4},{8,9},{9,10},{10,1... | collective-permute-start | bytes 24584 | tf_op jit(solution)/shard_map/ppermute | solution.py:192
  2.3 2.6 %collective-permute-start.1 = (f32[16,128]{1,0:T(8,128)S(1)}, f32[16,128]{1,0:T(8,128)S(1)}, u32[]{:S(2)}, u32[]{:S(2)}) collective-permute-start(f32[16,128]{1,0:T(8,128)S(1)} %get-tuple-element.18.refs_0_), channel_id=1, source_target_pairs={{0,2},{1,3},{2,0},{3,1},{4,6},{5,7},{6,4},{7,5},{8,10},{9,11},{10,... | collective-permute-start | bytes 24584 | tf_op jit(solution)/shard_map/ppermute | solution.py:192
  4.9 1.4 %collective-permute-start.2 = (f32[16,128]{1,0:T(8,128)S(1)}, f32[16,128]{1,0:T(8,128)S(1)}, u32[]{:S(2)}, u32[]{:S(2)}) collective-permute-start(f32[16,128]{1,0:T(8,128)S(1)} %get-tuple-element.18.refs_0_), channel_id=1, source_target_pairs={{0,3},{1,0},{2,1},{3,2},{4,7},{5,4},{6,5},{7,6},{8,11},{9,8},{10,9... | collective-permute-start | bytes 24584 | tf_op jit(solution)/shard_map/ppermute | solution.py:192
  6.3 0.0 copy-start
  6.3 4.0 %shard_map.119.pushed_ref = bf16[8,128,128]{2,1,0:T(8,128)(2,1)S(1)} custom-call(f32[3,2048]{1,0:T(4,128)S(1)} %get-tuple-element.15.offsets_ref, f32[3,2048]{1,0:T(4,128)S(1)} %get-tuple-element.17.vel_ref, f32[456,128]{1,0:T(8,128)S(1)} %get-tuple-element.16.shell_ref, bf16[4,456,456]{2,1,0:T(8,128)(2,1)} %m2l_ref.1, s32[4,1,32]{2,1,0:T(1,128)} %bitcast.22, ...), custom_call_target="tpu_custom_call" | custom-call | flops 80000000 | tf_op jit(solution)/shard_map/pallas_call | solution.py:236
  10.3 0.0 copy-start.1
  10.3 0.0 collective-permute-done.refs_1_
  10.3 0.0 collective-permute-done.1.refs_2_
  10.3 0.0 collective-permute-done.2.refs_3_
  10.4 0.7 %shard_map.120 = bf16[8,144,128]{2,1,0:T(8,128)(2,1)} custom-call(bf16[8,128,128]{2,1,0:T(8,128)(2,1)S(1)} %shard_map.119.pushed_ref, f32[16,128]{1,0:T(8,128)S(1)} %get-tuple-element.18.refs_0_, f32[16,128]{1,0:T(8,128)S(1)} %collective-permute-done.refs_1_, f32[16,128]{1,0:T(8,128)S(1)} %collective-permute-done.1.refs_2_, ...), custom_call_target="tpu_custom_call" | custom-call | flops 1000000 | bytes 1048576 | tf_op jit(solution)/shard_map/pallas_call | solution.py:262
  11.1 5.8 %all-to-all-start = ((bf16[8,144,128]{2,1,0:T(8,128)(2,1)}), bf16[8,144,128]{2,1,0:T(8,128)(2,1)S(1)}, u32[]{:S(2)}, u32[]{:S(2)}) async-start(bf16[8,144,128]{2,1,0:T(8,128)(2,1)} %shard_map.120), calls=%async_computation | async-start | bytes 589824 | tf_op jit(solution)/shard_map/all_to_all | solution.py:265
  16.9 0.0 copy-done.3
  16.9 0.0 copy-done.4
  16.9 0.0 copy-done.5
  16.9 0.0 copy-done.6
  16.9 6.7 %shard_map.121 = (f32[4,16,128]{2,1,0:T(8,128)S(1)}, bf16[4,32,128]{2,1,0:T(8,128)(2,1)S(1)}) custom-call(s32[4,32]{1,0:T(4,128)S(1)} %bitcast.18, s32[4,32]{1,0:T(4,128)S(1)} %bitcast.19, f32[3,2048]{1,0:T(4,128)S(1)} %get-tuple-element.15.offsets_ref, f32[3,2048]{1,0:T(4,128)S(1)} %get-tuple-element.17.vel_ref, s32[4,1,32]{2,1,0:T(1,128)S(1)} %bitcast.20, ...), custom_call_target="tpu_custom_call" | custom-call | flops 100000000 | bytes 1048576 | tf_op jit(solution)/shard_map/pallas_call | solution.py:341
  23.6 2.2 %all-to-all-done.got_ref = bf16[8,144,128]{2,1,0:T(8,128)(2,1)S(1)} async-done(((bf16[8,144,128]{2,1,0:T(8,128)(2,1)}), bf16[8,144,128]{2,1,0:T(8,128)(2,1)S(1)}, u32[]{:S(2)}, u32[]{:S(2)}) %all-to-all-start) | async-done | bytes 294944 | tf_op jit(solution)/shard_map/all_to_all | solution.py:265
  25.9 0.0 copy-start.2
  25.9 0.0 copy-done
  25.9 0.5 %shard_map.122 = (f32[64,128]{1,0:T(8,128)S(1)}, bf16[64,128]{1,0:T(8,128)(2,1)S(1)}, bf16[64,128]{1,0:T(8,128)(2,1)S(1)}, bf16[64,128]{1,0:T(8,128)(2,1)S(1)}) custom-call(bf16[8,144,128]{2,1,0:T(8,128)(2,1)S(1)} %all-to-all-done.got_ref, bf16[4,32,128]{2,1,0:T(8,128)(2,1)S(1)} %get-tuple-element.19.sel_ref, bf16[4,456,456]{2,1,0:T(8,128)(2,1)S(1)} %copy-done, ...), custom_call_target="tpu_custom_call" | custom-call | flops 20000000 | bytes 1048576 | tf_op jit(solution)/shard_map/pallas_call | solution.py:381
  26.4 0.0 collective-permute-start.3
  26.4 1.3 %collective-permute-start.4 = (bf16[64,128]{1,0:T(8,128)(2,1)S(1)}, bf16[64,128]{1,0:T(8,128)(2,1)S(1)}, u32[]{:S(2)}, u32[]{:S(2)}) collective-permute-start(bf16[64,128]{1,0:T(8,128)(2,1)S(1)} %get-tuple-element.23), channel_id=1, source_target_pairs={{0,2},{1,3},{2,0},{3,1},{4,6},{5,7},{6,4},{7,5},{8,10},{9,11},{10,... | collective-permute-start | bytes 49160 | tf_op jit(solution)/shard_map/ppermute | solution.py:192
  27.6 1.4 %collective-permute-start.5 = (bf16[64,128]{1,0:T(8,128)(2,1)S(1)}, bf16[64,128]{1,0:T(8,128)(2,1)S(1)}, u32[]{:S(2)}, u32[]{:S(2)}) collective-permute-start(bf16[64,128]{1,0:T(8,128)(2,1)S(1)} %get-tuple-element.24), channel_id=1, source_target_pairs={{0,3},{1,0},{2,1},{3,2},{4,7},{5,4},{6,5},{7,6},{8,11},{9,8},{10,9... | collective-permute-start | bytes 49160 | tf_op jit(solution)/shard_map/ppermute | solution.py:192
  29.0 0.5 %collective-permute-done.3.refs_1_ = bf16[64,128]{1,0:T(8,128)(2,1)S(1)} collective-permute-done((bf16[64,128]{1,0:T(8,128)(2,1)S(1)}, bf16[64,128]{1,0:T(8,128)(2,1)S(1)}, u32[]{:S(2)}, u32[]{:S(2)}) %collective-permute-start.3) | collective-permute-done | bytes 16416 | tf_op jit(solution)/shard_map/ppermute | solution.py:192
  29.5 0.6 %collective-permute-done.4.refs_2_ = bf16[64,128]{1,0:T(8,128)(2,1)S(1)} collective-permute-done((bf16[64,128]{1,0:T(8,128)(2,1)S(1)}, bf16[64,128]{1,0:T(8,128)(2,1)S(1)}, u32[]{:S(2)}, u32[]{:S(2)}) %collective-permute-start.4) | collective-permute-done | bytes 16416 | tf_op jit(solution)/shard_map/ppermute | solution.py:192
  30.2 0.3 collective-permute-done.5.refs_3_
  30.5 0.0 copy-done.1
  30.5 0.0 copy-done.2
  30.5 1.1 %shard_map.123.refs_0_ = f32[16,128]{1,0:T(8,128)S(1)} custom-call(bf16[2,456,456]{2,1,0:T(8,128)(2,1)S(1)} %copy-done.1, f32[456,456]{1,0:T(8,128)S(1)} %copy-done.2, f32[3,2048]{1,0:T(4,128)S(1)} %get-tuple-element.15.offsets_ref, f32[456,128]{1,0:T(8,128)S(1)} %get-tuple-element.16.shell_ref, f32[64,128]{1,0:T(8,128)S(1)} %get-tuple-element.21.refs_0_, ...), custom_call_target="tpu_custom_call" | custom-call | flops 20000000 | bytes 1048576 | tf_op jit(solution)/shard_map/pallas_call | solution.py:435
  31.5 1.0 %collective-permute-start.6 = (f32[16,128]{1,0:T(8,128)S(1)}, f32[16,128]{1,0:T(8,128)S(1)}, u32[]{:S(2)}, u32[]{:S(2)}) collective-permute-start(f32[16,128]{1,0:T(8,128)S(1)} %shard_map.123.refs_0_), channel_id=1, source_target_pairs={{0,1},{1,2},{2,3},{3,0},{4,5},{5,6},{6,7},{7,4},{8,9},{9,10},{10,1... | collective-permute-start | bytes 24584 | tf_op jit(solution)/shard_map/ppermute | solution.py:192
  32.5 1.2 %collective-permute-start.7 = (f32[16,128]{1,0:T(8,128)S(1)}, f32[16,128]{1,0:T(8,128)S(1)}, u32[]{:S(2)}, u32[]{:S(2)}) collective-permute-start(f32[16,128]{1,0:T(8,128)S(1)} %shard_map.123.refs_0_), channel_id=1, source_target_pairs={{0,2},{1,3},{2,0},{3,1},{4,6},{5,7},{6,4},{7,5},{8,10},{9,11},{10,... | collective-permute-start | bytes 24584 | tf_op jit(solution)/shard_map/ppermute | solution.py:192
  33.7 0.4 collective-permute-start.8
  34.1 0.6 %collective-permute-done.6.refs_1_ = f32[16,128]{1,0:T(8,128)S(1)} collective-permute-done((f32[16,128]{1,0:T(8,128)S(1)}, f32[16,128]{1,0:T(8,128)S(1)}, u32[]{:S(2)}, u32[]{:S(2)}) %collective-permute-start.6) | collective-permute-done | bytes 8224 | tf_op jit(solution)/shard_map/ppermute | solution.py:192
  34.7 1.5 %collective-permute-done.7.refs_2_ = f32[16,128]{1,0:T(8,128)S(1)} collective-permute-done((f32[16,128]{1,0:T(8,128)S(1)}, f32[16,128]{1,0:T(8,128)S(1)}, u32[]{:S(2)}, u32[]{:S(2)}) %collective-permute-start.7) | collective-permute-done | bytes 8224 | tf_op jit(solution)/shard_map/ppermute | solution.py:192
  36.2 0.0 collective-permute-done.8.refs_3_
  36.2 0.6 %shard_map.124 = f32[3,2048]{1,0:T(4,128)} custom-call(f32[16,128]{1,0:T(8,128)S(1)} %shard_map.123.refs_0_, f32[16,128]{1,0:T(8,128)S(1)} %collective-permute-done.6.refs_1_, f32[16,128]{1,0:T(8,128)S(1)} %collective-permute-done.7.refs_2_, f32[16,128]{1,0:T(8,128)S(1)} %collective-permute-done.8.refs_3_), custom_call_target="tpu_custom_call" | custom-call | flops 100000 | bytes 1048576 | tf_op jit(solution)/shard_map/pallas_call | solution.py:452
Async XLA Ops:
  1.7 15.2 %copy-start.3 = (s32[32,4]{0,1:T(4,128)S(1)}, s32[32,4]{0,1:T(4,128)}, u32[]{:S(2)}) copy-start(s32[32,4]{0,1:T(4,128)} %param.21) | copy-start | bytes 1540
  1.7 15.2 %copy-start.4 = (s32[32,4]{0,1:T(4,128)S(1)}, s32[32,4]{0,1:T(4,128)}, u32[]{:S(2)}) copy-start(s32[32,4]{0,1:T(4,128)} %param.22) | copy-start | bytes 1540
  1.7 15.2 %copy-start.5 = (s32[1,32,4,1]{1,3,2,0:T(1,128)S(1)}, s32[1,32,4,1]{1,3,2,0:T(1,128)}, u32[]{:S(2)}) copy-start(s32[1,32,4,1]{1,3,2,0:T(1,128)} %param.19) | copy-start | bytes 1540
  1.8 15.2 %copy-start.6 = (s32[1,32,4]{1,2,0:T(4,128)S(1)}, s32[1,32,4]{1,2,0:T(4,128)}, u32[]{:S(2)}) copy-start(s32[1,32,4]{1,2,0:T(4,128)} %param.20) | copy-start | bytes 1540
  1.8 8.6 %collective-permute-start = (f32[16,128]{1,0:T(8,128)S(1)}, f32[16,128]{1,0:T(8,128)S(1)}, u32[]{:S(2)}, u32[]{:S(2)}) collective-permute-start(f32[16,128]{1,0:T(8,128)S(1)} %get-tuple-element.18.refs_0_), channel_id=1, source_target_pairs={{0,1},{1,2},{2,3},{3,0},{4,5},{5,6},{6,7},{7,4},{8,9},{9,10},{10,1... | collective-permute-start | bytes 24584 | tf_op jit(solution)/shard_map/ppermute | solution.py:192
  2.3 8.0 %collective-permute-start.1 = (f32[16,128]{1,0:T(8,128)S(1)}, f32[16,128]{1,0:T(8,128)S(1)}, u32[]{:S(2)}, u32[]{:S(2)}) collective-permute-start(f32[16,128]{1,0:T(8,128)S(1)} %get-tuple-element.18.refs_0_), channel_id=1, source_target_pairs={{0,2},{1,3},{2,0},{3,1},{4,6},{5,7},{6,4},{7,5},{8,10},{9,11},{10,... | collective-permute-start | bytes 24584 | tf_op jit(solution)/shard_map/ppermute | solution.py:192
  4.9 5.5 %collective-permute-start.2 = (f32[16,128]{1,0:T(8,128)S(1)}, f32[16,128]{1,0:T(8,128)S(1)}, u32[]{:S(2)}, u32[]{:S(2)}) collective-permute-start(f32[16,128]{1,0:T(8,128)S(1)} %get-tuple-element.18.refs_0_), channel_id=1, source_target_pairs={{0,3},{1,0},{2,1},{3,2},{4,7},{5,4},{6,5},{7,6},{8,11},{9,8},{10,9... | collective-permute-start | bytes 24584 | tf_op jit(solution)/shard_map/ppermute | solution.py:192
  6.3 19.6 %copy-start = (bf16[4,456,456]{2,1,0:T(8,128)(2,1)S(1)}, bf16[4,456,456]{2,1,0:T(8,128)(2,1)}, u32[]{:S(2)}) copy-start(bf16[4,456,456]{2,1,0:T(8,128)(2,1)} %m2l_ref.1) | copy-start | bytes 4990468
  10.3 20.1 %copy-start.1 = (bf16[2,456,456]{2,1,0:T(8,128)(2,1)S(1)}, bf16[2,456,456]{2,1,0:T(8,128)(2,1)}, u32[]{:S(2)}) copy-start(bf16[2,456,456]{2,1,0:T(8,128)(2,1)} %child_ref.1) | copy-start | bytes 2495236
  11.1 14.8 %all-to-all-start = ((bf16[8,144,128]{2,1,0:T(8,128)(2,1)}), bf16[8,144,128]{2,1,0:T(8,128)(2,1)S(1)}, u32[]{:S(2)}, u32[]{:S(2)}) async-start(bf16[8,144,128]{2,1,0:T(8,128)(2,1)} %shard_map.120), calls=%async_computation | async-start | bytes 589824 | tf_op jit(solution)/shard_map/all_to_all | solution.py:265
  25.9 4.6 %copy-start.2 = (f32[456,456]{1,0:T(8,128)S(1)}, f32[456,456]{1,0:T(8,128)}, u32[]{:S(2)}) copy-start(f32[456,456]{1,0:T(8,128)} %map_ref.1) | copy-start | bytes 2495236
  26.4 3.2 %collective-permute-start.3 = (bf16[64,128]{1,0:T(8,128)(2,1)S(1)}, bf16[64,128]{1,0:T(8,128)(2,1)S(1)}, u32[]{:S(2)}, u32[]{:S(2)}) collective-permute-start(bf16[64,128]{1,0:T(8,128)(2,1)S(1)} %get-tuple-element.22), channel_id=1, source_target_pairs={{0,1},{1,2},{2,3},{3,0},{4,5},{5,6},{6,7},{7,4},{8,9},{9,10},{10,1... | collective-permute-start | bytes 49160 | tf_op jit(solution)/shard_map/ppermute | solution.py:192
  26.4 3.8 %collective-permute-start.4 = (bf16[64,128]{1,0:T(8,128)(2,1)S(1)}, bf16[64,128]{1,0:T(8,128)(2,1)S(1)}, u32[]{:S(2)}, u32[]{:S(2)}) collective-permute-start(bf16[64,128]{1,0:T(8,128)(2,1)S(1)} %get-tuple-element.23), channel_id=1, source_target_pairs={{0,2},{1,3},{2,0},{3,1},{4,6},{5,7},{6,4},{7,5},{8,10},{9,11},{10,... | collective-permute-start | bytes 49160 | tf_op jit(solution)/shard_map/ppermute | solution.py:192
  27.6 2.8 %collective-permute-start.5 = (bf16[64,128]{1,0:T(8,128)(2,1)S(1)}, bf16[64,128]{1,0:T(8,128)(2,1)S(1)}, u32[]{:S(2)}, u32[]{:S(2)}) collective-permute-start(bf16[64,128]{1,0:T(8,128)(2,1)S(1)} %get-tuple-element.24), channel_id=1, source_target_pairs={{0,3},{1,0},{2,1},{3,2},{4,7},{5,4},{6,5},{7,6},{8,11},{9,8},{10,9... | collective-permute-start | bytes 49160 | tf_op jit(solution)/shard_map/ppermute | solution.py:192
  31.5 3.1 %collective-permute-start.6 = (f32[16,128]{1,0:T(8,128)S(1)}, f32[16,128]{1,0:T(8,128)S(1)}, u32[]{:S(2)}, u32[]{:S(2)}) collective-permute-start(f32[16,128]{1,0:T(8,128)S(1)} %shard_map.123.refs_0_), channel_id=1, source_target_pairs={{0,1},{1,2},{2,3},{3,0},{4,5},{5,6},{6,7},{7,4},{8,9},{9,10},{10,1... | collective-permute-start | bytes 24584 | tf_op jit(solution)/shard_map/ppermute | solution.py:192
  32.5 3.7 %collective-permute-start.7 = (f32[16,128]{1,0:T(8,128)S(1)}, f32[16,128]{1,0:T(8,128)S(1)}, u32[]{:S(2)}, u32[]{:S(2)}) collective-permute-start(f32[16,128]{1,0:T(8,128)S(1)} %shard_map.123.refs_0_), channel_id=1, source_target_pairs={{0,2},{1,3},{2,0},{3,1},{4,6},{5,7},{6,4},{7,5},{8,10},{9,11},{10,... | collective-permute-start | bytes 24584 | tf_op jit(solution)/shard_map/ppermute | solution.py:192
  33.7 2.5 %collective-permute-start.8 = (f32[16,128]{1,0:T(8,128)S(1)}, f32[16,128]{1,0:T(8,128)S(1)}, u32[]{:S(2)}, u32[]{:S(2)}) collective-permute-start(f32[16,128]{1,0:T(8,128)S(1)} %shard_map.123.refs_0_), channel_id=1, source_target_pairs={{0,3},{1,0},{2,1},{3,2},{4,7},{5,4},{6,5},{7,6},{8,11},{9,8},{10,9... | collective-permute-start | bytes 24584 | tf_op jit(solution)/shard_map/ppermute | solution.py:192

commit v3 on v2

--- a/solution.py
+++ b/solution.py
@@ -14,7 +14,6 @@
 BF16 = jnp.bfloat16
 VMEM = pl.BlockSpec(memory_space=pltpu.VMEM)
 HBM = pl.BlockSpec(memory_space=pltpu.HBM)
-SMEM = pl.BlockSpec(memory_space=pltpu.SMEM)
 NN = (((1,), (0,)), ((), ()))
 NT = (((1,), (1,)), ((), ()))
 TN = (((0,), (0,)), ((), ()))
@@ -58,6 +57,20 @@
 
 def in_hbm(*arrays):
     return [pltpu.with_memory_space_constraint(array, pltpu.HBM) for array in arrays]
+
+
+def start_all(sources, targets, sems):
+    copies = [
+        pltpu.make_async_copy(source, target, sems.at[i])
+        for i, (source, target) in enumerate(zip(sources, targets))
+    ]
+    for copy in copies:
+        copy.start()
+    return copies
+
+
+def held(*arrays):
+    return [pltpu.VMEM(array.shape, array.dtype) for array in arrays]
 
 
 def shape(dims, dtype):
@@ -125,27 +138,37 @@
     def lanes_of(parent, lvl):
         return pl.ds(pl.multiple_of((parent * lvls + lvl) * LANES, LANES), LANES)
 
+    def box_row(octant, box):
+        return lax.rem(octant, octants) * parents + lax.div(box, 8)
+
     def rows3(ref, lanes):
         return [ref[c : c + 1, lanes] for c in range(3)]
 
     def up_body(
-        offsets_hbm, vel_hbm, child_hbm, shell_hbm, up_ref, offsets_ref, vel_ref, shell_ref, child_ref, fields, sems
+        offsets_hbm,
+        vel_hbm,
+        shell_hbm,
+        owner_hbm,
+        place_hbm,
+        child_hbm,
+        sent_ref,
+        offsets_ref,
+        vel_ref,
+        shell_ref,
+        owner_ref,
+        place_ref,
+        child_ref,
+        fields,
+        slot_ref,
+        sems,
     ):
         me = lax.axis_index("lvl")
-        copies = [
-            pltpu.make_async_copy(source, target, sems.at[i])
-            for i, (source, target) in enumerate(
-                (
-                    (offsets_hbm, offsets_ref),
-                    (vel_hbm, vel_ref),
-                    (shell_hbm, shell_ref),
-                    (child_hbm, child_ref),
-                )
-            )
-        ]
-        for copy in copies:
-            copy.start()
-        for copy in copies[:3]:
+        copies = start_all(
+            (offsets_hbm, vel_hbm, shell_hbm, owner_hbm, place_hbm, child_hbm),
+            (offsets_ref, vel_ref, shell_ref, owner_ref, place_ref, child_ref),
+            sems,
+        )
+        for copy in copies[:5]:
             copy.wait()
         for p in range(parents):
             lanes = lanes_of(p, me)
@@ -156,117 +179,66 @@
                 fields,
                 slice(p * LANES, (p + 1) * LANES),
             )
+        place = jnp.concatenate([place_ref[...], place_ref[...]], 0)
+        octant = lax.rem(place, 8)
+        spot = lax.div(octant, octants) * own + box_row(octant, place)
+        owner = jnp.concatenate(
+            [owner_ref[c] for c in range(classes)] + [jnp.zeros((classes, boxes), jnp.int32)], 0
+        )
+        ids = jnp.where(iota((2 * classes, boxes), 0) < classes, owner, spot)
+        box = iota((boxes, LANES), 0)
+        octant = lax.rem(box, 8)
+        spot = lax.div(octant, octants) * own + box_row(octant, box)
+        moved = iota((boxes, LANES), 1) == LANES - boxes + spot
+        ids = dot(ids.astype(F32).astype(BF16), moved.astype(F32).astype(BF16))
+
         here = parents * LANES
-        lane = iota((8 * octants, here), 1)
-        row = iota((8 * octants, here), 0)
-        target = (lane % LANES) // per_box * 8 + lane // LANES
+        lane = iota((own + 8 * octants, here), 1)
+        row = iota((own + 8 * octants, here), 0)
+        second, p = (lane % LANES) // per_box, lane // LANES
+        target = jnp.where(row < own, second * parents + p, own + second * 8 + p)
         pick = (row == target).astype(F32).astype(BF16)
-        leaf = dot(pick, fields[...].astype(BF16), NT).astype(BF16)
-        copies[3].wait()
-        total = dot(leaf[0:8], child_ref[0])
-        for o in range(1, octants):
-            total = total + dot(leaf[8 * o : 8 * o + 8], child_ref[o])
+        leaf = dot(pick, fields[...].astype(BF16), NT)
+        for k, block in enumerate(blocks128(leaf[0:own])):
+            slot_ref[k * own : (k + 1) * own, :] = block + (ids if k == pieces - 1 else 0.0)
+        leaf = leaf.astype(BF16)
+        copies[5].wait()
+        total = None
+        for o in range(octants):
+            part = dot(leaf[own + 8 * o : own + 8 * o + 8], child_ref[o])
+            total = part if total is None else total + part
         for k, block in enumerate(blocks128(total)):
-            up_ref[k * parents : (k + 1) * parents, :] = block[0:parents]
-
-    up, offsets, vel_cot, shell = call(
+            first = own_rows + k * parents
+            slot_ref[first : first + parents, :] = block[0:parents]
+        sent_ref[...] = jnp.broadcast_to(slot_ref[...].astype(BF16)[None], sent_ref.shape)
+
+    slot_rows = own_rows + up_rows
+    devices = leaves * lvls
+    up_inputs = (offsets, vel_cot, shell, leaf_owner, leaf_place, child_ops)
+    sent = call(
         up_body,
-        (
-            shape((up_rows, LANES), F32),
-            shape(offsets.shape, F32),
-            shape(vel_cot.shape, F32),
-            shape(shell.shape, F32),
-        ),
+        shape((devices, slot_rows, LANES), BF16),
         20_000_000,
-        [
-            pltpu.VMEM(child_ops.shape, BF16),
+        held(*up_inputs)
+        + [
             pltpu.VMEM((3 * count, parents * LANES), F32),
-            pltpu.SemaphoreType.DMA((4,)),
+            pltpu.VMEM((slot_rows, LANES), F32),
+            pltpu.SemaphoreType.DMA((6,)),
         ],
-        [HBM] * 4,
+        [HBM] * 6,
         40,
-        0,
-    )(*in_hbm(offsets, vel_cot, child_ops, shell))
+    )(*in_hbm(*up_inputs))
+    got = lax.all_to_all(sent, ("leaf", "lvl"), split_axis=0, concat_axis=0, tiled=True)
 
     def shifted(value, k):
         return lax.ppermute(value, "lvl", [(i, (i + k) % lvls) for i in range(lvls)])
 
-    ups = [up] + [shifted(up, k) for k in range(1, lvls)]
-
-    def push_body(
-        offsets_ref, vel_ref, shell_ref, m2l_hbm, owner_hbm, place_hbm, out_ref, m2l_ref, owner_ref, place_ref, fields, sems
-    ):
-        copies = [
-            pltpu.make_async_copy(source, target, sems.at[i])
-            for i, (source, target) in enumerate(
-                ((m2l_hbm, m2l_ref), (owner_hbm, owner_ref), (place_hbm, place_ref))
-            )
-        ]
-        for copy in copies:
-            copy.start()
-        leaf = jnp.zeros((boxes, 3 * count), F32)
-        for j in range(groups):
-            lanes = slice(j * LANES, (j + 1) * LANES)
-            surface_block(
-                rows3(offsets_ref, lanes), rows3(vel_ref, lanes), shell_ref, fields.at[j % 2], slice(None)
-            )
-            box = iota((boxes, LANES), 1) // per_box + j * LANES // per_box
-            pick = (iota((boxes, LANES), 0) == box).astype(F32).astype(BF16)
-            leaf = leaf + dot(pick, fields[j % 2].astype(BF16), NT)
-        leaf = leaf.astype(BF16)
-        for copy in copies:
+    def near_body(*refs):
+        sources, (near_ref, sel_ref), targets = refs[:6], refs[6:8], refs[8:14]
+        columns, table, sums, sems = refs[14:]
+        q_ref, dir_ref, offsets_ref, vel_ref, owner_ref, place_ref = targets
+        for copy in start_all(sources, targets, sems):
             copy.wait()
-        total = None
-        for c in range(classes):
-            term = dot(leaf, m2l_ref[c]).astype(BF16)
-            place = place_ref[c : c + 1, :]
-            octant = lax.rem(place, 8)
-            slot = (
-                lax.div(octant, octants) * own
-                + lax.rem(octant, octants) * parents
-                + lax.div(place, 8)
-            )
-            code = owner_ref[c] * boxes + slot
-            hit = (iota((leaves * boxes, boxes), 0) == code).astype(F32).astype(BF16)
-            part = dot(hit, term)
-            total = part if total is None else total + part
-        for k, block_k in enumerate(blocks128(total.astype(BF16))):
-            out_ref[:, k * boxes : (k + 1) * boxes, :] = block_k.reshape(leaves, boxes, LANES)
-
-    pushed = call(
-        push_body,
-        shape((leaves, leaf_rows, LANES), BF16),
-        80_000_000,
-        [
-            pltpu.VMEM(m2l_ops.shape, BF16),
-            pltpu.VMEM(leaf_owner.shape, jnp.int32),
-            pltpu.VMEM(leaf_place.shape, jnp.int32),
-            pltpu.VMEM((2, 3 * count, LANES), F32),
-            pltpu.SemaphoreType.DMA((3,)),
-        ],
-        [VMEM] * 3 + [HBM] * 3,
-        40,
-        0,
-    )(offsets, vel_cot, shell, *in_hbm(m2l_ops, leaf_owner, leaf_place))
-
-    def pack_body(pushed_ref, *refs):
-        *up_refs, out_ref = refs
-        total = up_refs[0][...]
-        for ref in up_refs[1:]:
-            total = total + ref[...]
-        out_ref[:, :leaf_rows, :] = pushed_ref[...]
-        out_ref[:, leaf_rows:, :] = jnp.broadcast_to(
-            total.astype(BF16)[None], (leaves, up_rows, LANES)
-        )
-
-    sent = call(
-        pack_body, shape((leaves, leaf_rows + up_rows, LANES), BF16), 1_000_000, (), [VMEM] * (1 + lvls)
-    )(pushed, *ups)
-    got = lax.all_to_all(sent, "leaf", split_axis=0, concat_axis=0, tiled=True)
-
-    def near_body(
-        q_ref, dir_ref, offsets_ref, vel_ref, owner_ref, place_ref, near_ref, sel_ref, columns, table, sums
-    ):
         mine = lax.axis_index("leaf") * parents
         coarse = leaves * parents
         pick = jnp.concatenate(
@@ -345,27 +317,64 @@
             shape((pieces, 8 * classes, leaves * up_rows), BF16),
         ),
         100_000_000,
-        [
+        [pltpu.SMEM(near_q.shape, jnp.int32), pltpu.SMEM(near_d.shape, jnp.int32)]
+        + held(offsets, vel_cot, coarse_owner, coarse_place)
+        + [
             pltpu.VMEM((tall, 8), F32),
             pltpu.VMEM((boxes, 8, LANES), F32),
             pltpu.VMEM((3, LANES, LANES), F32),
+            pltpu.SemaphoreType.DMA((6,)),
         ],
-        [SMEM, SMEM] + [VMEM] * 4,
+        [HBM] * 6,
         24,
-    )(near_q, near_d, offsets, vel_cot, coarse_owner, coarse_place)
+    )(*in_hbm(near_q, near_d, offsets, vel_cot, coarse_owner, coarse_place))
 
     def mid_body(got_ref, sel_ref, m2l_ref, near_ref, *refs):
         *out_refs, leaf_sum = refs
         me = lax.axis_index("lvl")
-        leaf_sum[...] = jnp.sum(got_ref[:, :leaf_rows, :].astype(F32), 0)
-        tops = got_ref[:, leaf_rows:, :].reshape(leaves * up_rows, LANES)
+        mine = lax.axis_index("leaf").astype(F32)
+        tops = got_ref[:, own_rows:, :].astype(F32).reshape(leaves, lvls, up_rows, LANES)
+        tops = jnp.sum(tops, 1).astype(BF16).reshape(leaves * up_rows, LANES)
         chosen = jnp.concatenate([dot(sel_ref[k], tops) for k in range(pieces)], 1)
         high = chosen.astype(BF16).astype(F32)
         parts = jnp.where(iota(chosen.shape, 0) % 8 < parents, high, chosen - high)
-        parts = parts[:, :width].astype(BF16)
-        total = dot(parts[0:8], m2l_ref[0])
-        for c in range(1, classes):
-            total = total + dot(parts[8 * c : 8 * c + 8], m2l_ref[c])
+
+        per_tile = LANES // boxes
+        lane = iota((2 * classes, LANES), 1)
+        ids = []
+        for first in range(0, leaves, per_tile):
+            tile = jnp.zeros((2 * classes, LANES), F32)
+            for i in range(min(per_tile, leaves - first)):
+                piece = got_ref[(first + i) * lvls + me, own_rows - own : own_rows, :].astype(F32)
+                piece = pltpu.roll(piece, (i + 1) * boxes % LANES, 1)
+                tile = jnp.where(lax.div(lane, boxes) == i, piece, tile)
+            ids.append(tile)
+        ids = jnp.concatenate(ids, 1)[:, : leaves * boxes]
+        row = iota((boxes, leaves * boxes), 0).astype(F32)
+        hits = jnp.concatenate(
+            [
+                ((ids[c : c + 1] == mine) & (ids[classes + c : classes + c + 1] == row)).astype(F32)
+                for c in range(classes)
+            ],
+            0,
+        ).astype(BF16)
+        gathered = jnp.concatenate(
+            [
+                dot(hits, got_ref[:, k * own : (k + 1) * own, :].reshape(devices * own, LANES))
+                for k in range(pieces)
+            ],
+            1,
+        )
+        total = None
+        for c in range(classes):
+            rows = jnp.concatenate(
+                [gathered[c * boxes : (c + 1) * boxes], parts[8 * c : 8 * c + 8]], 0
+            )
+            part = dot(rows[:, :width].astype(BF16), m2l_ref[c])
+            total = part if total is None else total + part
+        for k, block in enumerate(blocks128(total[:boxes])):
+            leaf_sum[k * boxes : (k + 1) * boxes, :] = block
+        total = total[boxes:]
         total = 0.5 * (total[0:parents] + total[parents : 2 * parents])
         total_blocks = blocks128(total)
         for k, out_ref in enumerate(out_refs):
@@ -384,6 +393,7 @@
         20_000_000,
         [pltpu.VMEM((leaf_rows, LANES), F32)],
         [VMEM] * 4,
+        40,
     )(got, select, m2l_ops, near)
     mids = [mids[0]] + [shifted(mids[k], k) for k in range(1, lvls)]
 

time: 37.1 us -> 34.7 us (0.935)
  waiting for transfers between devices: 5.78 us -> 10.4 us
  Pallas kernels: 15.4 us -> 11.3 us
  starting transfers between devices: 15.5 us -> 11.9 us
  local copies, waits for them, and re-layouts: 0.04 us -> 0.76 us
    ppermute x9 -> x6, starting transfers between devices: 9.69 us -> 4.59 us  [shifted(): lax.ppermute(value, 'lvl', [(i, (i + k) % lvls) for i in range(lvls)])]
    pallas_call x3 -> x1, Pallas kernels: 6.47 us -> 1.89 us  [local(): call(up_body, shape((devices, slot_rows, LANES), BF16), 20000000, held(*u...]
    all_to_all x1, waiting for transfers between devices: 2.22 us -> 6.26 us  [local(): lax.all_to_all(sent, ('leaf', 'lvl'), split_axis=0, concat_axis=0, tiled=...]
    all_to_all x1, starting transfers between devices: 5.81 us -> 7.33 us  [local(): lax.all_to_all(sent, ('leaf', 'lvl'), split_axis=0, concat_axis=0, tiled=...]
    unnamed x14 -> x12, local copies, waits for them, and re-layouts: 0.04 us -> 0.76 us
    ppermute x9 -> x6, waiting for transfers between devices: 3.56 us -> 4.17 us  [shifted(): lax.ppermute(value, 'lvl', [(i, (i + k) % lvls) for i in range(lvls)])]
  transfers between devices with their start and end apart: 10 -> 7, of which waited for: 6 -> 5; matrix products, arithmetic and copies ran while one was open for 0% -> 0% of each run, Pallas kernels for 29% -> 20%
where the time goes in v3:
time: 34.7 us; the launch traced here: 34.4 us
  starting transfers between devices  11.9 us (34%)
  Pallas kernels  11.3 us (33%)
  waiting for transfers between devices  10.4 us (30%)
  local copies, waits for them, and re-layouts  0.76 us (2%)
    all_to_all x1, starting transfers between devices, local(): lax.all_to_all(sent, ('leaf', 'lvl'), split_axis=0, concat_axis=0, tiled=...  7.33 us
    pallas_call x1, Pallas kernels, local(): call(near_body, (shape((lvls, parents * 4, LANES), F32), shape((pieces, 8...  6.98 us
    all_to_all x1, waiting for transfers between devices, local(): lax.all_to_all(sent, ('leaf', 'lvl'), split_axis=0, concat_axis=0, tiled=...  6.26 us
    ppermute x6, starting transfers between devices, shifted(): lax.ppermute(value, 'lvl', [(i, (i + k) % lvls) for i in range(lvls)])  4.59 us
    ppermute x6, waiting for transfers between devices, shifted(): lax.ppermute(value, 'lvl', [(i, (i + k) % lvls) for i in range(lvls)])  4.17 us
    pallas_call x1, Pallas kernels, local(): call(up_body, shape((devices, slot_rows, LANES), BF16), 20000000, held(*u...  1.89 us
    pallas_call x1, Pallas kernels, local(): call(down_body, shape((parents * 4, LANES), F32), 20000000, [pltpu.VMEM((...  1.09 us
    unnamed x12, local copies, waits for them, and re-layouts  0.76 us
  transfers between devices with their start and end apart: 7, of which 5 were waited for; matrix products, arithmetic and copies ran while one was open for 0% of the time, Pallas kernels for 20%

profile of v3, /device:TPU:0, one launch (start us, length us, event | category | flops | bytes accessed | tf_op | source)
XLA Modules:
  0.0 34.4 jit_solution(4512858167785765867)
XLA Ops:
  0.0 0.0 copy-start.1
  0.0 1.9 %shard_map.118 = bf16[32,48,128]{2,1,0:T(8,128)(2,1)S(1)} custom-call(f32[3,2048]{1,0:T(4,128)} %offsets_ref.1, f32[3,2048]{1,0:T(4,128)} %refs_3_.1, f32[456,128]{1,0:T(8,128)} %constant.2.clone.shell_hbm.shell_ref, s32[4,1,32]{2,1,0:T(1,128)} %bitcast.18, s32[4,32]{1,0:T(4,128)} %bitcast.19, bf16[2,456,456]{2,1,0:T(8,128)(2,1)} %child_ref.1), custom_call_target="tpu_custom_call" | custom-call | flops 20000000 | bytes 1048576 | tf_op jit(solution)/shard_map/pallas_call | solution.py:218
  1.9 0.0 copy-start.2
  1.9 0.7 %copy-done.2 = bf16[32,48,128]{2,1,0:T(8,128)(2,1)} copy-done((bf16[32,48,128]{2,1,0:T(8,128)(2,1)}, bf16[32,48,128]{2,1,0:T(8,128)(2,1)S(1)}, u32[]{:S(2)}) %copy-start.2) | copy-done | bytes 393240
  2.6 0.0 copy-start
  2.7 0.0 copy-start.3
  2.7 0.0 copy-start.5
  2.7 7.3 %all-to-all-start = ((bf16[32,48,128]{2,1,0:T(8,128)(2,1)}), bf16[32,48,128]{2,1,0:T(8,128)(2,1)S(1)}, u32[]{:S(2)}, u32[]{:S(2)}) async-start(bf16[32,48,128]{2,1,0:T(8,128)(2,1)} %copy-done.2), calls=%async_computation | async-start | bytes 786432 | tf_op jit(solution)/shard_map/all_to_all | solution.py:231
  10.0 7.0 %shard_map.119 = (f32[4,16,128]{2,1,0:T(8,128)S(1)}, bf16[4,32,128]{2,1,0:T(8,128)(2,1)S(1)}) custom-call(s32[4,32]{1,0:T(4,128)} %bitcast.20, s32[4,32]{1,0:T(4,128)} %bitcast.21, f32[3,2048]{1,0:T(4,128)} %offsets_ref.1, f32[3,2048]{1,0:T(4,128)} %refs_3_.1, s32[4,1,32]{2,1,0:T(1,128)} %bitcast.22, s32[4,32]{1,0:T(4,128)} %bitcast.23), custom_call_target="tpu_custom_call" | custom-call | flops 100000000 | bytes 1048576 | tf_op jit(solution)/shard_map/pallas_call | solution.py:313
  17.0 6.3 %all-to-all-done.got_ref = bf16[32,48,128]{2,1,0:T(8,128)(2,1)S(1)} async-done(((bf16[32,48,128]{2,1,0:T(8,128)(2,1)}), bf16[32,48,128]{2,1,0:T(8,128)(2,1)S(1)}, u32[]{:S(2)}, u32[]{:S(2)}) %all-to-all-start) | async-done | bytes 393248 | tf_op jit(solution)/shard_map/all_to_all | solution.py:231
  23.2 0.0 copy-start.4
  23.2 0.0 copy-done.1
  23.2 0.7 %shard_map.120 = (f32[64,128]{1,0:T(8,128)S(1)}, bf16[64,128]{1,0:T(8,128)(2,1)S(1)}, bf16[64,128]{1,0:T(8,128)(2,1)S(1)}, bf16[64,128]{1,0:T(8,128)(2,1)S(1)}) custom-call(bf16[32,48,128]{2,1,0:T(8,128)(2,1)S(1)} %all-to-all-done.got_ref, bf16[4,32,128]{2,1,0:T(8,128)(2,1)S(1)} %get-tuple-element.11.sel_ref, bf16[4,456,456]{2,1,0:T(8,128)(2,1)S(1)} %copy-done.1, ...), custom_call_target="tpu_custom_call" | custom-call | flops 20000000 | bytes 1048576 | tf_op jit(solution)/shard_map/pallas_call | solution.py:390
  23.9 0.1 collective-permute-start
  24.0 0.9 %collective-permute-start.1 = (bf16[64,128]{1,0:T(8,128)(2,1)S(1)}, bf16[64,128]{1,0:T(8,128)(2,1)S(1)}, u32[]{:S(2)}, u32[]{:S(2)}) collective-permute-start(bf16[64,128]{1,0:T(8,128)(2,1)S(1)} %get-tuple-element.15), channel_id=1, source_target_pairs={{0,2},{1,3},{2,0},{3,1},{4,6},{5,7},{6,4},{7,5},{8,10},{9,11},{10,... | collective-permute-start | bytes 49160 | tf_op jit(solution)/shard_map/ppermute | solution.py:234
  24.8 1.0 %collective-permute-start.2 = (bf16[64,128]{1,0:T(8,128)(2,1)S(1)}, bf16[64,128]{1,0:T(8,128)(2,1)S(1)}, u32[]{:S(2)}, u32[]{:S(2)}) collective-permute-start(bf16[64,128]{1,0:T(8,128)(2,1)S(1)} %get-tuple-element.16), channel_id=1, source_target_pairs={{0,3},{1,0},{2,1},{3,2},{4,7},{5,4},{6,5},{7,6},{8,11},{9,8},{10,9... | collective-permute-start | bytes 49160 | tf_op jit(solution)/shard_map/ppermute | solution.py:234
  25.8 1.3 %collective-permute-done.refs_1_ = bf16[64,128]{1,0:T(8,128)(2,1)S(1)} collective-permute-done((bf16[64,128]{1,0:T(8,128)(2,1)S(1)}, bf16[64,128]{1,0:T(8,128)(2,1)S(1)}, u32[]{:S(2)}, u32[]{:S(2)}) %collective-permute-start) | collective-permute-done | bytes 16416 | tf_op jit(solution)/shard_map/ppermute | solution.py:234
  27.1 0.7 %collective-permute-done.1.refs_2_ = bf16[64,128]{1,0:T(8,128)(2,1)S(1)} collective-permute-done((bf16[64,128]{1,0:T(8,128)(2,1)S(1)}, bf16[64,128]{1,0:T(8,128)(2,1)S(1)}, u32[]{:S(2)}, u32[]{:S(2)}) %collective-permute-start.1) | collective-permute-done | bytes 16416 | tf_op jit(solution)/shard_map/ppermute | solution.py:234
  27.8 0.0 collective-permute-done.2.refs_3_
  27.8 0.0 copy-done
  27.8 0.0 copy-done.3
  27.8 0.0 copy-done.5
  27.8 0.0 copy-done.4
  27.8 1.1 %shard_map.121.refs_0_ = f32[16,128]{1,0:T(8,128)S(1)} custom-call(bf16[2,456,456]{2,1,0:T(8,128)(2,1)S(1)} %copy-done, f32[456,456]{1,0:T(8,128)S(1)} %copy-done.4, f32[3,2048]{1,0:T(4,128)S(1)} %copy-done.5, f32[456,128]{1,0:T(8,128)S(1)} %copy-done.3, f32[64,128]{1,0:T(8,128)S(1)} %get-tuple-element.13.refs_0_, ...), custom_call_target="tpu_custom_call" | custom-call | flops 20000000 | bytes 1048576 | tf_op jit(solution)/shard_map/pallas_call | solution.py:445
  28.9 1.2 %collective-permute-start.3 = (f32[16,128]{1,0:T(8,128)S(1)}, f32[16,128]{1,0:T(8,128)S(1)}, u32[]{:S(2)}, u32[]{:S(2)}) collective-permute-start(f32[16,128]{1,0:T(8,128)S(1)} %shard_map.121.refs_0_), channel_id=1, source_target_pairs={{0,1},{1,2},{2,3},{3,0},{4,5},{5,6},{6,7},{7,4},{8,9},{9,10},{10,1... | collective-permute-start | bytes 24584 | tf_op jit(solution)/shard_map/ppermute | solution.py:234
  30.1 0.4 %collective-permute-start.4 = (f32[16,128]{1,0:T(8,128)S(1)}, f32[16,128]{1,0:T(8,128)S(1)}, u32[]{:S(2)}, u32[]{:S(2)}) collective-permute-start(f32[16,128]{1,0:T(8,128)S(1)} %shard_map.121.refs_0_), channel_id=1, source_target_pairs={{0,2},{1,3},{2,0},{3,1},{4,6},{5,7},{6,4},{7,5},{8,10},{9,11},{10,... | collective-permute-start | bytes 24584 | tf_op jit(solution)/shard_map/ppermute | solution.py:234
  30.5 1.0 %collective-permute-start.5 = (f32[16,128]{1,0:T(8,128)S(1)}, f32[16,128]{1,0:T(8,128)S(1)}, u32[]{:S(2)}, u32[]{:S(2)}) collective-permute-start(f32[16,128]{1,0:T(8,128)S(1)} %shard_map.121.refs_0_), channel_id=1, source_target_pairs={{0,3},{1,0},{2,1},{3,2},{4,7},{5,4},{6,5},{7,6},{8,11},{9,8},{10,9... | collective-permute-start | bytes 24584 | tf_op jit(solution)/shard_map/ppermute | solution.py:234
  31.6 0.5 %collective-permute-done.3.refs_1_ = f32[16,128]{1,0:T(8,128)S(1)} collective-permute-done((f32[16,128]{1,0:T(8,128)S(1)}, f32[16,128]{1,0:T(8,128)S(1)}, u32[]{:S(2)}, u32[]{:S(2)}) %collective-permute-start.3) | collective-permute-done | bytes 8224 | tf_op jit(solution)/shard_map/ppermute | solution.py:234
  32.0 1.8 %collective-permute-done.4.refs_2_ = f32[16,128]{1,0:T(8,128)S(1)} collective-permute-done((f32[16,128]{1,0:T(8,128)S(1)}, f32[16,128]{1,0:T(8,128)S(1)}, u32[]{:S(2)}, u32[]{:S(2)}) %collective-permute-start.4) | collective-permute-done | bytes 8224 | tf_op jit(solution)/shard_map/ppermute | solution.py:234
  33.8 0.0 collective-permute-done.5.refs_3_
  33.8 0.6 %shard_map.122 = f32[3,2048]{1,0:T(4,128)} custom-call(f32[16,128]{1,0:T(8,128)S(1)} %shard_map.121.refs_0_, f32[16,128]{1,0:T(8,128)S(1)} %collective-permute-done.3.refs_1_, f32[16,128]{1,0:T(8,128)S(1)} %collective-permute-done.4.refs_2_, f32[16,128]{1,0:T(8,128)S(1)} %collective-permute-done.5.refs_3_), custom_call_target="tpu_custom_call" | custom-call | flops 100000 | bytes 1048576 | tf_op jit(solution)/shard_map/pallas_call | solution.py:462
Async XLA Ops:
  0.0 23.2 %copy-start.1 = (bf16[4,456,456]{2,1,0:T(8,128)(2,1)S(1)}, bf16[4,456,456]{2,1,0:T(8,128)(2,1)}, u32[]{:S(2)}) copy-start(bf16[4,456,456]{2,1,0:T(8,128)(2,1)} %m2l_ref.1) | copy-start | bytes 4990468
  1.9 0.7 %copy-start.2 = (bf16[32,48,128]{2,1,0:T(8,128)(2,1)}, bf16[32,48,128]{2,1,0:T(8,128)(2,1)S(1)}, u32[]{:S(2)}) copy-start(bf16[32,48,128]{2,1,0:T(8,128)(2,1)S(1)} %shard_map.118) | copy-start | bytes 1179652
  2.6 25.1 %copy-start = (bf16[2,456,456]{2,1,0:T(8,128)(2,1)S(1)}, bf16[2,456,456]{2,1,0:T(8,128)(2,1)}, u32[]{:S(2)}) copy-start(bf16[2,456,456]{2,1,0:T(8,128)(2,1)} %child_ref.1) | copy-start | bytes 2495236
  2.7 25.1 %copy-start.3 = (f32[456,128]{1,0:T(8,128)S(1)}, f32[456,128]{1,0:T(8,128)}, u32[]{:S(2)}) copy-start(f32[456,128]{1,0:T(8,128)} %constant.2.clone.shell_hbm.shell_ref) | copy-start | bytes 700420
  2.7 25.1 %copy-start.5 = (f32[3,2048]{1,0:T(4,128)S(1)}, f32[3,2048]{1,0:T(4,128)}, u32[]{:S(2)}) copy-start(f32[3,2048]{1,0:T(4,128)} %offsets_ref.1) | copy-start | bytes 73732
  2.7 20.6 %all-to-all-start = ((bf16[32,48,128]{2,1,0:T(8,128)(2,1)}), bf16[32,48,128]{2,1,0:T(8,128)(2,1)S(1)}, u32[]{:S(2)}, u32[]{:S(2)}) async-start(bf16[32,48,128]{2,1,0:T(8,128)(2,1)} %copy-done.2), calls=%async_computation | async-start | bytes 786432 | tf_op jit(solution)/shard_map/all_to_all | solution.py:231
  23.2 4.6 %copy-start.4 = (f32[456,456]{1,0:T(8,128)S(1)}, f32[456,456]{1,0:T(8,128)}, u32[]{:S(2)}) copy-start(f32[456,456]{1,0:T(8,128)} %map_ref.1) | copy-start | bytes 2495236
  23.9 3.2 %collective-permute-start = (bf16[64,128]{1,0:T(8,128)(2,1)S(1)}, bf16[64,128]{1,0:T(8,128)(2,1)S(1)}, u32[]{:S(2)}, u32[]{:S(2)}) collective-permute-start(bf16[64,128]{1,0:T(8,128)(2,1)S(1)} %get-tuple-element.14), channel_id=1, source_target_pairs={{0,1},{1,2},{2,3},{3,0},{4,5},{5,6},{6,7},{7,4},{8,9},{9,10},{10,1... | collective-permute-start | bytes 49160 | tf_op jit(solution)/shard_map/ppermute | solution.py:234
  24.0 3.8 %collective-permute-start.1 = (bf16[64,128]{1,0:T(8,128)(2,1)S(1)}, bf16[64,128]{1,0:T(8,128)(2,1)S(1)}, u32[]{:S(2)}, u32[]{:S(2)}) collective-permute-start(bf16[64,128]{1,0:T(8,128)(2,1)S(1)} %get-tuple-element.15), channel_id=1, source_target_pairs={{0,2},{1,3},{2,0},{3,1},{4,6},{5,7},{6,4},{7,5},{8,10},{9,11},{10,... | collective-permute-start | bytes 49160 | tf_op jit(solution)/shard_map/ppermute | solution.py:234
  24.8 2.9 %collective-permute-start.2 = (bf16[64,128]{1,0:T(8,128)(2,1)S(1)}, bf16[64,128]{1,0:T(8,128)(2,1)S(1)}, u32[]{:S(2)}, u32[]{:S(2)}) collective-permute-start(bf16[64,128]{1,0:T(8,128)(2,1)S(1)} %get-tuple-element.16), channel_id=1, source_target_pairs={{0,3},{1,0},{2,1},{3,2},{4,7},{5,4},{6,5},{7,6},{8,11},{9,8},{10,9... | collective-permute-start | bytes 49160 | tf_op jit(solution)/shard_map/ppermute | solution.py:234
  28.9 3.1 %collective-permute-start.3 = (f32[16,128]{1,0:T(8,128)S(1)}, f32[16,128]{1,0:T(8,128)S(1)}, u32[]{:S(2)}, u32[]{:S(2)}) collective-permute-start(f32[16,128]{1,0:T(8,128)S(1)} %shard_map.121.refs_0_), channel_id=1, source_target_pairs={{0,1},{1,2},{2,3},{3,0},{4,5},{5,6},{6,7},{7,4},{8,9},{9,10},{10,1... | collective-permute-start | bytes 24584 | tf_op jit(solution)/shard_map/ppermute | solution.py:234
  30.1 3.7 %collective-permute-start.4 = (f32[16,128]{1,0:T(8,128)S(1)}, f32[16,128]{1,0:T(8,128)S(1)}, u32[]{:S(2)}, u32[]{:S(2)}) collective-permute-start(f32[16,128]{1,0:T(8,128)S(1)} %shard_map.121.refs_0_), channel_id=1, source_target_pairs={{0,2},{1,3},{2,0},{3,1},{4,6},{5,7},{6,4},{7,5},{8,10},{9,11},{10,... | collective-permute-start | bytes 24584 | tf_op jit(solution)/shard_map/ppermute | solution.py:234
  30.5 3.2 %collective-permute-start.5 = (f32[16,128]{1,0:T(8,128)S(1)}, f32[16,128]{1,0:T(8,128)S(1)}, u32[]{:S(2)}, u32[]{:S(2)}) collective-permute-start(f32[16,128]{1,0:T(8,128)S(1)} %shard_map.121.refs_0_), channel_id=1, source_target_pairs={{0,3},{1,0},{2,1},{3,2},{4,7},{5,4},{6,5},{7,6},{8,11},{9,8},{10,9... | collective-permute-start | bytes 24584 | tf_op jit(solution)/shard_map/ppermute | solution.py:234

commit v4 on v3

--- a/solution.py
+++ b/solution.py
@@ -43,14 +43,14 @@
     return [scale * v[c] + along * d[c] for c in range(3)]
 
 
-def call(body, outs, cost, scratch=(), ins=None, vmem=24, touched=1 << 20):
+def call(body, outs, cost, scratch=(), ins=None, vmem=24, spec=VMEM):
     return pl.pallas_call(
         body,
         out_shape=outs,
         in_specs=ins,
-        out_specs=jax.tree.map(lambda _: VMEM, outs),
+        out_specs=jax.tree.map(lambda _: spec, outs),
         scratch_shapes=list(scratch),
-        cost_estimate=pl.CostEstimate(flops=cost, bytes_accessed=touched, transcendentals=0),
+        cost_estimate=pl.CostEstimate(flops=cost, bytes_accessed=1 << 20, transcendentals=0),
         compiler_params=pltpu.CompilerParams(vmem_limit_bytes=vmem << 20),
     )
 
@@ -122,6 +122,9 @@
     group = octants * per_box
     groups = parents * lvls
     assert group == LANES and own == 8 and parents == 4 and lvls * octants == 8
+    assert octants == 2 and classes == parents and pieces == 4 and lvls % 2 == 0
+    ids_lanes = boxes // 2
+    assert width + 2 * ids_lanes <= pieces * LANES
     up_rows = pieces * parents
     leaf_rows = pieces * boxes
     own_rows = pieces * own
@@ -160,6 +163,7 @@
         child_ref,
         fields,
         slot_ref,
+        slots_ref,
         sems,
     ):
         me = lax.axis_index("lvl")
@@ -179,18 +183,24 @@
                 fields,
                 slice(p * LANES, (p + 1) * LANES),
             )
-        place = jnp.concatenate([place_ref[...], place_ref[...]], 0)
+        place = place_ref[...]
         octant = lax.rem(place, 8)
         spot = lax.div(octant, octants) * own + box_row(octant, place)
-        owner = jnp.concatenate(
-            [owner_ref[c] for c in range(classes)] + [jnp.zeros((classes, boxes), jnp.int32)], 0
-        )
-        ids = jnp.where(iota((2 * classes, boxes), 0) < classes, owner, spot)
+        spot = spot.astype(F32).astype(BF16)
+        owner = jnp.concatenate([owner_ref[c] for c in range(classes)], 0).astype(F32).astype(BF16)
         box = iota((boxes, LANES), 0)
         octant = lax.rem(box, 8)
-        spot = lax.div(octant, octants) * own + box_row(octant, box)
-        moved = iota((boxes, LANES), 1) == LANES - boxes + spot
-        ids = dot(ids.astype(F32).astype(BF16), moved.astype(F32).astype(BF16))
+        lane = iota((boxes, LANES), 1)
+        spread = lax.div(octant, octants) * parents + lax.div(box, 8)
+        ids = []
+        for half in range(2):
+            kept = lax.rem(octant, 2) == half
+            first = kept & (lane == spread + (LANES - 2 * ids_lanes))
+            second = kept & (lane == spread + (LANES - ids_lanes))
+            ids.append(
+                dot(owner, first.astype(F32).astype(BF16))
+                + dot(spot, second.astype(F32).astype(BF16))
+            )
 
         here = parents * LANES
         lane = iota((own + 8 * octants, here), 1)
@@ -200,7 +210,11 @@
         pick = (row == target).astype(F32).astype(BF16)
         leaf = dot(pick, fields[...].astype(BF16), NT)
         for k, block in enumerate(blocks128(leaf[0:own])):
-            slot_ref[k * own : (k + 1) * own, :] = block + (ids if k == pieces - 1 else 0.0)
+            for half in range(2):
+                rows = block[half * parents : (half + 1) * parents]
+                slot_ref[half, k * parents : (k + 1) * parents, :] = (
+                    rows + ids[half] if k == pieces - 1 else rows
+                )
         leaf = leaf.astype(BF16)
         copies[5].wait()
         total = None
@@ -208,36 +222,53 @@
             part = dot(leaf[own + 8 * o : own + 8 * o + 8], child_ref[o])
             total = part if total is None else total + part
         for k, block in enumerate(blocks128(total)):
-            first = own_rows + k * parents
-            slot_ref[first : first + parents, :] = block[0:parents]
-        sent_ref[...] = jnp.broadcast_to(slot_ref[...].astype(BF16)[None], sent_ref.shape)
-
-    slot_rows = own_rows + up_rows
+            for half in range(2):
+                first = up_rows + k * parents
+                slot_ref[half, first : first + parents, :] = block[0:parents]
+        slots_ref[...] = jnp.broadcast_to(
+            slot_ref[...].astype(BF16)[None], (devices // 2, 2, slot_rows, LANES)
+        ).reshape(slots_ref.shape)
+        copy = pltpu.make_async_copy(slots_ref, sent_ref, sems.at[6])
+        copy.start()
+        copy.wait()
+
+    slot_rows = 2 * up_rows
     devices = leaves * lvls
     up_inputs = (offsets, vel_cot, shell, leaf_owner, leaf_place, child_ops)
     sent = call(
         up_body,
-        shape((devices, slot_rows, LANES), BF16),
+        pltpu.HBM((devices, slot_rows, LANES), BF16),
         20_000_000,
         held(*up_inputs)
         + [
             pltpu.VMEM((3 * count, parents * LANES), F32),
-            pltpu.VMEM((slot_rows, LANES), F32),
-            pltpu.SemaphoreType.DMA((6,)),
+            pltpu.VMEM((2, slot_rows, LANES), F32),
+            pltpu.VMEM((devices, slot_rows, LANES), BF16),
+            pltpu.SemaphoreType.DMA((7,)),
         ],
         [HBM] * 6,
         40,
+        HBM,
     )(*in_hbm(*up_inputs))
     got = lax.all_to_all(sent, ("leaf", "lvl"), split_axis=0, concat_axis=0, tiled=True)
 
-    def shifted(value, k):
-        return lax.ppermute(value, "lvl", [(i, (i + k) % lvls) for i in range(lvls)])
+    def exchanged(values):
+        peers = []
+        for k in range(1, lvls):
+            peers.append(lax.ppermute(values[k], "lvl", [(i, i ^ k) for i in range(lvls)]))
+        return [values[0]] + peers
+
+    pair_ops = lax.ppermute(m2l_ops, "lvl", [(i, i ^ 1) for i in range(lvls)])
 
     def near_body(*refs):
-        sources, (near_ref, sel_ref), targets = refs[:6], refs[6:8], refs[8:14]
-        columns, table, sums, sems = refs[14:]
+        sources, pair_hbm, (near_ref, sel_ref, head_ref) = refs[:6], refs[6], refs[7:10]
+        targets = refs[10:16]
+        columns, table, sums, sems = refs[16:]
         q_ref, dir_ref, offsets_ref, vel_ref, owner_ref, place_ref = targets
-        for copy in start_all(sources, targets, sems):
+        *copies, head_copy = start_all(
+            (*sources, pair_hbm.at[: head_ref.shape[0]]), (*targets, head_ref), sems
+        )
+        for copy in copies:
             copy.wait()
         mine = lax.axis_index("leaf") * parents
         coarse = leaves * parents
@@ -309,12 +340,15 @@
             return 0
 
         lax.fori_loop(0, groups, block, 0)
-
-    near, select = call(
+        head_copy.wait()
+
+    heads = 2
+    near, select, pair_head = call(
         near_body,
         (
             shape((lvls, parents * 4, LANES), F32),
             shape((pieces, 8 * classes, leaves * up_rows), BF16),
+            shape((heads, width, width), BF16),
         ),
         100_000_000,
         [pltpu.SMEM(near_q.shape, jnp.int32), pltpu.SMEM(near_d.shape, jnp.int32)]
@@ -323,62 +357,85 @@
             pltpu.VMEM((tall, 8), F32),
             pltpu.VMEM((boxes, 8, LANES), F32),
             pltpu.VMEM((3, LANES, LANES), F32),
-            pltpu.SemaphoreType.DMA((6,)),
+            pltpu.SemaphoreType.DMA((7,)),
         ],
-        [HBM] * 6,
+        [HBM] * 7,
         24,
-    )(*in_hbm(near_q, near_d, offsets, vel_cot, coarse_owner, coarse_place))
-
-    def mid_body(got_ref, sel_ref, m2l_ref, near_ref, *refs):
-        *out_refs, leaf_sum = refs
+    )(*in_hbm(near_q, near_d, offsets, vel_cot, coarse_owner, coarse_place, pair_ops))
+
+    def mid_body(got_ref, sel_ref, m2l_ref, near_ref, head_ref, pair_hbm, *refs):
+        *out_refs, tail_ref, leaf_sum, sem = refs
+        copy = pltpu.make_async_copy(pair_hbm.at[heads:], tail_ref, sem)
+        copy.start()
         me = lax.axis_index("lvl")
         mine = lax.axis_index("leaf").astype(F32)
-        tops = got_ref[:, own_rows:, :].astype(F32).reshape(leaves, lvls, up_rows, LANES)
+        tops = got_ref[:, up_rows:, :].astype(F32).reshape(leaves, lvls, up_rows, LANES)
         tops = jnp.sum(tops, 1).astype(BF16).reshape(leaves * up_rows, LANES)
         chosen = jnp.concatenate([dot(sel_ref[k], tops) for k in range(pieces)], 1)
         high = chosen.astype(BF16).astype(F32)
         parts = jnp.where(iota(chosen.shape, 0) % 8 < parents, high, chosen - high)
 
-        per_tile = LANES // boxes
-        lane = iota((2 * classes, LANES), 1)
+        tile = (2 * classes, LANES)
+        lane, row = iota(tile, 1), iota(tile, 0)
+        doubled = iota((LANES, 2 * LANES), 1)
+        doubled = iota((LANES, 2 * LANES), 0) == lax.div(doubled, 8) * 4 + lax.rem(doubled, 4)
+        doubled = doubled.astype(F32).astype(BF16)
+        other = me + 1 - 2 * lax.rem(me, 2)
+        last = slice(up_rows - 8, up_rows)
         ids = []
-        for first in range(0, leaves, per_tile):
-            tile = jnp.zeros((2 * classes, LANES), F32)
-            for i in range(min(per_tile, leaves - first)):
-                piece = got_ref[(first + i) * lvls + me, own_rows - own : own_rows, :].astype(F32)
-                piece = pltpu.roll(piece, (i + 1) * boxes % LANES, 1)
-                tile = jnp.where(lax.div(lane, boxes) == i, piece, tile)
-            ids.append(tile)
-        ids = jnp.concatenate(ids, 1)[:, : leaves * boxes]
-        row = iota((boxes, leaves * boxes), 0).astype(F32)
+        for first in range(0, leaves, LANES // ids_lanes):
+            owner = spot = jnp.zeros(tile, F32)
+            for i in range(min(LANES // ids_lanes, leaves - first)):
+                at = (first + i) * lvls
+                piece = jnp.where(
+                    row < classes,
+                    pltpu.roll(got_ref[at + me, last, :].astype(F32), 4, 0),
+                    got_ref[at + other, last, :].astype(F32),
+                )
+                here = lax.div(lane, ids_lanes) == i
+                owner = jnp.where(here, pltpu.roll(piece, (i + 2) * ids_lanes % LANES, 1), owner)
+                spot = jnp.where(here, pltpu.roll(piece, (i + 1) * ids_lanes % LANES, 1), spot)
+            ids.append(dot(jnp.concatenate([owner, spot], 0).astype(BF16), doubled))
+        ids = jnp.concatenate(ids, 1)[:, : devices * 8]
+        spots = iota((boxes, devices * 8), 0).astype(F32)
         hits = jnp.concatenate(
             [
-                ((ids[c : c + 1] == mine) & (ids[classes + c : classes + c + 1] == row)).astype(F32)
-                for c in range(classes)
+                (
+                    (ids[c : c + 1] == mine) & (ids[2 * classes + c : 2 * classes + c + 1] == spots)
+                ).astype(F32)
+                for c in range(2 * classes)
             ],
             0,
-        ).astype(BF16)
+        )
+        upper = iota(hits.shape, 1) % 8 < 4
+        hits = [jnp.where(upper, hits, 0.0).astype(BF16), jnp.where(upper, 0.0, hits).astype(BF16)]
         gathered = jnp.concatenate(
             [
-                dot(hits, got_ref[:, k * own : (k + 1) * own, :].reshape(devices * own, LANES))
+                dot(hits[k % 2], got_ref[:, k // 2 * 8 : k // 2 * 8 + 8, :].reshape(devices * 8, LANES))
                 for k in range(pieces)
             ],
             1,
-        )
+        )[:, :width]
         total = None
         for c in range(classes):
             rows = jnp.concatenate(
-                [gathered[c * boxes : (c + 1) * boxes], parts[8 * c : 8 * c + 8]], 0
+                [gathered[c * boxes : (c + 1) * boxes], parts[8 * c : 8 * c + 8, :width]], 0
             )
-            part = dot(rows[:, :width].astype(BF16), m2l_ref[c])
+            part = dot(rows.astype(BF16), m2l_ref[c])
             total = part if total is None else total + part
-        for k, block in enumerate(blocks128(total[:boxes])):
+        leaf = total[:boxes]
+        for c in range(classes):
+            if c == heads:
+                copy.wait()
+            rows = gathered[(classes + c) * boxes : (classes + c + 1) * boxes]
+            leaf = leaf + dot(rows.astype(BF16), head_ref[c] if c < heads else tail_ref[c - heads])
+        for k, block in enumerate(blocks128(leaf)):
             leaf_sum[k * boxes : (k + 1) * boxes, :] = block
         total = total[boxes:]
         total = 0.5 * (total[0:parents] + total[parents : 2 * parents])
         total_blocks = blocks128(total)
         for k, out_ref in enumerate(out_refs):
-            peer = lax.rem(me + k, lvls)
+            peer = jnp.bitwise_xor(me, k)
             for i, block in enumerate(total_blocks):
                 out_ref[i * parents : (i + 1) * parents, :] = block.astype(out_ref.dtype)
             for i in range(pieces):
@@ -391,11 +448,15 @@
         mid_body,
         tuple(shape((pay_rows, LANES), BF16 if k else F32) for k in range(lvls)),
         20_000_000,
-        [pltpu.VMEM((leaf_rows, LANES), F32)],
-        [VMEM] * 4,
+        [
+            pltpu.VMEM((classes - heads, width, width), BF16),
+            pltpu.VMEM((leaf_rows, LANES), F32),
+            pltpu.SemaphoreType.DMA,
+        ],
+        [VMEM] * 5 + [HBM],
         40,
-    )(got, select, m2l_ops, near)
-    mids = [mids[0]] + [shifted(mids[k], k) for k in range(1, lvls)]
+    )(got, select, m2l_ops, near, pair_head, *in_hbm(pair_ops))
+    mids = exchanged(mids)
 
     def down_body(child_ref, map_ref, offsets_ref, shell_ref, *refs):
         *mid_refs, out_ref, dens = refs
@@ -449,13 +510,13 @@
         [pltpu.VMEM((3 * count, parents * LANES), F32)],
         [VMEM] * (4 + lvls),
     )(child_ops, check_map, offsets, shell, *mids)
-    forces = [forces] + [shifted(forces, k) for k in range(1, lvls)]
+    forces = exchanged([forces] * lvls)
 
     def join_body(*refs):
         *parts, out_ref = refs
         me = lax.axis_index("lvl")
         for k, ref in enumerate(parts):
-            peer = lax.rem(me + lvls - k, lvls)
+            peer = jnp.bitwise_xor(me, k)
             for p in range(parents):
                 out_ref[:, lanes_of(p, peer)] = ref[p * 4 : p * 4 + 3, :]
 

time: 34.7 us -> 33.2 us (0.957)
  waiting for transfers between devices: 10.4 us -> 8.52 us
  Pallas kernels: 11.3 us -> 13 us
  local copies, waits for them, and re-layouts: 0.76 us -> 0.02 us
  starting transfers between devices: 11.9 us -> 11.3 us
    all_to_all x1, waiting for transfers between devices: 6.26 us -> 3.56 us  [local(): lax.all_to_all(sent, ('leaf', 'lvl'), split_axis=0, concat_axis=0, tiled=...]
    pallas_call x1, Pallas kernels: 0.65 us -> 1.64 us  [local(): call(mid_body, tuple((shape((pay_rows, LANES), BF16 if k else F32) for k...]
    ppermute x6 -> x7, waiting for transfers between devices: 4.17 us -> 4.96 us  [the longest x6 4.96 us: exchanged(): lax.ppermute(values[k], 'lvl', [(i, i ^ k) for i in range(lvls)])]
    pallas_call x1, Pallas kernels: 1.89 us -> 2.64 us  [local(): call(up_body, pltpu.HBM((devices, slot_rows, LANES), BF16), 20000000, hel...]
    unnamed x12 -> x10, local copies, waits for them, and re-layouts: 0.76 us -> 0.02 us
    all_to_all x1, starting transfers between devices: 7.33 us -> 6.95 us  [local(): lax.all_to_all(sent, ('leaf', 'lvl'), split_axis=0, concat_axis=0, tiled=...]
    ppermute x6 -> x7, starting transfers between devices: 4.59 us -> 4.34 us  [the longest x6 3.84 us: exchanged(): lax.ppermute(values[k], 'lvl', [(i, i ^ k) for i in range(lvls)])]
  transfers between devices with their start and end apart: 7 -> 8, of which waited for: 5 -> 5; matrix products, arithmetic and copies ran while one was open for 0% -> 0% of each run, Pallas kernels for 20% -> 29%
where the time goes in v4:
time: 33.2 us; the launch traced here: 32.9 us
  Pallas kernels  13 us (39%)
  starting transfers between devices  11.3 us (34%)
  waiting for transfers between devices  8.52 us (26%)
    pallas_call x1, Pallas kernels, local(): call(near_body, (shape((lvls, parents * 4, LANES), F32), shape((pieces, 8...  6.99 us
    all_to_all x1, starting transfers between devices, local(): lax.all_to_all(sent, ('leaf', 'lvl'), split_axis=0, concat_axis=0, tiled=...  6.95 us
    ppermute x6, waiting for transfers between devices, exchanged(): lax.ppermute(values[k], 'lvl', [(i, i ^ k) for i in range(lvls)])  4.96 us
    ppermute x6, starting transfers between devices, exchanged(): lax.ppermute(values[k], 'lvl', [(i, i ^ k) for i in range(lvls)])  3.84 us
    all_to_all x1, waiting for transfers between devices, local(): lax.all_to_all(sent, ('leaf', 'lvl'), split_axis=0, concat_axis=0, tiled=...  3.56 us
    pallas_call x1, Pallas kernels, local(): call(up_body, pltpu.HBM((devices, slot_rows, LANES), BF16), 20000000, hel...  2.64 us
    pallas_call x1, Pallas kernels, local(): call(mid_body, tuple((shape((pay_rows, LANES), BF16 if k else F32) for k...  1.64 us
    pallas_call x1, Pallas kernels, local(): call(down_body, shape((parents * 4, LANES), F32), 20000000, [pltpu.VMEM((...  1.08 us
  transfers between devices with their start and end apart: 8, of which 5 were waited for; matrix products, arithmetic and copies ran while one was open for 0% of the time, Pallas kernels for 29%

profile of v4, /device:TPU:0, one launch (start us, length us, event | category | flops | bytes accessed | tf_op | source)
XLA Modules:
  0.0 32.9 jit_solution(4881974509775071805)
XLA Ops:
  0.0 0.5 %collective-permute-start = (bf16[4,456,456]{2,1,0:T(8,128)(2,1)}, bf16[4,456,456]{2,1,0:T(8,128)(2,1)}, u32[]{:S(2)}, u32[]{:S(2)}) collective-permute-start(bf16[4,456,456]{2,1,0:T(8,128)(2,1)} %m2l_ref.1), channel_id=1, source_target_pairs={{0,1},{1,0},{2,3},{3,2},{4,5},{5,4},{6,7},{7,6},{8,9},{9,8},{10,11... | collective-permute-start | bytes 4990472 | tf_op jit(solution)/shard_map/ppermute | solution.py:261
  0.5 0.0 copy-start.1
  0.5 2.6 %shard_map.118 = bf16[32,32,128]{2,1,0:T(8,128)(2,1)} custom-call(f32[3,2048]{1,0:T(4,128)} %offsets_ref.1, f32[3,2048]{1,0:T(4,128)} %refs_3_.1, f32[456,128]{1,0:T(8,128)} %constant.2.clone.shell_hbm.shell_ref, s32[4,1,32]{2,1,0:T(1,128)} %bitcast.18, s32[4,32]{1,0:T(4,128)} %bitcast.19, bf16[2,456,456]{2,1,0:T(8,128)(2,1)} %child_ref.1), custom_call_target="tpu_custom_call" | custom-call | flops 20000000 | bytes 1048576 | tf_op jit(solution)/shard_map/pallas_call | solution.py:238
  3.1 7.0 %all-to-all-start = ((bf16[32,32,128]{2,1,0:T(8,128)(2,1)}), bf16[32,32,128]{2,1,0:T(8,128)(2,1)S(1)}, u32[]{:S(2)}, u32[]{:S(2)}) async-start(bf16[32,32,128]{2,1,0:T(8,128)(2,1)} %shard_map.118), calls=%async_computation | async-start | bytes 524288 | tf_op jit(solution)/shard_map/all_to_all | solution.py:253
  10.1 0.0 collective-permute-done.refs_6_.pair_hbm
  10.1 7.0 %shard_map.119 = (f32[4,16,128]{2,1,0:T(8,128)S(1)}, bf16[4,32,128]{2,1,0:T(8,128)(2,1)S(1)}, bf16[2,456,456]{2,1,0:T(8,128)(2,1)S(1)}) custom-call(s32[4,32]{1,0:T(4,128)} %bitcast.20, s32[4,32]{1,0:T(4,128)} %bitcast.21, f32[3,2048]{1,0:T(4,128)} %offsets_ref.1, f32[3,2048]{1,0:T(4,128)} %refs_3_.1, s32[4,1,32]{2,1,0:T(1,128)} %bitcast.22, ...), custom_call_target="tpu_custom_call" | custom-call | flops 100000000 | bytes 1048576 | tf_op jit(solution)/shard_map/pallas_call | solution.py:346
  17.1 3.6 %all-to-all-done.got_ref = bf16[32,32,128]{2,1,0:T(8,128)(2,1)S(1)} async-done(((bf16[32,32,128]{2,1,0:T(8,128)(2,1)}), bf16[32,32,128]{2,1,0:T(8,128)(2,1)S(1)}, u32[]{:S(2)}, u32[]{:S(2)}) %all-to-all-start) | async-done | bytes 262176 | tf_op jit(solution)/shard_map/all_to_all | solution.py:253
  20.7 0.0 copy-done.1
  20.7 0.0 copy-start
  20.7 0.0 copy-start.2
  20.7 0.0 copy-start.3
  20.7 0.0 copy-start.4
  20.7 1.6 %shard_map.120 = (f32[64,128]{1,0:T(8,128)S(1)}, bf16[64,128]{1,0:T(8,128)(2,1)S(1)}, bf16[64,128]{1,0:T(8,128)(2,1)S(1)}, bf16[64,128]{1,0:T(8,128)(2,1)S(1)}) custom-call(bf16[32,32,128]{2,1,0:T(8,128)(2,1)S(1)} %all-to-all-done.got_ref, bf16[4,32,128]{2,1,0:T(8,128)(2,1)S(1)} %get-tuple-element.12.sel_ref, bf16[4,456,456]{2,1,0:T(8,128)(2,1)S(1)} %copy-done.1, ...), custom_call_target="tpu_custom_call" | custom-call | flops 20000000 | bytes 1048576 | tf_op jit(solution)/shard_map/pallas_call | solution.py:447
  22.4 0.1 collective-permute-start.1
  22.4 0.8 %collective-permute-start.2 = (bf16[64,128]{1,0:T(8,128)(2,1)S(1)}, bf16[64,128]{1,0:T(8,128)(2,1)S(1)}, u32[]{:S(2)}, u32[]{:S(2)}) collective-permute-start(bf16[64,128]{1,0:T(8,128)(2,1)S(1)} %get-tuple-element.17), channel_id=1, source_target_pairs={{0,2},{1,3},{2,0},{3,1},{4,6},{5,7},{6,4},{7,5},{8,10},{9,11},{10,... | collective-permute-start | bytes 49160 | tf_op jit(solution)/shard_map/ppermute | solution.py:258
  23.2 1.0 %collective-permute-start.3 = (bf16[64,128]{1,0:T(8,128)(2,1)S(1)}, bf16[64,128]{1,0:T(8,128)(2,1)S(1)}, u32[]{:S(2)}, u32[]{:S(2)}) collective-permute-start(bf16[64,128]{1,0:T(8,128)(2,1)S(1)} %get-tuple-element.18), channel_id=1, source_target_pairs={{0,3},{1,2},{2,1},{3,0},{4,7},{5,6},{6,5},{7,4},{8,11},{9,10},{10,... | collective-permute-start | bytes 49160 | tf_op jit(solution)/shard_map/ppermute | solution.py:258
  24.3 0.0 collective-permute-done.1.refs_1_
  24.3 2.0 %collective-permute-done.2.refs_2_ = bf16[64,128]{1,0:T(8,128)(2,1)S(1)} collective-permute-done((bf16[64,128]{1,0:T(8,128)(2,1)S(1)}, bf16[64,128]{1,0:T(8,128)(2,1)S(1)}, u32[]{:S(2)}, u32[]{:S(2)}) %collective-permute-start.2) | collective-permute-done | bytes 16416 | tf_op jit(solution)/shard_map/ppermute | solution.py:258
  26.2 0.3 %collective-permute-done.3.refs_3_ = bf16[64,128]{1,0:T(8,128)(2,1)S(1)} collective-permute-done((bf16[64,128]{1,0:T(8,128)(2,1)S(1)}, bf16[64,128]{1,0:T(8,128)(2,1)S(1)}, u32[]{:S(2)}, u32[]{:S(2)}) %collective-permute-start.3) | collective-permute-done | bytes 16416 | tf_op jit(solution)/shard_map/ppermute | solution.py:258
  26.6 0.0 copy-done
  26.6 0.0 copy-done.2
  26.6 0.0 copy-done.3
  26.6 0.0 copy-done.4
  26.6 1.1 %shard_map.121.refs_0_ = f32[16,128]{1,0:T(8,128)S(1)} custom-call(bf16[2,456,456]{2,1,0:T(8,128)(2,1)S(1)} %copy-done, f32[456,456]{1,0:T(8,128)S(1)} %copy-done.3, f32[3,2048]{1,0:T(4,128)S(1)} %copy-done.4, f32[456,128]{1,0:T(8,128)S(1)} %copy-done.2, f32[64,128]{1,0:T(8,128)S(1)} %get-tuple-element.15.refs_0_, ...), custom_call_target="tpu_custom_call" | custom-call | flops 20000000 | bytes 1048576 | tf_op jit(solution)/shard_map/pallas_call | solution.py:506
  27.7 0.9 %collective-permute-start.6 = (f32[16,128]{1,0:T(8,128)S(1)}, f32[16,128]{1,0:T(8,128)S(1)}, u32[]{:S(2)}, u32[]{:S(2)}) collective-permute-start(f32[16,128]{1,0:T(8,128)S(1)} %shard_map.121.refs_0_), channel_id=1, source_target_pairs={{0,3},{1,2},{2,1},{3,0},{4,7},{5,6},{6,5},{7,4},{8,11},{9,10},{10,... | collective-permute-start | bytes 24584 | tf_op jit(solution)/shard_map/ppermute | solution.py:258
  28.6 0.9 %collective-permute-start.5 = (f32[16,128]{1,0:T(8,128)S(1)}, f32[16,128]{1,0:T(8,128)S(1)}, u32[]{:S(2)}, u32[]{:S(2)}) collective-permute-start(f32[16,128]{1,0:T(8,128)S(1)} %shard_map.121.refs_0_), channel_id=1, source_target_pairs={{0,2},{1,3},{2,0},{3,1},{4,6},{5,7},{6,4},{7,5},{8,10},{9,11},{10,... | collective-permute-start | bytes 24584 | tf_op jit(solution)/shard_map/ppermute | solution.py:258
  29.5 0.1 collective-permute-start.4
  29.6 1.2 %collective-permute-done.6.refs_3_ = f32[16,128]{1,0:T(8,128)S(1)} collective-permute-done((f32[16,128]{1,0:T(8,128)S(1)}, f32[16,128]{1,0:T(8,128)S(1)}, u32[]{:S(2)}, u32[]{:S(2)}) %collective-permute-start.6) | collective-permute-done | bytes 8224 | tf_op jit(solution)/shard_map/ppermute | solution.py:258
  30.8 1.4 %collective-permute-done.5.refs_2_ = f32[16,128]{1,0:T(8,128)S(1)} collective-permute-done((f32[16,128]{1,0:T(8,128)S(1)}, f32[16,128]{1,0:T(8,128)S(1)}, u32[]{:S(2)}, u32[]{:S(2)}) %collective-permute-start.5) | collective-permute-done | bytes 8224 | tf_op jit(solution)/shard_map/ppermute | solution.py:258
  32.3 0.0 collective-permute-done.4.refs_1_
  32.3 0.6 %shard_map.122 = f32[3,2048]{1,0:T(4,128)} custom-call(f32[16,128]{1,0:T(8,128)S(1)} %shard_map.121.refs_0_, f32[16,128]{1,0:T(8,128)S(1)} %collective-permute-done.4.refs_1_, f32[16,128]{1,0:T(8,128)S(1)} %collective-permute-done.5.refs_2_, f32[16,128]{1,0:T(8,128)S(1)} %collective-permute-done.6.refs_3_), custom_call_target="tpu_custom_call" | custom-call | flops 100000 | bytes 1048576 | tf_op jit(solution)/shard_map/pallas_call | solution.py:523
Async XLA Ops:
  0.0 10.1 %collective-permute-start = (bf16[4,456,456]{2,1,0:T(8,128)(2,1)}, bf16[4,456,456]{2,1,0:T(8,128)(2,1)}, u32[]{:S(2)}, u32[]{:S(2)}) collective-permute-start(bf16[4,456,456]{2,1,0:T(8,128)(2,1)} %m2l_ref.1), channel_id=1, source_target_pairs={{0,1},{1,0},{2,3},{3,2},{4,5},{5,4},{6,7},{7,6},{8,9},{9,8},{10,11... | collective-permute-start | bytes 4990472 | tf_op jit(solution)/shard_map/ppermute | solution.py:261
  0.5 20.2 %copy-start.1 = (bf16[4,456,456]{2,1,0:T(8,128)(2,1)S(1)}, bf16[4,456,456]{2,1,0:T(8,128)(2,1)}, u32[]{:S(2)}) copy-start(bf16[4,456,456]{2,1,0:T(8,128)(2,1)} %m2l_ref.1) | copy-start | bytes 4990468
  3.1 17.5 %all-to-all-start = ((bf16[32,32,128]{2,1,0:T(8,128)(2,1)}), bf16[32,32,128]{2,1,0:T(8,128)(2,1)S(1)}, u32[]{:S(2)}, u32[]{:S(2)}) async-start(bf16[32,32,128]{2,1,0:T(8,128)(2,1)} %shard_map.118), calls=%async_computation | async-start | bytes 524288 | tf_op jit(solution)/shard_map/all_to_all | solution.py:253
  20.7 5.9 %copy-start = (bf16[2,456,456]{2,1,0:T(8,128)(2,1)S(1)}, bf16[2,456,456]{2,1,0:T(8,128)(2,1)}, u32[]{:S(2)}) copy-start(bf16[2,456,456]{2,1,0:T(8,128)(2,1)} %child_ref.1) | copy-start | bytes 2495236
  20.7 5.9 %copy-start.2 = (f32[456,128]{1,0:T(8,128)S(1)}, f32[456,128]{1,0:T(8,128)}, u32[]{:S(2)}) copy-start(f32[456,128]{1,0:T(8,128)} %constant.2.clone.shell_hbm.shell_ref) | copy-start | bytes 700420
  20.7 5.9 %copy-start.3 = (f32[456,456]{1,0:T(8,128)S(1)}, f32[456,456]{1,0:T(8,128)}, u32[]{:S(2)}) copy-start(f32[456,456]{1,0:T(8,128)} %map_ref.1) | copy-start | bytes 2495236
  20.7 5.9 %copy-start.4 = (f32[3,2048]{1,0:T(4,128)S(1)}, f32[3,2048]{1,0:T(4,128)}, u32[]{:S(2)}) copy-start(f32[3,2048]{1,0:T(4,128)} %offsets_ref.1) | copy-start | bytes 73732
  22.4 1.9 %collective-permute-start.1 = (bf16[64,128]{1,0:T(8,128)(2,1)S(1)}, bf16[64,128]{1,0:T(8,128)(2,1)S(1)}, u32[]{:S(2)}, u32[]{:S(2)}) collective-permute-start(bf16[64,128]{1,0:T(8,128)(2,1)S(1)} %get-tuple-element.16), channel_id=1, source_target_pairs={{0,1},{1,0},{2,3},{3,2},{4,5},{5,4},{6,7},{7,6},{8,9},{9,8},{10,11... | collective-permute-start | bytes 49160 | tf_op jit(solution)/shard_map/ppermute | solution.py:258
  22.4 3.8 %collective-permute-start.2 = (bf16[64,128]{1,0:T(8,128)(2,1)S(1)}, bf16[64,128]{1,0:T(8,128)(2,1)S(1)}, u32[]{:S(2)}, u32[]{:S(2)}) collective-permute-start(bf16[64,128]{1,0:T(8,128)(2,1)S(1)} %get-tuple-element.17), channel_id=1, source_target_pairs={{0,2},{1,3},{2,0},{3,1},{4,6},{5,7},{6,4},{7,5},{8,10},{9,11},{10,... | collective-permute-start | bytes 49160 | tf_op jit(solution)/shard_map/ppermute | solution.py:258
  23.2 3.3 %collective-permute-start.3 = (bf16[64,128]{1,0:T(8,128)(2,1)S(1)}, bf16[64,128]{1,0:T(8,128)(2,1)S(1)}, u32[]{:S(2)}, u32[]{:S(2)}) collective-permute-start(bf16[64,128]{1,0:T(8,128)(2,1)S(1)} %get-tuple-element.18), channel_id=1, source_target_pairs={{0,3},{1,2},{2,1},{3,0},{4,7},{5,6},{6,5},{7,4},{8,11},{9,10},{10,... | collective-permute-start | bytes 49160 | tf_op jit(solution)/shard_map/ppermute | solution.py:258
  27.7 3.1 %collective-permute-start.6 = (f32[16,128]{1,0:T(8,128)S(1)}, f32[16,128]{1,0:T(8,128)S(1)}, u32[]{:S(2)}, u32[]{:S(2)}) collective-permute-start(f32[16,128]{1,0:T(8,128)S(1)} %shard_map.121.refs_0_), channel_id=1, source_target_pairs={{0,3},{1,2},{2,1},{3,0},{4,7},{5,6},{6,5},{7,4},{8,11},{9,10},{10,... | collective-permute-start | bytes 24584 | tf_op jit(solution)/shard_map/ppermute | solution.py:258
  28.6 3.7 %collective-permute-start.5 = (f32[16,128]{1,0:T(8,128)S(1)}, f32[16,128]{1,0:T(8,128)S(1)}, u32[]{:S(2)}, u32[]{:S(2)}) collective-permute-start(f32[16,128]{1,0:T(8,128)S(1)} %shard_map.121.refs_0_), channel_id=1, source_target_pairs={{0,2},{1,3},{2,0},{3,1},{4,6},{5,7},{6,4},{7,5},{8,10},{9,11},{10,... | collective-permute-start | bytes 24584 | tf_op jit(solution)/shard_map/ppermute | solution.py:258
  29.5 2.8 %collective-permute-start.4 = (f32[16,128]{1,0:T(8,128)S(1)}, f32[16,128]{1,0:T(8,128)S(1)}, u32[]{:S(2)}, u32[]{:S(2)}) collective-permute-start(f32[16,128]{1,0:T(8,128)S(1)} %shard_map.121.refs_0_), channel_id=1, source_target_pairs={{0,1},{1,0},{2,3},{3,2},{4,5},{5,4},{6,7},{7,6},{8,9},{9,8},{10,11... | collective-permute-start | bytes 24584 | tf_op jit(solution)/shard_map/ppermute | solution.py:258

commit v5 on v4

--- a/solution.py
+++ b/solution.py
@@ -34,11 +34,15 @@
     return lax.broadcasted_iota(jnp.int32, shape, axis)
 
 
-def stokeslet(d, v):
+def factors(d):
     r2 = d[0] * d[0] + d[1] * d[1] + (d[2] * d[2] + EPSILON2)
     rs = lax.rsqrt(r2)
     weight = rs * (rs * rs)
-    scale = rs + EPSILON2 * weight
+    return rs + EPSILON2 * weight, weight
+
+
+def stokeslet(d, v):
+    scale, weight = factors(d)
     along = weight * (d[0] * v[0] + d[1] * v[1] + d[2] * v[2])
     return [scale * v[c] + along * d[c] for c in range(3)]
 
@@ -48,7 +52,7 @@
         body,
         out_shape=outs,
         in_specs=ins,
-        out_specs=jax.tree.map(lambda _: spec, outs),
+        out_specs=spec if isinstance(spec, tuple) else jax.tree.map(lambda _: spec, outs),
         scratch_shapes=list(scratch),
         cost_estimate=pl.CostEstimate(flops=cost, bytes_accessed=1 << 20, transcendentals=0),
         compiler_params=pltpu.CompilerParams(vmem_limit_bytes=vmem << 20),
@@ -216,6 +220,21 @@
                     rows + ids[half] if k == pieces - 1 else rows
                 )
         leaf = leaf.astype(BF16)
+        slots = (devices // 2, 2, up_rows, LANES)
+        parts = [slice(0, up_rows), slice(up_rows, slot_rows)]
+        leaving = [
+            pltpu.make_async_copy(slots_ref.at[:, part], sent_ref.at[:, part], sems.at[6 + i])
+            for i, part in enumerate(parts)
+        ]
+
+        def leave(i):
+            rows = slot_ref[:, parts[i], :].astype(BF16)
+            slots_ref[:, parts[i], :] = jnp.broadcast_to(rows[None], slots).reshape(
+                devices, up_rows, LANES
+            )
+            leaving[i].start()
+
+        leave(0)
         copies[5].wait()
         total = None
         for o in range(octants):
@@ -225,12 +244,9 @@
             for half in range(2):
                 first = up_rows + k * parents
                 slot_ref[half, first : first + parents, :] = block[0:parents]
-        slots_ref[...] = jnp.broadcast_to(
-            slot_ref[...].astype(BF16)[None], (devices // 2, 2, slot_rows, LANES)
-        ).reshape(slots_ref.shape)
-        copy = pltpu.make_async_copy(slots_ref, sent_ref, sems.at[6])
-        copy.start()
-        copy.wait()
+        leave(1)
+        for copy in leaving:
+            copy.wait()
 
     slot_rows = 2 * up_rows
     devices = leaves * lvls
@@ -244,7 +260,7 @@
             pltpu.VMEM((3 * count, parents * LANES), F32),
             pltpu.VMEM((2, slot_rows, LANES), F32),
             pltpu.VMEM((devices, slot_rows, LANES), BF16),
-            pltpu.SemaphoreType.DMA((7,)),
+            pltpu.SemaphoreType.DMA((8,)),
         ],
         [HBM] * 6,
         40,
@@ -261,14 +277,10 @@
     pair_ops = lax.ppermute(m2l_ops, "lvl", [(i, i ^ 1) for i in range(lvls)])
 
     def near_body(*refs):
-        sources, pair_hbm, (near_ref, sel_ref, head_ref) = refs[:6], refs[6], refs[7:10]
-        targets = refs[10:16]
-        columns, table, sums, sems = refs[16:]
+        sources, (near_ref, sel_ref), targets = refs[:6], refs[6:8], refs[8:14]
+        columns, table, sums, sems = refs[14:]
         q_ref, dir_ref, offsets_ref, vel_ref, owner_ref, place_ref = targets
-        *copies, head_copy = start_all(
-            (*sources, pair_hbm.at[: head_ref.shape[0]]), (*targets, head_ref), sems
-        )
-        for copy in copies:
+        for copy in start_all(sources, targets, sems):
             copy.wait()
         mine = lax.axis_index("leaf") * parents
         coarse = leaves * parents
@@ -340,15 +352,12 @@
             return 0
 
         lax.fori_loop(0, groups, block, 0)
-        head_copy.wait()
-
-    heads = 2
-    near, select, pair_head = call(
+
+    near, select = call(
         near_body,
         (
             shape((lvls, parents * 4, LANES), F32),
             shape((pieces, 8 * classes, leaves * up_rows), BF16),
-            shape((heads, width, width), BF16),
         ),
         100_000_000,
         [pltpu.SMEM(near_q.shape, jnp.int32), pltpu.SMEM(near_d.shape, jnp.int32)]
@@ -357,15 +366,37 @@
             pltpu.VMEM((tall, 8), F32),
             pltpu.VMEM((boxes, 8, LANES), F32),
             pltpu.VMEM((3, LANES, LANES), F32),
-            pltpu.SemaphoreType.DMA((7,)),
+            pltpu.SemaphoreType.DMA((6,)),
         ],
-        [HBM] * 7,
+        [HBM] * 6,
         24,
-    )(*in_hbm(near_q, near_d, offsets, vel_cot, coarse_owner, coarse_place, pair_ops))
-
-    def mid_body(got_ref, sel_ref, m2l_ref, near_ref, head_ref, pair_hbm, *refs):
+    )(*in_hbm(near_q, near_d, offsets, vel_cot, coarse_owner, coarse_place))
+
+    heads = classes // 2
+
+    def hold_body(m2l_hbm, pair_ref, near_ref, m2l_ref, head_ref, tail_ref, sems):
+        copies = start_all((m2l_hbm, pair_ref.at[heads:]), (m2l_ref, tail_ref), sems)
+        head_ref[...] = pair_ref[:heads]
+        for copy in copies:
+            copy.wait()
+
+    own_ops, head_ops, tail_ops = call(
+        hold_body,
+        (
+            shape(m2l_ops.shape, BF16),
+            shape((heads, width, width), BF16),
+            pltpu.HBM((classes - heads, width, width), BF16),
+        ),
+        1_000_000,
+        [pltpu.SemaphoreType.DMA((2,))],
+        [HBM, VMEM, VMEM],
+        24,
+        (VMEM, VMEM, HBM),
+    )(*in_hbm(m2l_ops), pair_ops, near)
+
+    def mid_body(got_ref, sel_ref, m2l_ref, near_ref, head_ref, tail_hbm, *refs):
         *out_refs, tail_ref, leaf_sum, sem = refs
-        copy = pltpu.make_async_copy(pair_hbm.at[heads:], tail_ref, sem)
+        copy = pltpu.make_async_copy(tail_hbm, tail_ref, sem)
         copy.start()
         me = lax.axis_index("lvl")
         mine = lax.axis_index("leaf").astype(F32)
@@ -448,17 +479,58 @@
         mid_body,
         tuple(shape((pay_rows, LANES), BF16 if k else F32) for k in range(lvls)),
         20_000_000,
-        [
-            pltpu.VMEM((classes - heads, width, width), BF16),
-            pltpu.VMEM((leaf_rows, LANES), F32),
-            pltpu.SemaphoreType.DMA,
-        ],
+        held(tail_ops) + [pltpu.VMEM((leaf_rows, LANES), F32), pltpu.SemaphoreType.DMA],
         [VMEM] * 5 + [HBM],
         40,
-    )(got, select, m2l_ops, near, pair_head, *in_hbm(pair_ops))
+    )(got, select, own_ops, near, head_ops, *in_hbm(tail_ops))
     mids = exchanged(mids)
 
-    def down_body(child_ref, map_ref, offsets_ref, shell_ref, *refs):
+    geo_rows = parents * count
+
+    def prep_body(
+        offsets_hbm, shell_hbm, child_hbm, map_hbm, offsets_ref, shell_ref, child_ref, split_ref, scale_ref, weight_ref, map_ref, sems
+    ):
+        copies = start_all(
+            (offsets_hbm, shell_hbm, map_hbm, child_hbm),
+            (offsets_ref, shell_ref, map_ref, child_ref),
+            sems,
+        )
+        me = lax.axis_index("lvl")
+        for copy in copies[:2]:
+            copy.wait()
+        for p in range(parents):
+            target = rows3(offsets_ref, lanes_of(p, me))
+            for row in range(0, count, 8):
+                d = [
+                    target[c] - shell_ref[c * count + row : c * count + row + 8, :]
+                    for c in range(3)
+                ]
+                rows = slice(p * count + row, p * count + row + 8)
+                scale_ref[rows, :], weight_ref[rows, :] = factors(d)
+        copies[2].wait()
+        mapped = map_ref[...]
+        high = mapped.astype(BF16)
+        split_ref[0] = high
+        split_ref[1] = (mapped - high.astype(F32)).astype(BF16)
+        copies[3].wait()
+
+    prep_inputs = (offsets, shell, child_ops, check_map)
+    prepared = call(
+        prep_body,
+        (
+            shape(offsets.shape, F32),
+            shape(shell.shape, F32),
+            shape(child_ops.shape, BF16),
+            shape((2, width, width), BF16),
+            shape((geo_rows, LANES), F32),
+            shape((geo_rows, LANES), F32),
+        ),
+        2_000_000,
+        held(check_map) + [pltpu.SemaphoreType.DMA((4,))],
+        [HBM] * 4,
+    )(*in_hbm(*prep_inputs))
+
+    def down_body(offsets_ref, shell_ref, child_ref, split_ref, scale_ref, weight_ref, *refs):
         *mid_refs, out_ref, dens = refs
         me = lax.axis_index("lvl")
         total = mid_refs[0][...]
@@ -474,10 +546,7 @@
         mult = leaf + lowered
         high = mult.astype(BF16)
         pair = jnp.concatenate([high.astype(F32), mult - high.astype(F32)], 0).astype(BF16)
-        mapped = map_ref[...]
-        coarse_map = mapped.astype(BF16)
-        fine_map = (mapped - coarse_map.astype(F32)).astype(BF16)
-        first, second = dot(pair, coarse_map), dot(pair, fine_map)
+        first, second = dot(pair, split_ref[0]), dot(pair, split_ref[1])
         check = first[0:own] + first[own:] + second[0:own] + second[own:]
         high = check.astype(BF16).astype(F32)
         pair = jnp.concatenate([high, check - high], 0).astype(BF16)
@@ -492,13 +561,13 @@
             lanes = slice(p * LANES, (p + 1) * LANES)
             force = [jnp.zeros((8, LANES), F32) for _ in range(3)]
             for row in range(0, count, 8):
-                d = [
-                    target[c] - shell_ref[c * count + row : c * count + row + 8, :]
-                    for c in range(3)
-                ]
-                q = [dens[c * count + row : c * count + row + 8, lanes] for c in range(3)]
-                part = stokeslet(d, q)
-                force = [force[c] + part[c] for c in range(3)]
+                spots = [slice(c * count + row, c * count + row + 8) for c in range(3)]
+                d = [target[c] - shell_ref[spots[c], :] for c in range(3)]
+                q = [dens[spots[c], lanes] for c in range(3)]
+                rows = slice(p * count + row, p * count + row + 8)
+                scale = scale_ref[rows, :]
+                along = weight_ref[rows, :] * (d[0] * q[0] + d[1] * q[1] + d[2] * q[2])
+                force = [force[c] + (scale * q[c] + along * d[c]) for c in range(3)]
             for c in range(3):
                 row = p * 4 + c
                 out_ref[row : row + 1, :] += jnp.sum(force[c], 0, keepdims=True)
@@ -508,8 +577,8 @@
         shape((parents * 4, LANES), F32),
         20_000_000,
         [pltpu.VMEM((3 * count, parents * LANES), F32)],
-        [VMEM] * (4 + lvls),
-    )(child_ops, check_map, offsets, shell, *mids)
+        [VMEM] * (6 + lvls),
+    )(*prepared, *mids)
     forces = exchanged([forces] * lvls)
 
     def join_body(*refs):

time: 33.2 us -> 34.4 us (1.036)
  waiting for transfers between devices: 8.52 us -> 3.62 us
  Pallas kernels: 13 us -> 16.2 us
  local copies, waits for them, and re-layouts: 0.02 us -> 2.78 us
    pallas_call x0 -> x2, Pallas kernels: none -> 3.52 us  [the longest x1 1.87 us: local(): call(hold_body, (shape(m2l_ops.shape, BF16), shape((heads, width, width),...]
    all_to_all x1, waiting for transfers between devices: 3.56 us -> 0.41 us  [local(): lax.all_to_all(sent, ('leaf', 'lvl'), split_axis=0, concat_axis=0, tiled=...]
    unnamed x10 -> x4, local copies, waits for them, and re-layouts: 0.02 us -> 2.78 us
    ppermute x6, waiting for transfers between devices: 4.96 us -> 3.2 us  [exchanged(): lax.ppermute(values[k], 'lvl', [(i, i ^ k) for i in range(lvls)])]
  transfers between devices with their start and end apart: 8 -> 8, of which waited for: 5 -> 5; matrix products, arithmetic and copies ran while one was open for 0% -> 0% of each run, Pallas kernels for 29% -> 38%
where the time goes in v5:
time: 34.4 us; the launch traced here: 34 us
  Pallas kernels  16.2 us (47%)
  starting transfers between devices  11.3 us (33%)
  waiting for transfers between devices  3.62 us (11%)
  local copies, waits for them, and re-layouts  2.78 us (8%)
    pallas_call x1, Pallas kernels, local(): call(near_body, (shape((lvls, parents * 4, LANES), F32), shape((pieces, 8...  6.98 us
    all_to_all x1, starting transfers between devices, local(): lax.all_to_all(sent, ('leaf', 'lvl'), split_axis=0, concat_axis=0, tiled=...  6.95 us
    ppermute x6, starting transfers between devices, exchanged(): lax.ppermute(values[k], 'lvl', [(i, i ^ k) for i in range(lvls)])  3.84 us
    ppermute x6, waiting for transfers between devices, exchanged(): lax.ppermute(values[k], 'lvl', [(i, i ^ k) for i in range(lvls)])  3.2 us
    unnamed x4, local copies, waits for them, and re-layouts  2.78 us
    pallas_call x1, Pallas kernels, local(): call(up_body, pltpu.HBM((devices, slot_rows, LANES), BF16), 20000000, hel...  2.47 us
    pallas_call x1, Pallas kernels, local(): call(hold_body, (shape(m2l_ops.shape, BF16), shape((heads, width, width),...  1.87 us
    pallas_call x1, Pallas kernels, local(): call(prep_body, (shape(offsets.shape, F32), shape(shell.shape, F32), shap...  1.64 us
  transfers between devices with their start and end apart: 8, of which 5 were waited for; matrix products, arithmetic and copies ran while one was open for 0% of the time, Pallas kernels for 38%

profile of v5, /device:TPU:0, one launch (start us, length us, event | category | flops | bytes accessed | tf_op | source)
XLA Modules:
  0.0 34.0 jit_solution(18350730131752333189)
XLA Ops:
  0.0 0.5 %collective-permute-start = (bf16[4,456,456]{2,1,0:T(8,128)(2,1)}, bf16[4,456,456]{2,1,0:T(8,128)(2,1)S(1)}, u32[]{:S(2)}, u32[]{:S(2)}) collective-permute-start(bf16[4,456,456]{2,1,0:T(8,128)(2,1)} %m2l_hbm.1), channel_id=1, source_target_pairs={{0,1},{1,0},{2,3},{3,2},{4,5},{5,4},{6,7},{7,6},{8,9},{9,8},{10,11... | collective-permute-start | bytes 4990472 | tf_op jit(solution)/shard_map/ppermute | solution.py:277
  0.5 2.5 %shard_map.119 = bf16[32,32,128]{2,1,0:T(8,128)(2,1)} custom-call(f32[3,2048]{1,0:T(4,128)} %refs_2_.1, f32[3,2048]{1,0:T(4,128)} %refs_3_.1, f32[456,128]{1,0:T(8,128)} %constant.2.clone.shell_hbm, s32[4,1,32]{2,1,0:T(1,128)} %bitcast.18, s32[4,32]{1,0:T(4,128)} %bitcast.19, bf16[2,456,456]{2,1,0:T(8,128)(2,1)} %child_hbm.3), custom_call_target="tpu_custom_call" | custom-call | flops 20000000 | bytes 1048576 | tf_op jit(solution)/shard_map/pallas_call | solution.py:254
  3.0 7.0 %all-to-all-start = ((bf16[32,32,128]{2,1,0:T(8,128)(2,1)}), bf16[32,32,128]{2,1,0:T(8,128)(2,1)S(1)}, u32[]{:S(2)}, u32[]{:S(2)}) async-start(bf16[32,32,128]{2,1,0:T(8,128)(2,1)} %shard_map.119), calls=%async_computation | async-start | bytes 524288 | tf_op jit(solution)/shard_map/all_to_all | solution.py:269
  9.9 7.0 %shard_map.120 = (f32[4,16,128]{2,1,0:T(8,128)S(1)}, bf16[4,32,128]{2,1,0:T(8,128)(2,1)S(1)}) custom-call(s32[4,32]{1,0:T(4,128)} %bitcast.20, s32[4,32]{1,0:T(4,128)} %bitcast.21, f32[3,2048]{1,0:T(4,128)} %refs_2_.1, f32[3,2048]{1,0:T(4,128)} %refs_3_.1, s32[4,1,32]{2,1,0:T(1,128)} %bitcast.22, s32[4,32]{1,0:T(4,128)} %bitcast.23), custom_call_target="tpu_custom_call" | custom-call | flops 100000000 | bytes 1048576 | tf_op jit(solution)/shard_map/pallas_call | solution.py:356
  16.9 0.0 collective-permute-done.pair_ref
  16.9 1.9 %shard_map.121 = (bf16[4,456,456]{2,1,0:T(8,128)(2,1)S(1)}, bf16[2,456,456]{2,1,0:T(8,128)(2,1)S(1)}, bf16[2,456,456]{2,1,0:T(8,128)(2,1)}) custom-call(bf16[4,456,456]{2,1,0:T(8,128)(2,1)} %m2l_hbm.1, bf16[4,456,456]{2,1,0:T(8,128)(2,1)S(1)} %collective-permute-done.pair_ref, f32[4,16,128]{2,1,0:T(8,128)S(1)} %get-tuple-element.27.near_ref), custom_call_target="tpu_custom_call" | custom-call | flops 1000000 | bytes 1048576 | tf_op jit(solution)/shard_map/pallas_call | solution.py:383
  18.8 0.0 copy-start
  18.8 1.3 %copy-done = bf16[4,456,456]{2,1,0:T(8,128)(2,1)} copy-done((bf16[4,456,456]{2,1,0:T(8,128)(2,1)}, bf16[4,456,456]{2,1,0:T(8,128)(2,1)S(1)}, u32[]{:S(2)}) %copy-start) | copy-done | bytes 1663512
  20.1 0.4 %all-to-all-done.got_ref = bf16[32,32,128]{2,1,0:T(8,128)(2,1)S(1)} async-done(((bf16[32,32,128]{2,1,0:T(8,128)(2,1)}), bf16[32,32,128]{2,1,0:T(8,128)(2,1)S(1)}, u32[]{:S(2)}, u32[]{:S(2)}) %all-to-all-start) | async-done | bytes 262176 | tf_op jit(solution)/shard_map/all_to_all | solution.py:269
  20.5 0.0 copy-start.1
  20.5 1.5 %copy-done.1 = bf16[4,456,456]{2,1,0:T(8,128)(2,1)S(1)} copy-done((bf16[4,456,456]{2,1,0:T(8,128)(2,1)S(1)}, bf16[4,456,456]{2,1,0:T(8,128)(2,1)}, u32[]{:S(2)}) %copy-start.1) | copy-done | bytes 1663512
  22.0 1.5 %shard_map.122 = (f32[64,128]{1,0:T(8,128)S(1)}, bf16[64,128]{1,0:T(8,128)(2,1)S(1)}, bf16[64,128]{1,0:T(8,128)(2,1)S(1)}, bf16[64,128]{1,0:T(8,128)(2,1)S(1)}) custom-call(bf16[32,32,128]{2,1,0:T(8,128)(2,1)S(1)} %all-to-all-done.got_ref, bf16[4,32,128]{2,1,0:T(8,128)(2,1)S(1)} %get-tuple-element.26.sel_ref, bf16[4,456,456]{2,1,0:T(8,128)(2,1)S(1)} %copy-done.1, ...), custom_call_target="tpu_custom_call" | custom-call | flops 20000000 | bytes 1048576 | tf_op jit(solution)/shard_map/pallas_call | solution.py:478
  23.5 0.1 collective-permute-start.1
  23.6 1.5 %collective-permute-start.2 = (bf16[64,128]{1,0:T(8,128)(2,1)S(1)}, bf16[64,128]{1,0:T(8,128)(2,1)S(1)}, u32[]{:S(2)}, u32[]{:S(2)}) collective-permute-start(bf16[64,128]{1,0:T(8,128)(2,1)S(1)} %get-tuple-element.33), channel_id=1, source_target_pairs={{0,2},{1,3},{2,0},{3,1},{4,6},{5,7},{6,4},{7,5},{8,10},{9,11},{10,... | collective-permute-start | bytes 49160 | tf_op jit(solution)/shard_map/ppermute | solution.py:274
  25.1 0.4 %collective-permute-start.3 = (bf16[64,128]{1,0:T(8,128)(2,1)S(1)}, bf16[64,128]{1,0:T(8,128)(2,1)S(1)}, u32[]{:S(2)}, u32[]{:S(2)}) collective-permute-start(bf16[64,128]{1,0:T(8,128)(2,1)S(1)} %get-tuple-element.34), channel_id=1, source_target_pairs={{0,3},{1,2},{2,1},{3,0},{4,7},{5,6},{6,5},{7,4},{8,11},{9,10},{10,... | collective-permute-start | bytes 49160 | tf_op jit(solution)/shard_map/ppermute | solution.py:274
  25.4 1.6 %shard_map.118 = (f32[3,2048]{1,0:T(4,128)S(1)}, f32[456,128]{1,0:T(8,128)S(1)}, bf16[2,456,456]{2,1,0:T(8,128)(2,1)S(1)}, bf16[2,456,456]{2,1,0:T(8,128)(2,1)S(...) custom-call(f32[3,2048]{1,0:T(4,128)} %refs_2_.1, f32[456,128]{1,0:T(8,128)} %constant.2.clone.shell_hbm, ...), custom_call_target="tpu_custom_call" | custom-call | flops 2000000 | bytes 1048576 | tf_op jit(solution)/shard_map/pallas_call | solution.py:518
  27.1 0.0 collective-permute-done.1.refs_1_
  27.1 0.3 collective-permute-done.2.refs_2_
  27.4 0.8 %collective-permute-done.3.refs_3_ = bf16[64,128]{1,0:T(8,128)(2,1)S(1)} collective-permute-done((bf16[64,128]{1,0:T(8,128)(2,1)S(1)}, bf16[64,128]{1,0:T(8,128)(2,1)S(1)}, u32[]{:S(2)}, u32[]{:S(2)}) %collective-permute-start.3) | collective-permute-done | bytes 16416 | tf_op jit(solution)/shard_map/ppermute | solution.py:274
  28.2 1.1 %shard_map.123.refs_0_ = f32[16,128]{1,0:T(8,128)S(1)} custom-call(f32[3,2048]{1,0:T(4,128)S(1)} %get-tuple-element.20.offsets_ref, f32[456,128]{1,0:T(8,128)S(1)} %get-tuple-element.21.shell_ref, bf16[2,456,456]{2,1,0:T(8,128)(2,1)S(1)} %get-tuple-element.22.child_ref, bf16[2,456,456]{2,1,0:T(8,128)(2,1)S(1)} %get-tuple-element.23.split_ref, ...), custom_call_target="tpu_custom_call" | custom-call | flops 20000000 | bytes 1048576 | tf_op jit(solution)/shard_map/pallas_call | solution.py:575
  29.3 0.2 collective-permute-start.4
  29.5 0.8 %collective-permute-start.5 = (f32[16,128]{1,0:T(8,128)S(1)}, f32[16,128]{1,0:T(8,128)S(1)}, u32[]{:S(2)}, u32[]{:S(2)}) collective-permute-start(f32[16,128]{1,0:T(8,128)S(1)} %shard_map.123.refs_0_), channel_id=1, source_target_pairs={{0,2},{1,3},{2,0},{3,1},{4,6},{5,7},{6,4},{7,5},{8,10},{9,11},{10,... | collective-permute-start | bytes 24584 | tf_op jit(solution)/shard_map/ppermute | solution.py:274
  30.3 1.0 %collective-permute-start.6 = (f32[16,128]{1,0:T(8,128)S(1)}, f32[16,128]{1,0:T(8,128)S(1)}, u32[]{:S(2)}, u32[]{:S(2)}) collective-permute-start(f32[16,128]{1,0:T(8,128)S(1)} %shard_map.123.refs_0_), channel_id=1, source_target_pairs={{0,3},{1,2},{2,1},{3,0},{4,7},{5,6},{6,5},{7,4},{8,11},{9,10},{10,... | collective-permute-start | bytes 24584 | tf_op jit(solution)/shard_map/ppermute | solution.py:274
  31.3 0.0 collective-permute-done.4.refs_1_
  31.3 1.9 %collective-permute-done.5.refs_2_ = f32[16,128]{1,0:T(8,128)S(1)} collective-permute-done((f32[16,128]{1,0:T(8,128)S(1)}, f32[16,128]{1,0:T(8,128)S(1)}, u32[]{:S(2)}, u32[]{:S(2)}) %collective-permute-start.5) | collective-permute-done | bytes 8224 | tf_op jit(solution)/shard_map/ppermute | solution.py:274
  33.2 0.2 collective-permute-done.6.refs_3_
  33.3 0.6 %shard_map.124 = f32[3,2048]{1,0:T(4,128)} custom-call(f32[16,128]{1,0:T(8,128)S(1)} %shard_map.123.refs_0_, f32[16,128]{1,0:T(8,128)S(1)} %collective-permute-done.4.refs_1_, f32[16,128]{1,0:T(8,128)S(1)} %collective-permute-done.5.refs_2_, f32[16,128]{1,0:T(8,128)S(1)} %collective-permute-done.6.refs_3_), custom_call_target="tpu_custom_call" | custom-call | flops 100000 | bytes 1048576 | tf_op jit(solution)/shard_map/pallas_call | solution.py:592
Async XLA Ops:
  0.0 16.9 %collective-permute-start = (bf16[4,456,456]{2,1,0:T(8,128)(2,1)}, bf16[4,456,456]{2,1,0:T(8,128)(2,1)S(1)}, u32[]{:S(2)}, u32[]{:S(2)}) collective-permute-start(bf16[4,456,456]{2,1,0:T(8,128)(2,1)} %m2l_hbm.1), channel_id=1, source_target_pairs={{0,1},{1,0},{2,3},{3,2},{4,5},{5,4},{6,7},{7,6},{8,9},{9,8},{10,11... | collective-permute-start | bytes 4990472 | tf_op jit(solution)/shard_map/ppermute | solution.py:277
  3.0 17.5 %all-to-all-start = ((bf16[32,32,128]{2,1,0:T(8,128)(2,1)}), bf16[32,32,128]{2,1,0:T(8,128)(2,1)S(1)}, u32[]{:S(2)}, u32[]{:S(2)}) async-start(bf16[32,32,128]{2,1,0:T(8,128)(2,1)} %shard_map.119), calls=%async_computation | async-start | bytes 524288 | tf_op jit(solution)/shard_map/all_to_all | solution.py:269
  18.8 1.3 %copy-start = (bf16[4,456,456]{2,1,0:T(8,128)(2,1)}, bf16[4,456,456]{2,1,0:T(8,128)(2,1)S(1)}, u32[]{:S(2)}) copy-start(bf16[4,456,456]{2,1,0:T(8,128)(2,1)S(1)} %get-tuple-element.28.m2l_ref) | copy-start | bytes 4990468
  20.5 1.5 %copy-start.1 = (bf16[4,456,456]{2,1,0:T(8,128)(2,1)S(1)}, bf16[4,456,456]{2,1,0:T(8,128)(2,1)}, u32[]{:S(2)}) copy-start(bf16[4,456,456]{2,1,0:T(8,128)(2,1)} %copy-done) | copy-start | bytes 4990468
  23.5 3.6 %collective-permute-start.1 = (bf16[64,128]{1,0:T(8,128)(2,1)S(1)}, bf16[64,128]{1,0:T(8,128)(2,1)S(1)}, u32[]{:S(2)}, u32[]{:S(2)}) collective-permute-start(bf16[64,128]{1,0:T(8,128)(2,1)S(1)} %get-tuple-element.32), channel_id=1, source_target_pairs={{0,1},{1,0},{2,3},{3,2},{4,5},{5,4},{6,7},{7,6},{8,9},{9,8},{10,11... | collective-permute-start | bytes 49160 | tf_op jit(solution)/shard_map/ppermute | solution.py:274
  23.6 3.8 %collective-permute-start.2 = (bf16[64,128]{1,0:T(8,128)(2,1)S(1)}, bf16[64,128]{1,0:T(8,128)(2,1)S(1)}, u32[]{:S(2)}, u32[]{:S(2)}) collective-permute-start(bf16[64,128]{1,0:T(8,128)(2,1)S(1)} %get-tuple-element.33), channel_id=1, source_target_pairs={{0,2},{1,3},{2,0},{3,1},{4,6},{5,7},{6,4},{7,5},{8,10},{9,11},{10,... | collective-permute-start | bytes 49160 | tf_op jit(solution)/shard_map/ppermute | solution.py:274
  25.1 3.2 %collective-permute-start.3 = (bf16[64,128]{1,0:T(8,128)(2,1)S(1)}, bf16[64,128]{1,0:T(8,128)(2,1)S(1)}, u32[]{:S(2)}, u32[]{:S(2)}) collective-permute-start(bf16[64,128]{1,0:T(8,128)(2,1)S(1)} %get-tuple-element.34), channel_id=1, source_target_pairs={{0,3},{1,2},{2,1},{3,0},{4,7},{5,6},{6,5},{7,4},{8,11},{9,10},{10,... | collective-permute-start | bytes 49160 | tf_op jit(solution)/shard_map/ppermute | solution.py:274
  29.3 1.9 %collective-permute-start.4 = (f32[16,128]{1,0:T(8,128)S(1)}, f32[16,128]{1,0:T(8,128)S(1)}, u32[]{:S(2)}, u32[]{:S(2)}) collective-permute-start(f32[16,128]{1,0:T(8,128)S(1)} %shard_map.123.refs_0_), channel_id=1, source_target_pairs={{0,1},{1,0},{2,3},{3,2},{4,5},{5,4},{6,7},{7,6},{8,9},{9,8},{10,11... | collective-permute-start | bytes 24584 | tf_op jit(solution)/shard_map/ppermute | solution.py:274
  29.5 3.7 %collective-permute-start.5 = (f32[16,128]{1,0:T(8,128)S(1)}, f32[16,128]{1,0:T(8,128)S(1)}, u32[]{:S(2)}, u32[]{:S(2)}) collective-permute-start(f32[16,128]{1,0:T(8,128)S(1)} %shard_map.123.refs_0_), channel_id=1, source_target_pairs={{0,2},{1,3},{2,0},{3,1},{4,6},{5,7},{6,4},{7,5},{8,10},{9,11},{10,... | collective-permute-start | bytes 24584 | tf_op jit(solution)/shard_map/ppermute | solution.py:274
  30.3 3.1 %collective-permute-start.6 = (f32[16,128]{1,0:T(8,128)S(1)}, f32[16,128]{1,0:T(8,128)S(1)}, u32[]{:S(2)}, u32[]{:S(2)}) collective-permute-start(f32[16,128]{1,0:T(8,128)S(1)} %shard_map.123.refs_0_), channel_id=1, source_target_pairs={{0,3},{1,2},{2,1},{3,0},{4,7},{5,6},{6,5},{7,4},{8,11},{9,10},{10,... | collective-permute-start | bytes 24584 | tf_op jit(solution)/shard_map/ppermute | solution.py:274

commit v6 on v5

--- a/solution.py
+++ b/solution.py
@@ -10,6 +10,7 @@
 EPSILON2 = 0.01
 RADIUS = 0.525
 LANES = 128
+UNROLL = 4
 F32 = jnp.float32
 BF16 = jnp.bfloat16
 VMEM = pl.BlockSpec(memory_space=pltpu.VMEM)
@@ -130,6 +131,7 @@
     ids_lanes = boxes // 2
     assert width + 2 * ids_lanes <= pieces * LANES
     up_rows = pieces * parents
+    half_rows = up_rows // 2
     leaf_rows = pieces * boxes
     own_rows = pieces * own
     tall = groups * LANES
@@ -220,7 +222,6 @@
                     rows + ids[half] if k == pieces - 1 else rows
                 )
         leaf = leaf.astype(BF16)
-        slots = (devices // 2, 2, up_rows, LANES)
         parts = [slice(0, up_rows), slice(up_rows, slot_rows)]
         leaving = [
             pltpu.make_async_copy(slots_ref.at[:, part], sent_ref.at[:, part], sems.at[6 + i])
@@ -229,9 +230,10 @@
 
         def leave(i):
             rows = slot_ref[:, parts[i], :].astype(BF16)
-            slots_ref[:, parts[i], :] = jnp.broadcast_to(rows[None], slots).reshape(
-                devices, up_rows, LANES
-            )
+            high = rows.shape[1]
+            slots_ref[:, parts[i], :] = jnp.broadcast_to(
+                rows[None], (devices // 2, 2, high, LANES)
+            ).reshape(devices, high, LANES)
             leaving[i].start()
 
         leave(0)
@@ -241,14 +243,14 @@
             part = dot(leaf[own + 8 * o : own + 8 * o + 8], child_ref[o])
             total = part if total is None else total + part
         for k, block in enumerate(blocks128(total)):
-            for half in range(2):
-                first = up_rows + k * parents
-                slot_ref[half, first : first + parents, :] = block[0:parents]
+            for p in range(parents):
+                row = up_rows + k * (parents // 2) + p // 2
+                slot_ref[p % 2, row : row + 1, :] = block[p : p + 1]
         leave(1)
         for copy in leaving:
             copy.wait()
 
-    slot_rows = 2 * up_rows
+    slot_rows = up_rows + half_rows
     devices = leaves * lvls
     up_inputs = (offsets, vel_cot, shell, leaf_owner, leaf_place, child_ops)
     sent = call(
@@ -274,48 +276,31 @@
             peers.append(lax.ppermute(values[k], "lvl", [(i, i ^ k) for i in range(lvls)]))
         return [values[0]] + peers
 
-    pair_ops = lax.ppermute(m2l_ops, "lvl", [(i, i ^ 1) for i in range(lvls)])
+    pair_ops, pair_owner, pair_place = [
+        lax.ppermute(value, "lvl", [(i, i ^ 1) for i in range(lvls)])
+        for value in (m2l_ops, coarse_owner, coarse_place)
+    ]
 
     def near_body(*refs):
-        sources, (near_ref, sel_ref), targets = refs[:6], refs[6:8], refs[8:14]
-        columns, table, sums, sems = refs[14:]
-        q_ref, dir_ref, offsets_ref, vel_ref, owner_ref, place_ref = targets
+        sources, near_ref, targets = refs[:4], refs[4], refs[5:9]
+        table, sums, sems = refs[9:]
+        q_ref, dir_ref, offsets_ref, vel_ref = targets
         for copy in start_all(sources, targets, sems):
             copy.wait()
-        mine = lax.axis_index("leaf") * parents
-        coarse = leaves * parents
-        pick = jnp.concatenate(
-            [
-                (
-                    owner_ref[c] * parents + place_ref[c : c + 1, :]
-                    == mine + iota((8, coarse), 0) % parents
-                ).astype(F32)
-                for c in range(classes)
-            ],
-            0,
-        ).astype(BF16)
-        spread = (coarse, leaves * up_rows)
-        lane = iota(spread, 1)
-        for k in range(pieces):
-            expand = (iota(spread, 0) == lane // up_rows * parents + lane % parents) & (
-                lane % up_rows // parents == k
-            )
-            sel_ref[k] = dot(pick, expand.astype(F32).astype(BF16)).astype(BF16)
-
         left = iota((8, LANES), 1) < per_box
         for j in range(groups):
             lanes = slice(j * LANES, (j + 1) * LANES)
             tile = jnp.concatenate(
                 [offsets_ref[:, lanes], vel_ref[:, lanes], jnp.zeros((2, LANES), F32)], 0
             )
-            columns[lanes, :] = tile.T
             turned = pltpu.roll(tile, per_box, 1)
             table[2 * j] = jnp.where(left, tile, turned)
             table[2 * j + 1] = jnp.where(left, turned, tile)
         near_ref[...] = jnp.zeros_like(near_ref)
         ones = jnp.ones((8, LANES), BF16)
 
-        def block(j, _):
+        def block(j, slot):
+            columns = jnp.where(left, table[2 * j], table[2 * j + 1]).T
             for h in range(2):
                 box = 2 * j + h
                 sources = []
@@ -337,62 +322,85 @@
                         )
                     sources.append(rows)
                 for row in range(0, per_box, 8):
-                    tile = columns[pl.ds(pl.multiple_of(box * per_box + row, 8), 8), :]
+                    tile = columns[h * per_box + row : h * per_box + row + 8]
                     target = [jnp.broadcast_to(tile[:, c : c + 1], (8, LANES)) for c in range(3)]
                     force = None
                     for rows in sources:
                         part = stokeslet([target[c] - rows[c] for c in range(3)], rows[3:])
                         force = part if force is None else [x + y for x, y in zip(force, part)]
                     for c in range(3):
-                        sums[c, h * per_box + row : h * per_box + row + 8, :] = force[c]
+                        sums[slot, c, h * per_box + row : h * per_box + row + 8, :] = force[c]
             p, lvl = lax.div(j, lvls), lax.rem(j, lvls)
             for c in range(3):
-                total = dot(ones, sums[c].astype(BF16), NT)
+                total = dot(ones, sums[slot, c].astype(BF16), NT)
                 near_ref[lvl, pl.ds(p * 4 + c, 1), :] = total[0:1]
+
+        def step(i, _):
+            for part in range(UNROLL):
+                block(i * UNROLL + part, part)
             return 0
 
-        lax.fori_loop(0, groups, block, 0)
-
-    near, select = call(
+        lax.fori_loop(0, groups // UNROLL, step, 0)
+
+    near = call(
         near_body,
-        (
-            shape((lvls, parents * 4, LANES), F32),
-            shape((pieces, 8 * classes, leaves * up_rows), BF16),
-        ),
+        shape((lvls, parents * 4, LANES), F32),
         100_000_000,
         [pltpu.SMEM(near_q.shape, jnp.int32), pltpu.SMEM(near_d.shape, jnp.int32)]
-        + held(offsets, vel_cot, coarse_owner, coarse_place)
+        + held(offsets, vel_cot)
         + [
-            pltpu.VMEM((tall, 8), F32),
             pltpu.VMEM((boxes, 8, LANES), F32),
-            pltpu.VMEM((3, LANES, LANES), F32),
-            pltpu.SemaphoreType.DMA((6,)),
+            pltpu.VMEM((UNROLL, 3, LANES, LANES), F32),
+            pltpu.SemaphoreType.DMA((4,)),
         ],
-        [HBM] * 6,
+        [HBM] * 4,
         24,
-    )(*in_hbm(near_q, near_d, offsets, vel_cot, coarse_owner, coarse_place))
+    )(*in_hbm(near_q, near_d, offsets, vel_cot))
 
     heads = classes // 2
 
-    def hold_body(m2l_hbm, pair_ref, near_ref, m2l_ref, head_ref, tail_ref, sems):
-        copies = start_all((m2l_hbm, pair_ref.at[heads:]), (m2l_ref, tail_ref), sems)
+    def hold_body(
+        owner_hbm, place_hbm, pair_ref, near_ref, *refs
+    ):
+        (pair_owner_ref, pair_place_ref), (sel_ref, head_ref, tail_ref) = refs[:2], refs[2:5]
+        owner_ref, place_ref, sems = refs[5:]
+        copies = start_all(
+            (owner_hbm, place_hbm, pair_ref.at[heads:]), (owner_ref, place_ref, tail_ref), sems
+        )
         head_ref[...] = pair_ref[:heads]
-        for copy in copies:
+        coarse = leaves * parents
+        spread = (coarse, leaves * half_rows)
+        lane = iota(spread, 1)
+        parent = lane // half_rows * parents + lane % 2 * 2 + lax.rem(lax.axis_index("lvl"), 2)
+        for copy in copies[:2]:
             copy.wait()
-
-    own_ops, head_ops, tail_ops = call(
+        mine = lax.axis_index("leaf") * parents + iota((8, coarse), 0) % parents
+        pick = jnp.concatenate(
+            [
+                (owners[c] * parents + places[c : c + 1, :] == mine).astype(F32)
+                for owners, places in ((owner_ref, place_ref), (pair_owner_ref, pair_place_ref))
+                for c in range(classes)
+            ],
+            0,
+        ).astype(BF16)
+        for k in range(pieces):
+            expand = (iota(spread, 0) == parent) & (lane % half_rows // 2 == k)
+            sel_ref[k] = dot(pick, expand.astype(F32).astype(BF16)).astype(BF16)
+        copies[2].wait()
+
+    select, head_ops, tail_ops = call(
         hold_body,
         (
-            shape(m2l_ops.shape, BF16),
+            shape((pieces, 16 * classes, leaves * half_rows), BF16),
             shape((heads, width, width), BF16),
             pltpu.HBM((classes - heads, width, width), BF16),
         ),
         1_000_000,
-        [pltpu.SemaphoreType.DMA((2,))],
-        [HBM, VMEM, VMEM],
+        held(coarse_owner, coarse_place) + [pltpu.SemaphoreType.DMA((3,))],
+        [HBM] * 2 + [VMEM] * 4,
         24,
         (VMEM, VMEM, HBM),
-    )(*in_hbm(m2l_ops), pair_ops, near)
+    )(*in_hbm(coarse_owner, coarse_place), pair_ops, near, pair_owner, pair_place)
 
     def mid_body(got_ref, sel_ref, m2l_ref, near_ref, head_ref, tail_hbm, *refs):
         *out_refs, tail_ref, leaf_sum, sem = refs
@@ -400,8 +408,8 @@
         copy.start()
         me = lax.axis_index("lvl")
         mine = lax.axis_index("leaf").astype(F32)
-        tops = got_ref[:, up_rows:, :].astype(F32).reshape(leaves, lvls, up_rows, LANES)
-        tops = jnp.sum(tops, 1).astype(BF16).reshape(leaves * up_rows, LANES)
+        tops = got_ref[:, up_rows:, :].astype(F32).reshape(leaves, lvls, half_rows, LANES)
+        tops = jnp.sum(tops, 1).astype(BF16).reshape(leaves * half_rows, LANES)
         chosen = jnp.concatenate([dot(sel_ref[k], tops) for k in range(pieces)], 1)
         high = chosen.astype(BF16).astype(F32)
         parts = jnp.where(iota(chosen.shape, 0) % 8 < parents, high, chosen - high)
@@ -448,18 +456,21 @@
             1,
         )[:, :width]
         total = None
-        for c in range(classes):
+        for c in range(2 * classes):
             rows = jnp.concatenate(
                 [gathered[c * boxes : (c + 1) * boxes], parts[8 * c : 8 * c + 8, :width]], 0
             )
-            part = dot(rows.astype(BF16), m2l_ref[c])
+            if c < classes:
+                operator = m2l_ref[c]
+            elif c < classes + heads:
+                operator = head_ref[c - classes]
+            else:
+                if c == classes + heads:
+                    copy.wait()
+                operator = tail_ref[c - classes - heads]
+            part = dot(rows.astype(BF16), operator)
             total = part if total is None else total + part
         leaf = total[:boxes]
-        for c in range(classes):
-            if c == heads:
-                copy.wait()
-            rows = gathered[(classes + c) * boxes : (classes + c + 1) * boxes]
-            leaf = leaf + dot(rows.astype(BF16), head_ref[c] if c < heads else tail_ref[c - heads])
         for k, block in enumerate(blocks128(leaf)):
             leaf_sum[k * boxes : (k + 1) * boxes, :] = block
         total = total[boxes:]
@@ -482,7 +493,7 @@
         held(tail_ops) + [pltpu.VMEM((leaf_rows, LANES), F32), pltpu.SemaphoreType.DMA],
         [VMEM] * 5 + [HBM],
         40,
-    )(got, select, own_ops, near, head_ops, *in_hbm(tail_ops))
+    )(got, select, m2l_ops, near, head_ops, *in_hbm(tail_ops))
     mids = exchanged(mids)
 
     geo_rows = parents * count

time: 34.4 us -> 31.7 us (0.922)
  local copies, waits for them, and re-layouts: 2.78 us -> 0.01 us
  Pallas kernels: 16.2 us -> 14.5 us
  waiting for transfers between devices: 3.62 us -> 4.78 us
  starting transfers between devices: 11.3 us -> 12 us
    unnamed x4 -> x2, local copies, waits for them, and re-layouts: 2.78 us -> 0.01 us
    pallas_call x2, Pallas kernels: 8.85 us -> 7.1 us  [the longest x1 4.61 us: local(): call(near_body, shape((lvls, parents * 4, LANES), F32), 100000000, [pltpu...]
    all_to_all x1, waiting for transfers between devices: 0.41 us -> 1.23 us  [local(): lax.all_to_all(sent, ('leaf', 'lvl'), split_axis=0, concat_axis=0, tiled=...]
    ppermute x1 -> x3, starting transfers between devices: 0.49 us -> 1.07 us  [local(): lax.ppermute(value, 'lvl', [(i, i ^ 1) for i in range(lvls)])]
    ppermute x6, waiting for transfers between devices: 3.2 us -> 3.55 us  [exchanged(): lax.ppermute(values[k], 'lvl', [(i, i ^ k) for i in range(lvls)])]
  transfers between devices with their start and end apart: 8 -> 10, of which waited for: 5 -> 4; matrix products, arithmetic and copies ran while one was open for 0% -> 0% of each run, Pallas kernels for 38% -> 36%
where the time goes in v6:
time: 31.7 us; the launch traced here: 31.3 us
  Pallas kernels  14.5 us (46%)
  starting transfers between devices  12 us (38%)
  waiting for transfers between devices  4.78 us (15%)
    all_to_all x1, starting transfers between devices, local(): lax.all_to_all(sent, ('leaf', 'lvl'), split_axis=0, concat_axis=0, tiled=...  6.96 us
    pallas_call x1, Pallas kernels, local(): call(near_body, shape((lvls, parents * 4, LANES), F32), 100000000, [pltpu...  4.61 us
    ppermute x6, starting transfers between devices, exchanged(): lax.ppermute(values[k], 'lvl', [(i, i ^ k) for i in range(lvls)])  3.93 us
    ppermute x6, waiting for transfers between devices, exchanged(): lax.ppermute(values[k], 'lvl', [(i, i ^ k) for i in range(lvls)])  3.55 us
    pallas_call x1, Pallas kernels, local(): call(up_body, pltpu.HBM((devices, slot_rows, LANES), BF16), 20000000, hel...  2.56 us
    pallas_call x1, Pallas kernels, local(): call(hold_body, (shape((pieces, 16 * classes, leaves * half_rows), BF16),...  2.49 us
    pallas_call x1, Pallas kernels, local(): call(prep_body, (shape(offsets.shape, F32), shape(shell.shape, F32), shap...  1.64 us
    pallas_call x1, Pallas kernels, local(): call(mid_body, tuple((shape((pay_rows, LANES), BF16 if k else F32) for k...  1.5 us
  transfers between devices with their start and end apart: 10, of which 4 were waited for; matrix products, arithmetic and copies ran while one was open for 0% of the time, Pallas kernels for 36%

profile of v6, /device:TPU:0, one launch (start us, length us, event | category | flops | bytes accessed | tf_op | source)
XLA Modules:
  0.0 31.3 jit_solution(7305479131054481861)
XLA Ops:
  0.0 0.5 %collective-permute-start = (bf16[4,456,456]{2,1,0:T(8,128)(2,1)}, bf16[4,456,456]{2,1,0:T(8,128)(2,1)}, u32[]{:S(2)}, u32[]{:S(2)}) collective-permute-start(bf16[4,456,456]{2,1,0:T(8,128)(2,1)} %m2l_ref.1), channel_id=1, source_target_pairs={{0,1},{1,0},{2,3},{3,2},{4,5},{5,4},{6,7},{7,6},{8,9},{9,8},{10,11... | collective-permute-start | bytes 4990472 | tf_op jit(solution)/shard_map/ppermute | solution.py:280
  0.5 0.0 copy-start
  0.5 2.6 %shard_map.119 = bf16[32,24,128]{2,1,0:T(8,128)(2,1)} custom-call(f32[3,2048]{1,0:T(4,128)} %refs_2_.1, f32[3,2048]{1,0:T(4,128)} %refs_3_.1, f32[456,128]{1,0:T(8,128)} %constant.2.clone.shell_hbm, s32[4,1,32]{2,1,0:T(1,128)} %bitcast.18, s32[4,32]{1,0:T(4,128)} %bitcast.19, bf16[2,456,456]{2,1,0:T(8,128)(2,1)} %child_hbm.3), custom_call_target="tpu_custom_call" | custom-call | flops 20000000 | bytes 1048576 | tf_op jit(solution)/shard_map/pallas_call | solution.py:256
  3.1 7.0 %all-to-all-start = ((bf16[32,24,128]{2,1,0:T(8,128)(2,1)}), bf16[32,24,128]{2,1,0:T(8,128)(2,1)S(1)}, u32[]{:S(2)}, u32[]{:S(2)}) async-start(bf16[32,24,128]{2,1,0:T(8,128)(2,1)} %shard_map.119), calls=%async_computation | async-start | bytes 393216 | tf_op jit(solution)/shard_map/all_to_all | solution.py:271
  10.0 0.3 %collective-permute-start.1 = (s32[4,1,32]{2,1,0:T(1,128)}, s32[4,1,32]{2,1,0:T(1,128)S(1)}, u32[]{:S(2)}, u32[]{:S(2)}) collective-permute-start(s32[4,1,32]{2,1,0:T(1,128)} %bitcast.20), channel_id=1, source_target_pairs={{0,1},{1,0},{2,3},{3,2},{4,5},{5,4},{6,7},{7,6},{8,9},{9,8},{10,11... | collective-permute-start | bytes 1544 | tf_op jit(solution)/shard_map/ppermute | solution.py:280
  10.3 0.3 collective-permute-start.2
  10.6 4.6 %shard_map.120.near_ref = f32[4,16,128]{2,1,0:T(8,128)S(1)} custom-call(s32[4,32]{1,0:T(4,128)} %bitcast.24, s32[4,32]{1,0:T(4,128)} %bitcast.25, f32[3,2048]{1,0:T(4,128)} %refs_2_.1, f32[3,2048]{1,0:T(4,128)} %refs_3_.1), custom_call_target="tpu_custom_call" | custom-call | flops 100000000 | bytes 1048576 | tf_op jit(solution)/shard_map/pallas_call | solution.py:345
  15.2 0.0 collective-permute-done.1.refs_0_
  15.2 0.0 collective-permute-done.2.refs_1_
  15.2 0.0 collective-permute-done.pair_ref
  15.3 2.5 %shard_map.121 = (bf16[4,64,64]{2,1,0:T(8,128)(2,1)S(1)}, bf16[2,456,456]{2,1,0:T(8,128)(2,1)S(1)}, bf16[2,456,456]{2,1,0:T(8,128)(2,1)}) custom-call(s32[4,1,32]{2,1,0:T(1,128)} %bitcast.21, s32[4,32]{1,0:T(4,128)} %bitcast.23, bf16[4,456,456]{2,1,0:T(8,128)(2,1)} %collective-permute-done.pair_ref, f32[4,16,128]{2,1,0:T(8,128)S(1)} %shard_map.120.near_ref, ...), custom_call_target="tpu_custom_call" | custom-call | flops 1000000 | bytes 1048576 | tf_op jit(solution)/shard_map/pallas_call | solution.py:391
  17.8 1.2 %all-to-all-done.got_ref = bf16[32,24,128]{2,1,0:T(8,128)(2,1)S(1)} async-done(((bf16[32,24,128]{2,1,0:T(8,128)(2,1)}), bf16[32,24,128]{2,1,0:T(8,128)(2,1)S(1)}, u32[]{:S(2)}, u32[]{:S(2)}) %all-to-all-start) | async-done | bytes 196640 | tf_op jit(solution)/shard_map/all_to_all | solution.py:271
  19.0 0.0 copy-done
  19.0 1.5 %shard_map.122 = (f32[64,128]{1,0:T(8,128)S(1)}, bf16[64,128]{1,0:T(8,128)(2,1)S(1)}, bf16[64,128]{1,0:T(8,128)(2,1)S(1)}, bf16[64,128]{1,0:T(8,128)(2,1)S(1)}) custom-call(bf16[32,24,128]{2,1,0:T(8,128)(2,1)S(1)} %all-to-all-done.got_ref, bf16[4,64,64]{2,1,0:T(8,128)(2,1)S(1)} %get-tuple-element.24.sel_ref, bf16[4,456,456]{2,1,0:T(8,128)(2,1)S(1)} %copy-done, ...), custom_call_target="tpu_custom_call" | custom-call | flops 20000000 | bytes 1048576 | tf_op jit(solution)/shard_map/pallas_call | solution.py:489
  20.5 0.6 %collective-permute-start.3 = (bf16[64,128]{1,0:T(8,128)(2,1)S(1)}, bf16[64,128]{1,0:T(8,128)(2,1)S(1)}, u32[]{:S(2)}, u32[]{:S(2)}) collective-permute-start(bf16[64,128]{1,0:T(8,128)(2,1)S(1)} %get-tuple-element.28), channel_id=1, source_target_pairs={{0,1},{1,0},{2,3},{3,2},{4,5},{5,4},{6,7},{7,6},{8,9},{9,8},{10,11... | collective-permute-start | bytes 49160 | tf_op jit(solution)/shard_map/ppermute | solution.py:276
  21.1 0.5 %collective-permute-start.4 = (bf16[64,128]{1,0:T(8,128)(2,1)S(1)}, bf16[64,128]{1,0:T(8,128)(2,1)S(1)}, u32[]{:S(2)}, u32[]{:S(2)}) collective-permute-start(bf16[64,128]{1,0:T(8,128)(2,1)S(1)} %get-tuple-element.29), channel_id=1, source_target_pairs={{0,2},{1,3},{2,0},{3,1},{4,6},{5,7},{6,4},{7,5},{8,10},{9,11},{10,... | collective-permute-start | bytes 49160 | tf_op jit(solution)/shard_map/ppermute | solution.py:276
  21.5 1.0 %collective-permute-start.5 = (bf16[64,128]{1,0:T(8,128)(2,1)S(1)}, bf16[64,128]{1,0:T(8,128)(2,1)S(1)}, u32[]{:S(2)}, u32[]{:S(2)}) collective-permute-start(bf16[64,128]{1,0:T(8,128)(2,1)S(1)} %get-tuple-element.30), channel_id=1, source_target_pairs={{0,3},{1,2},{2,1},{3,0},{4,7},{5,6},{6,5},{7,4},{8,11},{9,10},{10,... | collective-permute-start | bytes 49160 | tf_op jit(solution)/shard_map/ppermute | solution.py:276
  22.5 1.6 %shard_map.118 = (f32[3,2048]{1,0:T(4,128)S(1)}, f32[456,128]{1,0:T(8,128)S(1)}, bf16[2,456,456]{2,1,0:T(8,128)(2,1)S(1)}, bf16[2,456,456]{2,1,0:T(8,128)(2,1)S(...) custom-call(f32[3,2048]{1,0:T(4,128)} %refs_2_.1, f32[456,128]{1,0:T(8,128)} %constant.2.clone.shell_hbm, ...), custom_call_target="tpu_custom_call" | custom-call | flops 2000000 | bytes 1048576 | tf_op jit(solution)/shard_map/pallas_call | solution.py:529
  24.1 0.0 collective-permute-done.3.refs_1_
  24.2 0.7 %collective-permute-done.4.refs_2_ = bf16[64,128]{1,0:T(8,128)(2,1)S(1)} collective-permute-done((bf16[64,128]{1,0:T(8,128)(2,1)S(1)}, bf16[64,128]{1,0:T(8,128)(2,1)S(1)}, u32[]{:S(2)}, u32[]{:S(2)}) %collective-permute-start.4) | collective-permute-done | bytes 16416 | tf_op jit(solution)/shard_map/ppermute | solution.py:276
  24.9 0.0 collective-permute-done.5.refs_3_
  24.9 1.1 %shard_map.123.refs_0_ = f32[16,128]{1,0:T(8,128)S(1)} custom-call(f32[3,2048]{1,0:T(4,128)S(1)} %get-tuple-element.18.offsets_ref, f32[456,128]{1,0:T(8,128)S(1)} %get-tuple-element.19.shell_ref, bf16[2,456,456]{2,1,0:T(8,128)(2,1)S(1)} %get-tuple-element.20.child_ref, bf16[2,456,456]{2,1,0:T(8,128)(2,1)S(1)} %get-tuple-element.21.split_ref, ...), custom_call_target="tpu_custom_call" | custom-call | flops 20000000 | bytes 1048576 | tf_op jit(solution)/shard_map/pallas_call | solution.py:586
  25.9 0.2 collective-permute-start.6
  26.1 1.5 %collective-permute-start.7 = (f32[16,128]{1,0:T(8,128)S(1)}, f32[16,128]{1,0:T(8,128)S(1)}, u32[]{:S(2)}, u32[]{:S(2)}) collective-permute-start(f32[16,128]{1,0:T(8,128)S(1)} %shard_map.123.refs_0_), channel_id=1, source_target_pairs={{0,2},{1,3},{2,0},{3,1},{4,6},{5,7},{6,4},{7,5},{8,10},{9,11},{10,... | collective-permute-start | bytes 24584 | tf_op jit(solution)/shard_map/ppermute | solution.py:276
  27.6 0.2 collective-permute-start.8
  27.8 0.0 collective-permute-done.6.refs_1_
  27.9 1.9 %collective-permute-done.7.refs_2_ = f32[16,128]{1,0:T(8,128)S(1)} collective-permute-done((f32[16,128]{1,0:T(8,128)S(1)}, f32[16,128]{1,0:T(8,128)S(1)}, u32[]{:S(2)}, u32[]{:S(2)}) %collective-permute-start.7) | collective-permute-done | bytes 8224 | tf_op jit(solution)/shard_map/ppermute | solution.py:276
  29.7 1.0 %collective-permute-done.8.refs_3_ = f32[16,128]{1,0:T(8,128)S(1)} collective-permute-done((f32[16,128]{1,0:T(8,128)S(1)}, f32[16,128]{1,0:T(8,128)S(1)}, u32[]{:S(2)}, u32[]{:S(2)}) %collective-permute-start.8) | collective-permute-done | bytes 8224 | tf_op jit(solution)/shard_map/ppermute | solution.py:276
  30.7 0.6 %shard_map.124 = f32[3,2048]{1,0:T(4,128)} custom-call(f32[16,128]{1,0:T(8,128)S(1)} %shard_map.123.refs_0_, f32[16,128]{1,0:T(8,128)S(1)} %collective-permute-done.6.refs_1_, f32[16,128]{1,0:T(8,128)S(1)} %collective-permute-done.7.refs_2_, f32[16,128]{1,0:T(8,128)S(1)} %collective-permute-done.8.refs_3_), custom_call_target="tpu_custom_call" | custom-call | flops 100000 | bytes 1048576 | tf_op jit(solution)/shard_map/pallas_call | solution.py:603
Async XLA Ops:
  0.0 15.3 %collective-permute-start = (bf16[4,456,456]{2,1,0:T(8,128)(2,1)}, bf16[4,456,456]{2,1,0:T(8,128)(2,1)}, u32[]{:S(2)}, u32[]{:S(2)}) collective-permute-start(bf16[4,456,456]{2,1,0:T(8,128)(2,1)} %m2l_ref.1), channel_id=1, source_target_pairs={{0,1},{1,0},{2,3},{3,2},{4,5},{5,4},{6,7},{7,6},{8,9},{9,8},{10,11... | collective-permute-start | bytes 4990472 | tf_op jit(solution)/shard_map/ppermute | solution.py:280
  0.5 18.5 %copy-start = (bf16[4,456,456]{2,1,0:T(8,128)(2,1)S(1)}, bf16[4,456,456]{2,1,0:T(8,128)(2,1)}, u32[]{:S(2)}) copy-start(bf16[4,456,456]{2,1,0:T(8,128)(2,1)} %m2l_ref.1) | copy-start | bytes 4990468
  3.1 15.9 %all-to-all-start = ((bf16[32,24,128]{2,1,0:T(8,128)(2,1)}), bf16[32,24,128]{2,1,0:T(8,128)(2,1)S(1)}, u32[]{:S(2)}, u32[]{:S(2)}) async-start(bf16[32,24,128]{2,1,0:T(8,128)(2,1)} %shard_map.119), calls=%async_computation | async-start | bytes 393216 | tf_op jit(solution)/shard_map/all_to_all | solution.py:271
  10.0 5.2 %collective-permute-start.1 = (s32[4,1,32]{2,1,0:T(1,128)}, s32[4,1,32]{2,1,0:T(1,128)S(1)}, u32[]{:S(2)}, u32[]{:S(2)}) collective-permute-start(s32[4,1,32]{2,1,0:T(1,128)} %bitcast.20), channel_id=1, source_target_pairs={{0,1},{1,0},{2,3},{3,2},{4,5},{5,4},{6,7},{7,6},{8,9},{9,8},{10,11... | collective-permute-start | bytes 1544 | tf_op jit(solution)/shard_map/ppermute | solution.py:280
  10.3 4.9 %collective-permute-start.2 = (s32[4,32]{1,0:T(4,128)}, s32[4,32]{1,0:T(4,128)S(1)}, u32[]{:S(2)}, u32[]{:S(2)}) collective-permute-start(s32[4,32]{1,0:T(4,128)} %bitcast.22), channel_id=1, source_target_pairs={{0,1},{1,0},{2,3},{3,2},{4,5},{5,4},{6,7},{7,6},{8,9},{9,8},{10,11... | collective-permute-start | bytes 1544 | tf_op jit(solution)/shard_map/ppermute | solution.py:280
  20.5 3.7 %collective-permute-start.3 = (bf16[64,128]{1,0:T(8,128)(2,1)S(1)}, bf16[64,128]{1,0:T(8,128)(2,1)S(1)}, u32[]{:S(2)}, u32[]{:S(2)}) collective-permute-start(bf16[64,128]{1,0:T(8,128)(2,1)S(1)} %get-tuple-element.28), channel_id=1, source_target_pairs={{0,1},{1,0},{2,3},{3,2},{4,5},{5,4},{6,7},{7,6},{8,9},{9,8},{10,11... | collective-permute-start | bytes 49160 | tf_op jit(solution)/shard_map/ppermute | solution.py:276
  21.1 3.8 %collective-permute-start.4 = (bf16[64,128]{1,0:T(8,128)(2,1)S(1)}, bf16[64,128]{1,0:T(8,128)(2,1)S(1)}, u32[]{:S(2)}, u32[]{:S(2)}) collective-permute-start(bf16[64,128]{1,0:T(8,128)(2,1)S(1)} %get-tuple-element.29), channel_id=1, source_target_pairs={{0,2},{1,3},{2,0},{3,1},{4,6},{5,7},{6,4},{7,5},{8,10},{9,11},{10,... | collective-permute-start | bytes 49160 | tf_op jit(solution)/shard_map/ppermute | solution.py:276
  21.5 3.3 %collective-permute-start.5 = (bf16[64,128]{1,0:T(8,128)(2,1)S(1)}, bf16[64,128]{1,0:T(8,128)(2,1)S(1)}, u32[]{:S(2)}, u32[]{:S(2)}) collective-permute-start(bf16[64,128]{1,0:T(8,128)(2,1)S(1)} %get-tuple-element.30), channel_id=1, source_target_pairs={{0,3},{1,2},{2,1},{3,0},{4,7},{5,6},{6,5},{7,4},{8,11},{9,10},{10,... | collective-permute-start | bytes 49160 | tf_op jit(solution)/shard_map/ppermute | solution.py:276
  25.9 1.9 %collective-permute-start.6 = (f32[16,128]{1,0:T(8,128)S(1)}, f32[16,128]{1,0:T(8,128)S(1)}, u32[]{:S(2)}, u32[]{:S(2)}) collective-permute-start(f32[16,128]{1,0:T(8,128)S(1)} %shard_map.123.refs_0_), channel_id=1, source_target_pairs={{0,1},{1,0},{2,3},{3,2},{4,5},{5,4},{6,7},{7,6},{8,9},{9,8},{10,11... | collective-permute-start | bytes 24584 | tf_op jit(solution)/shard_map/ppermute | solution.py:276
  26.1 3.7 %collective-permute-start.7 = (f32[16,128]{1,0:T(8,128)S(1)}, f32[16,128]{1,0:T(8,128)S(1)}, u32[]{:S(2)}, u32[]{:S(2)}) collective-permute-start(f32[16,128]{1,0:T(8,128)S(1)} %shard_map.123.refs_0_), channel_id=1, source_target_pairs={{0,2},{1,3},{2,0},{3,1},{4,6},{5,7},{6,4},{7,5},{8,10},{9,11},{10,... | collective-permute-start | bytes 24584 | tf_op jit(solution)/shard_map/ppermute | solution.py:276
  27.6 3.1 %collective-permute-start.8 = (f32[16,128]{1,0:T(8,128)S(1)}, f32[16,128]{1,0:T(8,128)S(1)}, u32[]{:S(2)}, u32[]{:S(2)}) collective-permute-start(f32[16,128]{1,0:T(8,128)S(1)} %shard_map.123.refs_0_), channel_id=1, source_target_pairs={{0,3},{1,2},{2,1},{3,0},{4,7},{5,6},{6,5},{7,4},{8,11},{9,10},{10,... | collective-permute-start | bytes 24584 | tf_op jit(solution)/shard_map/ppermute | solution.py:276

commit v7 on v6

--- a/solution.py
+++ b/solution.py
@@ -40,6 +40,13 @@
     rs = lax.rsqrt(r2)
     weight = rs * (rs * rs)
     return rs + EPSILON2 * weight, weight
+
+
+def scaled(d):
+    r2 = d[0] * d[0] + d[1] * d[1] + (d[2] * d[2] + EPSILON2)
+    rs = lax.rsqrt(r2)
+    root = rs * (rs * lax.rsqrt(rs))
+    return rs + EPSILON2 * (rs * (rs * rs)), [root * d[c] for c in range(3)]
 
 
 def stokeslet(d, v):
@@ -357,7 +364,7 @@
         24,
     )(*in_hbm(near_q, near_d, offsets, vel_cot))
 
-    heads = classes // 2
+    heads = classes - 1
 
     def hold_body(
         owner_hbm, place_hbm, pair_ref, near_ref, *refs
@@ -383,15 +390,14 @@
             ],
             0,
         ).astype(BF16)
-        for k in range(pieces):
-            expand = (iota(spread, 0) == parent) & (lane % half_rows // 2 == k)
-            sel_ref[k] = dot(pick, expand.astype(F32).astype(BF16)).astype(BF16)
+        expand = (iota(spread, 0) == parent).astype(F32).astype(BF16)
+        sel_ref[...] = dot(pick, expand).astype(BF16)
         copies[2].wait()
 
     select, head_ops, tail_ops = call(
         hold_body,
         (
-            shape((pieces, 16 * classes, leaves * half_rows), BF16),
+            shape((16 * classes, leaves * half_rows), BF16),
             shape((heads, width, width), BF16),
             pltpu.HBM((classes - heads, width, width), BF16),
         ),
@@ -410,7 +416,15 @@
         mine = lax.axis_index("leaf").astype(F32)
         tops = got_ref[:, up_rows:, :].astype(F32).reshape(leaves, lvls, half_rows, LANES)
         tops = jnp.sum(tops, 1).astype(BF16).reshape(leaves * half_rows, LANES)
-        chosen = jnp.concatenate([dot(sel_ref[k], tops) for k in range(pieces)], 1)
+        select = sel_ref[...].astype(F32)
+        piece = iota(select.shape, 1) % half_rows // 2
+        chosen = jnp.concatenate(
+            [
+                dot(jnp.where(piece == k, select, 0.0).astype(BF16), tops)
+                for k in range(pieces)
+            ],
+            1,
+        )
         high = chosen.astype(BF16).astype(F32)
         parts = jnp.where(iota(chosen.shape, 0) % 8 < parents, high, chosen - high)
 
@@ -499,7 +513,7 @@
     geo_rows = parents * count
 
     def prep_body(
-        offsets_hbm, shell_hbm, child_hbm, map_hbm, offsets_ref, shell_ref, child_ref, split_ref, scale_ref, weight_ref, map_ref, sems
+        offsets_hbm, shell_hbm, child_hbm, map_hbm, child_ref, split_ref, scale_ref, turned_ref, offsets_ref, shell_ref, map_ref, sems
     ):
         copies = start_all(
             (offsets_hbm, shell_hbm, map_hbm, child_hbm),
@@ -517,7 +531,9 @@
                     for c in range(3)
                 ]
                 rows = slice(p * count + row, p * count + row + 8)
-                scale_ref[rows, :], weight_ref[rows, :] = factors(d)
+                scale_ref[rows, :], turned = scaled(d)
+                for c in range(3):
+                    turned_ref[c, rows, :] = turned[c]
         copies[2].wait()
         mapped = map_ref[...]
         high = mapped.astype(BF16)
@@ -529,21 +545,18 @@
     prepared = call(
         prep_body,
         (
-            shape(offsets.shape, F32),
-            shape(shell.shape, F32),
             shape(child_ops.shape, BF16),
             shape((2, width, width), BF16),
             shape((geo_rows, LANES), F32),
-            shape((geo_rows, LANES), F32),
+            shape((3, geo_rows, LANES), F32),
         ),
         2_000_000,
-        held(check_map) + [pltpu.SemaphoreType.DMA((4,))],
+        held(offsets, shell, check_map) + [pltpu.SemaphoreType.DMA((4,))],
         [HBM] * 4,
     )(*in_hbm(*prep_inputs))
 
-    def down_body(offsets_ref, shell_ref, child_ref, split_ref, scale_ref, weight_ref, *refs):
+    def down_body(child_ref, split_ref, scale_ref, turned_ref, *refs):
         *mid_refs, out_ref, dens = refs
-        me = lax.axis_index("lvl")
         total = mid_refs[0][...]
         for ref in mid_refs[1:]:
             total = total + ref[...].astype(F32)
@@ -568,17 +581,14 @@
         dens[...] = dot(pair, hit, TN)
         out_ref[...] = total[up_rows + own_rows :]
         for p in range(parents):
-            target = rows3(offsets_ref, lanes_of(p, me))
             lanes = slice(p * LANES, (p + 1) * LANES)
             force = [jnp.zeros((8, LANES), F32) for _ in range(3)]
             for row in range(0, count, 8):
-                spots = [slice(c * count + row, c * count + row + 8) for c in range(3)]
-                d = [target[c] - shell_ref[spots[c], :] for c in range(3)]
-                q = [dens[spots[c], lanes] for c in range(3)]
+                q = [dens[c * count + row : c * count + row + 8, lanes] for c in range(3)]
                 rows = slice(p * count + row, p * count + row + 8)
-                scale = scale_ref[rows, :]
-                along = weight_ref[rows, :] * (d[0] * q[0] + d[1] * q[1] + d[2] * q[2])
-                force = [force[c] + (scale * q[c] + along * d[c]) for c in range(3)]
+                scale, e = scale_ref[rows, :], [turned_ref[c, rows, :] for c in range(3)]
+                along = e[0] * q[0] + e[1] * q[1] + e[2] * q[2]
+                force = [force[c] + (scale * q[c] + along * e[c]) for c in range(3)]
             for c in range(3):
                 row = p * 4 + c
                 out_ref[row : row + 1, :] += jnp.sum(force[c], 0, keepdims=True)
@@ -588,7 +598,7 @@
         shape((parents * 4, LANES), F32),
         20_000_000,
         [pltpu.VMEM((3 * count, parents * LANES), F32)],
-        [VMEM] * (6 + lvls),
+        [VMEM] * (4 + lvls),
     )(*prepared, *mids)
     forces = exchanged([forces] * lvls)
 

time: 31.7 us -> 31.4 us (level)
  Pallas kernels: 14.5 us -> 14.1 us
where the time goes in v7:
time: 31.4 us; the launch traced here: 31 us
  Pallas kernels  14.1 us (45%)
  starting transfers between devices  12 us (38%)
  waiting for transfers between devices  4.88 us (16%)
    all_to_all x1, starting transfers between devices, local(): lax.all_to_all(sent, ('leaf', 'lvl'), split_axis=0, concat_axis=0, tiled=...  6.96 us
    pallas_call x1, Pallas kernels, local(): call(near_body, shape((lvls, parents * 4, LANES), F32), 100000000, [pltpu...  4.61 us
    ppermute x6, starting transfers between devices, exchanged(): lax.ppermute(values[k], 'lvl', [(i, i ^ k) for i in range(lvls)])  3.93 us
    ppermute x6, waiting for transfers between devices, exchanged(): lax.ppermute(values[k], 'lvl', [(i, i ^ k) for i in range(lvls)])  3.55 us
    pallas_call x1, Pallas kernels, local(): call(up_body, pltpu.HBM((devices, slot_rows, LANES), BF16), 20000000, hel...  2.55 us
    pallas_call x1, Pallas kernels, local(): call(hold_body, (shape((16 * classes, leaves * half_rows), BF16), shape((...  2.39 us
    pallas_call x1, Pallas kernels, local(): call(prep_body, (shape(child_ops.shape, BF16), shape((2, width, width), B...  1.64 us
    all_to_all x1, waiting for transfers between devices, local(): lax.all_to_all(sent, ('leaf', 'lvl'), split_axis=0, concat_axis=0, tiled=...  1.32 us
  transfers between devices with their start and end apart: 10, of which 4 were waited for; matrix products, arithmetic and copies ran while one was open for 0% of the time, Pallas kernels for 36%

profile of v7, /device:TPU:0, one launch (start us, length us, event | category | flops | bytes accessed | tf_op | source)
XLA Modules:
  0.0 31.0 jit_solution(12259868723145886345)
XLA Ops:
  0.0 0.5 %collective-permute-start = (bf16[4,456,456]{2,1,0:T(8,128)(2,1)}, bf16[4,456,456]{2,1,0:T(8,128)(2,1)}, u32[]{:S(2)}, u32[]{:S(2)}) collective-permute-start(bf16[4,456,456]{2,1,0:T(8,128)(2,1)} %m2l_ref.1), channel_id=1, source_target_pairs={{0,1},{1,0},{2,3},{3,2},{4,5},{5,4},{6,7},{7,6},{8,9},{9,8},{10,11... | collective-permute-start | bytes 4990472 | tf_op jit(solution)/shard_map/ppermute | solution.py:287
  0.5 0.0 copy-start
  0.5 2.6 %shard_map.119 = bf16[32,24,128]{2,1,0:T(8,128)(2,1)} custom-call(f32[3,2048]{1,0:T(4,128)} %refs_2_.1, f32[3,2048]{1,0:T(4,128)} %refs_3_.1, f32[456,128]{1,0:T(8,128)} %constant.2.clone.shell_hbm, s32[4,1,32]{2,1,0:T(1,128)} %bitcast.18, s32[4,32]{1,0:T(4,128)} %bitcast.19, bf16[2,456,456]{2,1,0:T(8,128)(2,1)} %child_hbm.3), custom_call_target="tpu_custom_call" | custom-call | flops 20000000 | bytes 1048576 | tf_op jit(solution)/shard_map/pallas_call | solution.py:263
  3.1 7.0 %all-to-all-start = ((bf16[32,24,128]{2,1,0:T(8,128)(2,1)}), bf16[32,24,128]{2,1,0:T(8,128)(2,1)S(1)}, u32[]{:S(2)}, u32[]{:S(2)}) async-start(bf16[32,24,128]{2,1,0:T(8,128)(2,1)} %shard_map.119), calls=%async_computation | async-start | bytes 393216 | tf_op jit(solution)/shard_map/all_to_all | solution.py:278
  10.0 0.3 %collective-permute-start.1 = (s32[4,1,32]{2,1,0:T(1,128)}, s32[4,1,32]{2,1,0:T(1,128)S(1)}, u32[]{:S(2)}, u32[]{:S(2)}) collective-permute-start(s32[4,1,32]{2,1,0:T(1,128)} %bitcast.20), channel_id=1, source_target_pairs={{0,1},{1,0},{2,3},{3,2},{4,5},{5,4},{6,7},{7,6},{8,9},{9,8},{10,11... | collective-permute-start | bytes 1544 | tf_op jit(solution)/shard_map/ppermute | solution.py:287
  10.3 0.3 collective-permute-start.2
  10.6 4.6 %shard_map.120.near_ref = f32[4,16,128]{2,1,0:T(8,128)S(1)} custom-call(s32[4,32]{1,0:T(4,128)} %bitcast.24, s32[4,32]{1,0:T(4,128)} %bitcast.25, f32[3,2048]{1,0:T(4,128)} %refs_2_.1, f32[3,2048]{1,0:T(4,128)} %refs_3_.1), custom_call_target="tpu_custom_call" | custom-call | flops 100000000 | bytes 1048576 | tf_op jit(solution)/shard_map/pallas_call | solution.py:352
  15.2 0.0 collective-permute-done.1.refs_0_
  15.2 0.0 collective-permute-done.2.refs_1_
  15.2 0.0 collective-permute-done.pair_ref
  15.2 2.4 %shard_map.121 = (bf16[64,64]{1,0:T(8,128)(2,1)S(1)}, bf16[3,456,456]{2,1,0:T(8,128)(2,1)S(1)}, bf16[1,456,456]{2,1,0:T(8,128)(2,1)}) custom-call(s32[4,1,32]{2,1,0:T(1,128)} %bitcast.21, s32[4,32]{1,0:T(4,128)} %bitcast.23, bf16[4,456,456]{2,1,0:T(8,128)(2,1)} %collective-permute-done.pair_ref, f32[4,16,128]{2,1,0:T(8,128)S(1)} %shard_map.120.near_ref, ...), custom_call_target="tpu_custom_call" | custom-call | flops 1000000 | bytes 1048576 | tf_op jit(solution)/shard_map/pallas_call | solution.py:397
  17.6 1.3 %all-to-all-done.got_ref = bf16[32,24,128]{2,1,0:T(8,128)(2,1)S(1)} async-done(((bf16[32,24,128]{2,1,0:T(8,128)(2,1)}), bf16[32,24,128]{2,1,0:T(8,128)(2,1)S(1)}, u32[]{:S(2)}, u32[]{:S(2)}) %all-to-all-start) | async-done | bytes 196640 | tf_op jit(solution)/shard_map/all_to_all | solution.py:278
  19.0 0.0 copy-done
  19.0 1.3 %shard_map.122 = (f32[64,128]{1,0:T(8,128)S(1)}, bf16[64,128]{1,0:T(8,128)(2,1)S(1)}, bf16[64,128]{1,0:T(8,128)(2,1)S(1)}, bf16[64,128]{1,0:T(8,128)(2,1)S(1)}) custom-call(bf16[32,24,128]{2,1,0:T(8,128)(2,1)S(1)} %all-to-all-done.got_ref, bf16[64,64]{1,0:T(8,128)(2,1)S(1)} %get-tuple-element.20.sel_ref, bf16[4,456,456]{2,1,0:T(8,128)(2,1)S(1)} %copy-done, ...), custom_call_target="tpu_custom_call" | custom-call | flops 20000000 | bytes 1048576 | tf_op jit(solution)/shard_map/pallas_call | solution.py:503
  20.2 0.6 %collective-permute-start.3 = (bf16[64,128]{1,0:T(8,128)(2,1)S(1)}, bf16[64,128]{1,0:T(8,128)(2,1)S(1)}, u32[]{:S(2)}, u32[]{:S(2)}) collective-permute-start(bf16[64,128]{1,0:T(8,128)(2,1)S(1)} %get-tuple-element.24), channel_id=1, source_target_pairs={{0,1},{1,0},{2,3},{3,2},{4,5},{5,4},{6,7},{7,6},{8,9},{9,8},{10,11... | collective-permute-start | bytes 49160 | tf_op jit(solution)/shard_map/ppermute | solution.py:283
  20.8 0.4 %collective-permute-start.4 = (bf16[64,128]{1,0:T(8,128)(2,1)S(1)}, bf16[64,128]{1,0:T(8,128)(2,1)S(1)}, u32[]{:S(2)}, u32[]{:S(2)}) collective-permute-start(bf16[64,128]{1,0:T(8,128)(2,1)S(1)} %get-tuple-element.25), channel_id=1, source_target_pairs={{0,2},{1,3},{2,0},{3,1},{4,6},{5,7},{6,4},{7,5},{8,10},{9,11},{10,... | collective-permute-start | bytes 49160 | tf_op jit(solution)/shard_map/ppermute | solution.py:283
  21.3 1.0 %collective-permute-start.5 = (bf16[64,128]{1,0:T(8,128)(2,1)S(1)}, bf16[64,128]{1,0:T(8,128)(2,1)S(1)}, u32[]{:S(2)}, u32[]{:S(2)}) collective-permute-start(bf16[64,128]{1,0:T(8,128)(2,1)S(1)} %get-tuple-element.26), channel_id=1, source_target_pairs={{0,3},{1,2},{2,1},{3,0},{4,7},{5,6},{6,5},{7,4},{8,11},{9,10},{10,... | collective-permute-start | bytes 49160 | tf_op jit(solution)/shard_map/ppermute | solution.py:283
  22.2 1.6 %shard_map.118 = (bf16[2,456,456]{2,1,0:T(8,128)(2,1)S(1)}, bf16[2,456,456]{2,1,0:T(8,128)(2,1)S(1)}, f32[608,128]{1,0:T(8,128)S(1)}, f32[3,608,128]{2,1,0:T(8,128)S(1)}) custom-call(f32[3,2048]{1,0:T(4,128)} %refs_2_.1, f32[456,128]{1,0:T(8,128)} %constant.2.clone.shell_hbm, bf16[2,456,456]{2,1,0:T(8,128)(2,1)} %child_hbm.3, f32[456,456]{1,0:T(8,128)} %map_hbm.1), custom_call_target="tpu_custom_call" | custom-call | flops 2000000 | bytes 1048576 | tf_op jit(solution)/shard_map/pallas_call | solution.py:545
  23.9 0.0 collective-permute-done.3.refs_1_
  23.9 0.7 %collective-permute-done.4.refs_2_ = bf16[64,128]{1,0:T(8,128)(2,1)S(1)} collective-permute-done((bf16[64,128]{1,0:T(8,128)(2,1)S(1)}, bf16[64,128]{1,0:T(8,128)(2,1)S(1)}, u32[]{:S(2)}, u32[]{:S(2)}) %collective-permute-start.4) | collective-permute-done | bytes 16416 | tf_op jit(solution)/shard_map/ppermute | solution.py:283
  24.6 0.0 collective-permute-done.5.refs_3_
  24.6 1.0 %shard_map.123.refs_0_ = f32[16,128]{1,0:T(8,128)S(1)} custom-call(bf16[2,456,456]{2,1,0:T(8,128)(2,1)S(1)} %get-tuple-element.16.child_ref, bf16[2,456,456]{2,1,0:T(8,128)(2,1)S(1)} %get-tuple-element.17.split_ref, f32[608,128]{1,0:T(8,128)S(1)} %get-tuple-element.18.scale_ref, f32[3,608,128]{2,1,0:T(8,128)S(1)} %get-tuple-element.19.turned_ref, ...), custom_call_target="tpu_custom_call" | custom-call | flops 20000000 | bytes 1048576 | tf_op jit(solution)/shard_map/pallas_call | solution.py:596
  25.6 0.2 collective-permute-start.6
  25.8 1.5 %collective-permute-start.7 = (f32[16,128]{1,0:T(8,128)S(1)}, f32[16,128]{1,0:T(8,128)S(1)}, u32[]{:S(2)}, u32[]{:S(2)}) collective-permute-start(f32[16,128]{1,0:T(8,128)S(1)} %shard_map.123.refs_0_), channel_id=1, source_target_pairs={{0,2},{1,3},{2,0},{3,1},{4,6},{5,7},{6,4},{7,5},{8,10},{9,11},{10,... | collective-permute-start | bytes 24584 | tf_op jit(solution)/shard_map/ppermute | solution.py:283
  27.3 0.2 collective-permute-start.8
  27.5 0.0 collective-permute-done.6.refs_1_
  27.6 1.9 %collective-permute-done.7.refs_2_ = f32[16,128]{1,0:T(8,128)S(1)} collective-permute-done((f32[16,128]{1,0:T(8,128)S(1)}, f32[16,128]{1,0:T(8,128)S(1)}, u32[]{:S(2)}, u32[]{:S(2)}) %collective-permute-start.7) | collective-permute-done | bytes 8224 | tf_op jit(solution)/shard_map/ppermute | solution.py:283
  29.4 1.0 %collective-permute-done.8.refs_3_ = f32[16,128]{1,0:T(8,128)S(1)} collective-permute-done((f32[16,128]{1,0:T(8,128)S(1)}, f32[16,128]{1,0:T(8,128)S(1)}, u32[]{:S(2)}, u32[]{:S(2)}) %collective-permute-start.8) | collective-permute-done | bytes 8224 | tf_op jit(solution)/shard_map/ppermute | solution.py:283
  30.4 0.6 %shard_map.124 = f32[3,2048]{1,0:T(4,128)} custom-call(f32[16,128]{1,0:T(8,128)S(1)} %shard_map.123.refs_0_, f32[16,128]{1,0:T(8,128)S(1)} %collective-permute-done.6.refs_1_, f32[16,128]{1,0:T(8,128)S(1)} %collective-permute-done.7.refs_2_, f32[16,128]{1,0:T(8,128)S(1)} %collective-permute-done.8.refs_3_), custom_call_target="tpu_custom_call" | custom-call | flops 100000 | bytes 1048576 | tf_op jit(solution)/shard_map/pallas_call | solution.py:613
Async XLA Ops:
  0.0 15.2 %collective-permute-start = (bf16[4,456,456]{2,1,0:T(8,128)(2,1)}, bf16[4,456,456]{2,1,0:T(8,128)(2,1)}, u32[]{:S(2)}, u32[]{:S(2)}) collective-permute-start(bf16[4,456,456]{2,1,0:T(8,128)(2,1)} %m2l_ref.1), channel_id=1, source_target_pairs={{0,1},{1,0},{2,3},{3,2},{4,5},{5,4},{6,7},{7,6},{8,9},{9,8},{10,11... | collective-permute-start | bytes 4990472 | tf_op jit(solution)/shard_map/ppermute | solution.py:287
  0.5 18.5 %copy-start = (bf16[4,456,456]{2,1,0:T(8,128)(2,1)S(1)}, bf16[4,456,456]{2,1,0:T(8,128)(2,1)}, u32[]{:S(2)}) copy-start(bf16[4,456,456]{2,1,0:T(8,128)(2,1)} %m2l_ref.1) | copy-start | bytes 4990468
  3.1 15.9 %all-to-all-start = ((bf16[32,24,128]{2,1,0:T(8,128)(2,1)}), bf16[32,24,128]{2,1,0:T(8,128)(2,1)S(1)}, u32[]{:S(2)}, u32[]{:S(2)}) async-start(bf16[32,24,128]{2,1,0:T(8,128)(2,1)} %shard_map.119), calls=%async_computation | async-start | bytes 393216 | tf_op jit(solution)/shard_map/all_to_all | solution.py:278
  10.0 5.2 %collective-permute-start.1 = (s32[4,1,32]{2,1,0:T(1,128)}, s32[4,1,32]{2,1,0:T(1,128)S(1)}, u32[]{:S(2)}, u32[]{:S(2)}) collective-permute-start(s32[4,1,32]{2,1,0:T(1,128)} %bitcast.20), channel_id=1, source_target_pairs={{0,1},{1,0},{2,3},{3,2},{4,5},{5,4},{6,7},{7,6},{8,9},{9,8},{10,11... | collective-permute-start | bytes 1544 | tf_op jit(solution)/shard_map/ppermute | solution.py:287
  10.3 4.9 %collective-permute-start.2 = (s32[4,32]{1,0:T(4,128)}, s32[4,32]{1,0:T(4,128)S(1)}, u32[]{:S(2)}, u32[]{:S(2)}) collective-permute-start(s32[4,32]{1,0:T(4,128)} %bitcast.22), channel_id=1, source_target_pairs={{0,1},{1,0},{2,3},{3,2},{4,5},{5,4},{6,7},{7,6},{8,9},{9,8},{10,11... | collective-permute-start | bytes 1544 | tf_op jit(solution)/shard_map/ppermute | solution.py:287
  20.2 3.7 %collective-permute-start.3 = (bf16[64,128]{1,0:T(8,128)(2,1)S(1)}, bf16[64,128]{1,0:T(8,128)(2,1)S(1)}, u32[]{:S(2)}, u32[]{:S(2)}) collective-permute-start(bf16[64,128]{1,0:T(8,128)(2,1)S(1)} %get-tuple-element.24), channel_id=1, source_target_pairs={{0,1},{1,0},{2,3},{3,2},{4,5},{5,4},{6,7},{7,6},{8,9},{9,8},{10,11... | collective-permute-start | bytes 49160 | tf_op jit(solution)/shard_map/ppermute | solution.py:283
  20.8 3.8 %collective-permute-start.4 = (bf16[64,128]{1,0:T(8,128)(2,1)S(1)}, bf16[64,128]{1,0:T(8,128)(2,1)S(1)}, u32[]{:S(2)}, u32[]{:S(2)}) collective-permute-start(bf16[64,128]{1,0:T(8,128)(2,1)S(1)} %get-tuple-element.25), channel_id=1, source_target_pairs={{0,2},{1,3},{2,0},{3,1},{4,6},{5,7},{6,4},{7,5},{8,10},{9,11},{10,... | collective-permute-start | bytes 49160 | tf_op jit(solution)/shard_map/ppermute | solution.py:283
  21.3 3.3 %collective-permute-start.5 = (bf16[64,128]{1,0:T(8,128)(2,1)S(1)}, bf16[64,128]{1,0:T(8,128)(2,1)S(1)}, u32[]{:S(2)}, u32[]{:S(2)}) collective-permute-start(bf16[64,128]{1,0:T(8,128)(2,1)S(1)} %get-tuple-element.26), channel_id=1, source_target_pairs={{0,3},{1,2},{2,1},{3,0},{4,7},{5,6},{6,5},{7,4},{8,11},{9,10},{10,... | collective-permute-start | bytes 49160 | tf_op jit(solution)/shard_map/ppermute | solution.py:283
  25.6 1.9 %collective-permute-start.6 = (f32[16,128]{1,0:T(8,128)S(1)}, f32[16,128]{1,0:T(8,128)S(1)}, u32[]{:S(2)}, u32[]{:S(2)}) collective-permute-start(f32[16,128]{1,0:T(8,128)S(1)} %shard_map.123.refs_0_), channel_id=1, source_target_pairs={{0,1},{1,0},{2,3},{3,2},{4,5},{5,4},{6,7},{7,6},{8,9},{9,8},{10,11... | collective-permute-start | bytes 24584 | tf_op jit(solution)/shard_map/ppermute | solution.py:283
  25.8 3.7 %collective-permute-start.7 = (f32[16,128]{1,0:T(8,128)S(1)}, f32[16,128]{1,0:T(8,128)S(1)}, u32[]{:S(2)}, u32[]{:S(2)}) collective-permute-start(f32[16,128]{1,0:T(8,128)S(1)} %shard_map.123.refs_0_), channel_id=1, source_target_pairs={{0,2},{1,3},{2,0},{3,1},{4,6},{5,7},{6,4},{7,5},{8,10},{9,11},{10,... | collective-permute-start | bytes 24584 | tf_op jit(solution)/shard_map/ppermute | solution.py:283
  27.3 3.1 %collective-permute-start.8 = (f32[16,128]{1,0:T(8,128)S(1)}, f32[16,128]{1,0:T(8,128)S(1)}, u32[]{:S(2)}, u32[]{:S(2)}) collective-permute-start(f32[16,128]{1,0:T(8,128)S(1)} %shard_map.123.refs_0_), channel_id=1, source_target_pairs={{0,3},{1,2},{2,1},{3,0},{4,7},{5,6},{6,5},{7,4},{8,11},{9,10},{10,... | collective-permute-start | bytes 24584 | tf_op jit(solution)/shard_map/ppermute | solution.py:283
